TPU v7x, 32 devices: a whole 2x2x4 slice. The times are simulated.
32 devices in a mesh: section: 4 (over x, core), dp: 8 (over z, y).
Axes of the slice: x: 2, y: 2, z: 4, core: 2. Of those that a mesh axis runs over, the one named last changes fastest.
Arguments:
- section_rows: bfloat16 [4, 12288, 768], P('section', 'dp'), may hold values from -6 to 6
- span_lengths: int32 [24, 6], P('dp'), may hold values from 1 to 256, 512 in all within a row
- first_weights: bfloat16 [4, 768, 3072], P('section'), may hold values from -3 to 3, as said below
- second_weights: bfloat16 [4, 768, 1536], P('section'), may hold values from -0.109375 to 0.109375
- norm_gain: float32 [4, 768], P('section'), may hold values from 0.25 to 1.75
- norm_shift: float32 [4, 768], P('section'), may hold values from -1.5 to 1.5
Outputs:
- section_out: float32 [4, 12288, 768], P('section', 'dp')
- grad_first: float32 [4, 768, 3072], P('section')
- grad_second: float32 [4, 768, 1536], P('section')
- grad_gain: float32 [4, 768], P('section')
- grad_shift: float32 [4, 768], P('section')
Inputs may be any that keep to these rules, and one draw needn't show every extreme that they name: `span_lengths`: each row's 6 entries sum to 512; the last entry is the row's padding; every row has an entry equal to 256. `first_weights`: independent entries.
All inputs are finite; a program needn't handle non-finite values.
Results may differ from a plain program's by a relative error of at most 0.014.
Values may be sent and summed in bfloat16 or wider, within the bound.
A program may use at most 192 MiB of HBM per device.

v0:
```python
import jax
import jax.numpy as jnp
from jax import lax
from jax.sharding import PartitionSpec as P

HEAD_DIM = 64
SEQ = 512


epsilon = 1e-12
contract_rows = (((0,), (0,)), ((), ()))
contract_cols = (((1,), (1,)), ((), ()))


def passed_along(block, axis, distance):
    devices = range(lax.axis_size(axis))
    route = [(i - distance, i) for i in devices if i - distance in devices]
    return lax.ppermute(block, axis, route)


def layer_norm(summed, gain_row, shift_row):
    centered = summed - jnp.mean(summed, axis=-1, keepdims=True)
    factor = lax.rsqrt(jnp.mean(centered * centered, axis=-1, keepdims=True) + epsilon)
    return centered * factor * gain_row + shift_row


def span_tables(lengths, seq_len):
    span_ends = jnp.cumsum(lengths)
    span_starts = span_ends - lengths
    positions = jnp.arange(seq_len, dtype=jnp.int32)
    segment = jnp.sum((positions[:, None] >= span_ends[None, :]).astype(jnp.int32), axis=1)
    leading = jnp.any(positions[:, None] == span_starts[None, :-1], axis=1)
    allowed = segment[:, None] == segment[None, :]
    return (leading, allowed)


def attend(inputs, weights, allowed):
    seq_len, features = inputs.shape
    heads = features // HEAD_DIM
    score_scale = HEAD_DIM ** (-0.5)
    projected = jnp.dot(
        inputs, weights[:, : 3 * features], preferred_element_type=jnp.float32
    ).astype(jnp.bfloat16)
    queries = projected[:, :features].reshape(seq_len, heads, HEAD_DIM)
    keys_h = projected[:, features : 2 * features].reshape(seq_len, heads, HEAD_DIM)
    values_h = projected[:, 2 * features :].reshape(seq_len, heads, HEAD_DIM)
    scores = (
        jnp.einsum("qhd,khd->hqk", queries, keys_h, preferred_element_type=jnp.float32)
        * score_scale
    )
    scores = jnp.where(allowed[None], scores, -1e30)
    row_max = jnp.max(scores, axis=-1, keepdims=True)
    exponent = jnp.exp(scores - row_max)
    soft_probs = exponent / jnp.sum(exponent, axis=-1, keepdims=True)
    low_probs = soft_probs.astype(jnp.bfloat16)
    context = jnp.einsum("hqk,khd->qhd", low_probs, values_h, preferred_element_type=jnp.float32)
    context = context.reshape(seq_len, features).astype(jnp.bfloat16)
    branch = jnp.dot(context, weights[:, 3 * features :], preferred_element_type=jnp.float32)
    saved = (queries, keys_h, values_h, soft_probs, low_probs, context)
    return (inputs.astype(jnp.float32) + branch, saved)


def attend_back(inputs, weights, gain_row, shift_row, allowed, upstream):
    seq_len, features = inputs.shape
    heads = features // HEAD_DIM
    score_scale = HEAD_DIM ** (-0.5)
    summed, saved = attend(inputs, weights, allowed)
    queries, keys_h, values_h, soft_probs, low_probs, context = saved
    normed, pullback = jax.vjp(layer_norm, summed, gain_row, shift_row)
    d_summed, d_gain, d_shift = pullback(upstream)
    d_branch = d_summed.astype(jnp.bfloat16)
    out_weights = weights[:, 3 * features :]
    d_out = lax.dot_general(context, d_branch, contract_rows, preferred_element_type=jnp.float32)
    d_context = lax.dot_general(
        d_branch, out_weights, contract_cols, preferred_element_type=jnp.float32
    )
    d_context = d_context.astype(jnp.bfloat16).reshape(seq_len, heads, HEAD_DIM)
    d_probs = jnp.einsum("qhd,khd->hqk", d_context, values_h, preferred_element_type=jnp.float32)
    d_values = jnp.einsum(
        "hqk,qhd->khd", low_probs, d_context, preferred_element_type=jnp.float32
    ).astype(jnp.bfloat16)
    d_scores = soft_probs * (d_probs - jnp.sum(d_probs * soft_probs, axis=-1, keepdims=True))
    d_scores = d_scores.astype(jnp.bfloat16)
    d_queries = (
        jnp.einsum("hqk,khd->qhd", d_scores, keys_h, preferred_element_type=jnp.float32)
        * score_scale
    ).astype(jnp.bfloat16)
    d_keys = (
        jnp.einsum("hqk,qhd->khd", d_scores, queries, preferred_element_type=jnp.float32)
        * score_scale
    ).astype(jnp.bfloat16)
    d_projected = jnp.concatenate(
        [
            d_queries.reshape(seq_len, features),
            d_keys.reshape(seq_len, features),
            d_values.reshape(seq_len, features),
        ],
        axis=1,
    )
    d_proj_w = lax.dot_general(
        inputs, d_projected, contract_rows, preferred_element_type=jnp.float32
    )
    d_inputs = d_summed + lax.dot_general(
        d_projected, weights[:, : 3 * features], contract_cols, preferred_element_type=jnp.float32
    )
    d_first = jnp.concatenate([d_proj_w, d_out], axis=1)
    return (d_inputs, d_first, jnp.zeros(weights.shape, jnp.float32), d_gain, d_shift)


def expand(inputs, weights, second_t):
    hidden = jnp.dot(inputs, weights, preferred_element_type=jnp.float32)
    active = jax.nn.gelu(hidden, approximate=False).astype(jnp.bfloat16)
    branch = lax.dot_general(active, second_t, contract_cols, preferred_element_type=jnp.float32)
    return (inputs.astype(jnp.float32) + branch, (hidden, active))


def gelu_exact(values):
    return jax.nn.gelu(values, approximate=False)


def expand_back(inputs, weights, second_t, gain_row, shift_row, upstream):
    summed, saved = expand(inputs, weights, second_t)
    hidden, active = saved
    normed, pullback = jax.vjp(layer_norm, summed, gain_row, shift_row)
    d_summed, d_gain, d_shift = pullback(upstream)
    d_branch = d_summed.astype(jnp.bfloat16)
    d_second = lax.dot_general(d_branch, active, contract_rows, preferred_element_type=jnp.float32)
    d_active = jnp.dot(d_branch, second_t, preferred_element_type=jnp.float32)
    activated, gelu_pull = jax.vjp(gelu_exact, hidden)
    d_hidden = gelu_pull(d_active)[0].astype(jnp.bfloat16)
    d_first = lax.dot_general(inputs, d_hidden, contract_rows, preferred_element_type=jnp.float32)
    d_inputs = d_summed + lax.dot_general(
        d_hidden, weights, contract_cols, preferred_element_type=jnp.float32
    )
    return (d_inputs, d_first, d_second, d_gain, d_shift)


def per_device(section_rows, span_lengths, first_weights, second_weights, norm_gain, norm_shift):
    section_id = lax.axis_index("section")
    section_count = lax.axis_size("section")
    rows_local = section_rows[0]
    total_tokens, features = rows_local.shape
    seq_len = SEQ
    micro_count = total_tokens // seq_len
    weights = first_weights[0]
    own_half = second_weights[0]
    gain_row = norm_gain[0]
    shift_row = norm_shift[0]
    parity = section_id % 2
    lower_half = passed_along(own_half, "section", 1)
    second_t = jnp.concatenate([lower_half, own_half], axis=1)
    steps_total = micro_count + section_count - 1

    def empty_forward(inputs, allowed):
        return jnp.zeros(inputs.shape, jnp.float32)

    def attend_forward(inputs, allowed):
        summed, saved = attend(inputs, weights, allowed)
        return layer_norm(summed, gain_row, shift_row)

    def expand_forward(inputs, allowed):
        summed, saved = expand(inputs, weights, second_t)
        return layer_norm(summed, gain_row, shift_row)

    def forward_step(step_index, carried):
        arrived, arrived_skip, kept_inputs, results = carried
        micro_index = step_index - section_id
        active = (micro_index >= 0) & (micro_index < micro_count)
        micro_slot = jnp.clip(micro_index, 0, micro_count - 1)
        lengths = lax.dynamic_index_in_dim(span_lengths, micro_slot, 0, keepdims=False)
        leading, allowed = span_tables(lengths, seq_len)
        own_rows = lax.dynamic_slice_in_dim(rows_local, micro_slot * seq_len, seq_len, 0)
        head_rows = jnp.where(leading[:, None], arrived, arrived_skip)
        inputs = jnp.where(
            section_id == 0, own_rows, jnp.where(section_id == 2, head_rows, arrived)
        )
        choose = jnp.where(active, 1 + parity, 0)
        output = lax.switch(
            choose, [empty_forward, attend_forward, expand_forward], inputs, allowed
        )
        old_input = lax.dynamic_slice_in_dim(kept_inputs, micro_slot * seq_len, seq_len, 0)
        kept_inputs = lax.dynamic_update_slice_in_dim(
            kept_inputs, jnp.where(active, inputs, old_input), micro_slot * seq_len, 0
        )
        stored = jnp.where(section_id == 2, arrived.astype(jnp.float32), output)
        old_result = lax.dynamic_slice_in_dim(results, micro_slot * seq_len, seq_len, 0)
        results = lax.dynamic_update_slice_in_dim(
            results, jnp.where(active, stored, old_result), micro_slot * seq_len, 0
        )
        arrived, arrived_skip = passed_along((output.astype(jnp.bfloat16), own_rows), "section", 1)
        return (arrived, arrived_skip, kept_inputs, results)

    start_rows = jnp.zeros((seq_len, features), jnp.bfloat16)
    kept_start = jnp.zeros((total_tokens, features), jnp.bfloat16)
    results_start = jnp.zeros((total_tokens, features), jnp.float32)
    arrived, arrived_skip, kept_inputs, results = lax.fori_loop(
        0, steps_total, forward_step, (start_rows, start_rows, kept_start, results_start)
    )
    ff_cols = weights.shape[1]

    def empty_backward(inputs, upstream, allowed):
        zero_cols = jnp.zeros((features, ff_cols), jnp.float32)
        zero_row = jnp.zeros((features,), jnp.float32)
        return (jnp.zeros(upstream.shape, jnp.float32), zero_cols, zero_cols, zero_row, zero_row)

    def attend_backward(inputs, upstream, allowed):
        return attend_back(inputs, weights, gain_row, shift_row, allowed, upstream)

    def expand_backward(inputs, upstream, allowed):
        return expand_back(inputs, weights, second_t, gain_row, shift_row, upstream)

    grad_start = (
        jnp.zeros((features, ff_cols), jnp.float32),
        jnp.zeros((features, ff_cols), jnp.float32),
        jnp.zeros((features,), jnp.float32),
        jnp.zeros((features,), jnp.float32),
    )

    def backward_step(step_index, carried):
        arrived, arrived_skip, results, skip_grads, gradients = carried
        micro_index = step_index - (section_count - 1 - section_id)
        active = (micro_index >= 0) & (micro_index < micro_count)
        micro_slot = jnp.clip(micro_index, 0, micro_count - 1)
        lengths = lax.dynamic_index_in_dim(span_lengths, micro_slot, 0, keepdims=False)
        leading, allowed = span_tables(lengths, seq_len)
        own_rows = lax.dynamic_slice_in_dim(rows_local, micro_slot * seq_len, seq_len, 0).astype(
            jnp.float32
        )
        upstream = jnp.where(section_id == section_count - 1, own_rows, arrived.astype(jnp.float32))
        inputs = lax.dynamic_slice_in_dim(kept_inputs, micro_slot * seq_len, seq_len, 0)
        choose = jnp.where(active, 1 + parity, 0)
        d_inputs, d_first, d_second, d_gain, d_shift = lax.switch(
            choose, [empty_backward, attend_backward, expand_backward], inputs, upstream, allowed
        )
        at_head = jnp.where(leading[:, None], d_inputs, 0.0) + own_rows
        sent = jnp.where(section_id == 2, at_head, d_inputs).astype(jnp.bfloat16)
        skip_part = jnp.where(leading[:, None], 0.0, d_inputs).astype(jnp.bfloat16)
        old_skip = lax.dynamic_slice_in_dim(skip_grads, micro_slot * seq_len, seq_len, 0)
        skip_grads = lax.dynamic_update_slice_in_dim(
            skip_grads,
            jnp.where(active & (section_id == 1), arrived_skip, old_skip),
            micro_slot * seq_len,
            0,
        )
        old_result = lax.dynamic_slice_in_dim(results, micro_slot * seq_len, seq_len, 0)
        results = lax.dynamic_update_slice_in_dim(
            results,
            jnp.where(active & (section_id == 0), d_inputs, old_result),
            micro_slot * seq_len,
            0,
        )
        gradients = (
            gradients[0] + d_first,
            gradients[1] + d_second,
            gradients[2] + d_gain,
            gradients[3] + d_shift,
        )
        arrived, arrived_skip = passed_along((sent, skip_part), "section", -1)
        return (arrived, arrived_skip, results, skip_grads, gradients)

    arrived, arrived_skip, results, skip_grads, gradients = lax.fori_loop(
        0, steps_total, backward_step, (start_rows, start_rows, results, kept_start, grad_start)
    )
    first_sum, second_sum, gain_sum, shift_sum = gradients
    half_cols = own_half.shape[1]
    from_next = passed_along(second_sum[:, :half_cols].astype(jnp.bfloat16), "section", -1).astype(
        jnp.float32
    )
    second_own = jnp.where(parity == 1, second_sum[:, half_cols:], from_next)
    first_sum, second_own, gain_sum, shift_sum = lax.psum(
        (first_sum, second_own, gain_sum, shift_sum), "dp"
    )
    results = jnp.where(section_id == 1, skip_grads.astype(jnp.float32), results)
    return (results[None], first_sum[None], second_own[None], gain_sum[None], shift_sum[None])


def solution(mesh):
    in_specs = (
        P("section", "dp", None),
        P("dp", None),
        P("section", None, None),
        P("section", None, None),
        P("section", None),
        P("section", None),
    )
    out_specs = (
        P("section", "dp", None),
        P("section", None, None),
        P("section", None, None),
        P("section", None),
        P("section", None),
    )
    return jax.shard_map(
        per_device, mesh=mesh, in_specs=in_specs, out_specs=out_specs, check_vma=False
    )
```

profile of v0, /device:TPU:0, one launch (start us, length us, event | category | flops | bytes accessed | tf_op | source)
XLA Modules:
  0.0 1487.1 jit_solution(17050838300599295596)
XLA Ops:
  23.3 277.6 %while.51 = (s32[]{:T(128)}, bf16[512,768]{1,0:T(8,128)(2,1)S(1)}, bf16[512,768]{1,0:T(8,128)(2,1)S(1)}, bf16[1536,768]{1,0:T(8,128)(2,1)}, f32[1536,768]{1,0:T(...) while((s32[]{:T(128)}, bf16[512,768]{1,0:T(8,128)(2,1)S(1)}, ...), condition=%wide.region_13.14_spmd, body=%wide.region_0.13_spmd.sunk | while | flops 4941163520 | bytes 78499096 | solution.py:196
  28.5 21.9 %conditional.5 = (f32[512,768]{1,0:T(8,128)S(1)}) conditional(s32[]{:T(128)} %clamp.21, () %tuple.135, (bf16[512,768]{1,0:T(8,128)(2,1)}, bf16[768,3072]{1,0:T(8,128)(2,1)}, s32[512,6]{0,1:T(8,128)S(1)}, f32[1,768]{1,0:T(1,128)S(1)}, f32[1,768]{1,0:T(1,128)S(1)}) %tuple.136, (bf16[512,768]{1,0:T(8,128)(2,1)}, ...), branch_computations={%region_3.3_spmd, %region_4.9_spmd, %region_10.12_spmd} | conditional | flops 4938007040 | bytes 57249840 | solution.py:178
  69.6 21.9 %conditional.5 = (f32[512,768]{1,0:T(8,128)S(1)}) conditional(s32[]{:T(128)} %clamp.21, () %tuple.135, (bf16[512,768]{1,0:T(8,128)(2,1)}, bf16[768,3072]{1,0:T(8,128)(2,1)}, s32[512,6]{0,1:T(8,128)S(1)}, f32[1,768]{1,0:T(1,128)S(1)}, f32[1,768]{1,0:T(1,128)S(1)}) %tuple.136, (bf16[512,768]{1,0:T(8,128)(2,1)}, ...), branch_computations={%region_3.3_spmd, %region_4.9_spmd, %region_10.12_spmd} | conditional | flops 4938007040 | bytes 57249840 | solution.py:178
  94.7 15.4 %collective-permute-start = (bf16[512,768]{1,0:T(8,128)(2,1)}, bf16[512,768]{1,0:T(8,128)(2,1)S(1)}, u32[]{:S(2)}, u32[]{:S(2)}) collective-permute-start(bf16[512,768]{1,0:T(8,128)(2,1)} %get-tuple-element.1231), channel_id=1, source_target_pairs={{0,8},{8,16},{16,24},{1,9},{9,17},{17,25},{2,10},{10,18},{18,26},{... | collective-permute-start | bytes 2359304 | tf_op jit(solution)/shard_map/while/body/eval_jaxpr/ppermute | solution.py:18
  119.2 21.9 %conditional.5 = (f32[512,768]{1,0:T(8,128)S(1)}) conditional(s32[]{:T(128)} %clamp.21, () %tuple.135, (bf16[512,768]{1,0:T(8,128)(2,1)}, bf16[768,3072]{1,0:T(8,128)(2,1)}, s32[512,6]{0,1:T(8,128)S(1)}, f32[1,768]{1,0:T(1,128)S(1)}, f32[1,768]{1,0:T(1,128)S(1)}) %tuple.136, (bf16[512,768]{1,0:T(8,128)(2,1)}, ...), branch_computations={%region_3.3_spmd, %region_4.9_spmd, %region_10.12_spmd} | conditional | flops 4938007040 | bytes 57249840 | solution.py:178
  144.3 15.4 %collective-permute-start = (bf16[512,768]{1,0:T(8,128)(2,1)}, bf16[512,768]{1,0:T(8,128)(2,1)S(1)}, u32[]{:S(2)}, u32[]{:S(2)}) collective-permute-start(bf16[512,768]{1,0:T(8,128)(2,1)} %get-tuple-element.1231), channel_id=1, source_target_pairs={{0,8},{8,16},{16,24},{1,9},{9,17},{17,25},{2,10},{10,18},{18,26},{... | collective-permute-start | bytes 2359304 | tf_op jit(solution)/shard_map/while/body/eval_jaxpr/ppermute | solution.py:18
  174.8 37.1 %collective-permute-start = (bf16[512,768]{1,0:T(8,128)(2,1)}, bf16[512,768]{1,0:T(8,128)(2,1)S(1)}, u32[]{:S(2)}, u32[]{:S(2)}) collective-permute-start(bf16[512,768]{1,0:T(8,128)(2,1)} %get-tuple-element.1231), channel_id=1, source_target_pairs={{0,8},{8,16},{16,24},{1,9},{9,17},{17,25},{2,10},{10,18},{18,26},{... | collective-permute-start | bytes 2359304 | tf_op jit(solution)/shard_map/while/body/eval_jaxpr/ppermute | solution.py:18
  226.9 15.6 %collective-permute-start = (bf16[512,768]{1,0:T(8,128)(2,1)}, bf16[512,768]{1,0:T(8,128)(2,1)S(1)}, u32[]{:S(2)}, u32[]{:S(2)}) collective-permute-start(bf16[512,768]{1,0:T(8,128)(2,1)} %get-tuple-element.1231), channel_id=1, source_target_pairs={{0,8},{8,16},{16,24},{1,9},{9,17},{17,25},{2,10},{10,18},{18,26},{... | collective-permute-start | bytes 2359304 | tf_op jit(solution)/shard_map/while/body/eval_jaxpr/ppermute | solution.py:18
  242.5 26.0 %collective-permute-start.1 = (bf16[512,768]{1,0:T(8,128)(2,1)}, bf16[512,768]{1,0:T(8,128)(2,1)S(1)}, u32[]{:S(2)}, u32[]{:S(2)}) collective-permute-start(bf16[512,768]{1,0:T(8,128)(2,1)} %get-tuple-element.1232), channel_id=1, source_target_pairs={{0,8},{8,16},{16,24},{1,9},{9,17},{17,25},{2,10},{10,18},{18,26},{... | collective-permute-start | bytes 2359304 | tf_op jit(solution)/shard_map/while/body/eval_jaxpr/ppermute | solution.py:18
  279.0 15.6 %collective-permute-start = (bf16[512,768]{1,0:T(8,128)(2,1)}, bf16[512,768]{1,0:T(8,128)(2,1)S(1)}, u32[]{:S(2)}, u32[]{:S(2)}) collective-permute-start(bf16[512,768]{1,0:T(8,128)(2,1)} %get-tuple-element.1231), channel_id=1, source_target_pairs={{0,8},{8,16},{16,24},{1,9},{9,17},{17,25},{2,10},{10,18},{18,26},{... | collective-permute-start | bytes 2359304 | tf_op jit(solution)/shard_map/while/body/eval_jaxpr/ppermute | solution.py:18
  303.5 684.5 %while.52 = (s32[]{:T(128)}, bf16[512,768]{1,0:T(8,128)(2,1)S(1)}, bf16[512,768]{1,0:T(8,128)(2,1)}, f32[1536,768]{1,0:T(8,128)}, bf16[1536,768]{1,0:T(8,128)(2,...) while((s32[]{:T(128)}, bf16[512,768]{1,0:T(8,128)(2,1)S(1)}, ...), condition=%wide.region_36.37_spmd.clone, body=%wide.region_14.36_spmd.clone.sunk | while | flops 14644165632 | bytes 382330496 | solution.py:261
  317.2 14.2 conditional.6
  384.8 11.3 select_add_fusion.7
  396.1 13.0 select_add_fusion.8
  446.9 13.0 select_add_fusion.8
  462.2 122.1 %collective-permute-done.3 = bf16[512,768]{1,0:T(8,128)(2,1)S(1)} collective-permute-done((bf16[512,768]{1,0:T(8,128)(2,1)S(1)}, bf16[512,768]{1,0:T(8,128)(2,1)S(1)}, u32[]{:S(2)}, u32[]{:S(2)}) %collective-permute-start.3) | collective-permute-done | bytes 786464 | tf_op jit(solution)/shard_map/while/body/eval_jaxpr/ppermute | solution.py:18
  590.2 90.6 %conditional.6 = (f32[512,768]{1,0:T(8,128)}, f32[768,3072]{0,1:T(8,128)}, f32[768,3072]{1,0:T(8,128)}, f32[768]{0:T(1024)S(1)}, f32[768]{0:T(1024)S(1)}) conditional(s32[]{:T(128)} %clamp.22, () %tuple.141, (f32[1,768]{1,0:T(1,128)S(1)}, f32[512,768]{1,0:T(8,128)S(1)}, bf16[512,768]{1,0:T(8,128)(2,1)S(1)}, ...), branch_computations={%region_17.17_spmd, %region_18.28_spmd, %region_29.35_spmd} | conditional | flops 14630389760 | bytes 298859168 | solution.py:232
  700.1 13.0 select_add_fusion.8
  726.4 90.4 %conditional.6 = (f32[512,768]{1,0:T(8,128)}, f32[768,3072]{0,1:T(8,128)}, f32[768,3072]{1,0:T(8,128)}, f32[768]{0:T(1024)S(1)}, f32[768]{0:T(1024)S(1)}) conditional(s32[]{:T(128)} %clamp.22, () %tuple.141, (f32[1,768]{1,0:T(1,128)S(1)}, f32[512,768]{1,0:T(8,128)S(1)}, bf16[512,768]{1,0:T(8,128)(2,1)S(1)}, ...), branch_computations={%region_17.17_spmd, %region_18.28_spmd, %region_29.35_spmd} | conditional | flops 14630389760 | bytes 298859168 | solution.py:232
  836.2 13.0 select_add_fusion.8
  858.9 90.7 %conditional.6 = (f32[512,768]{1,0:T(8,128)}, f32[768,3072]{0,1:T(8,128)}, f32[768,3072]{1,0:T(8,128)}, f32[768]{0:T(1024)S(1)}, f32[768]{0:T(1024)S(1)}) conditional(s32[]{:T(128)} %clamp.22, () %tuple.141, (f32[1,768]{1,0:T(1,128)S(1)}, f32[512,768]{1,0:T(8,128)S(1)}, bf16[512,768]{1,0:T(8,128)(2,1)S(1)}, ...), branch_computations={%region_17.17_spmd, %region_18.28_spmd, %region_29.35_spmd} | conditional | flops 14630389760 | bytes 298859168 | solution.py:232
  969.0 13.0 select_add_fusion.8
  1009.6 22.5 %all-reduce = (f32[1,768]{1,0:T(1,128)}, f32[1,768]{1,0:T(1,128)}) all-reduce(f32[1,768]{1,0:T(1,128)S(1)} %broadcast_in_dim.170, f32[1,768]{1,0:T(1,128)S(1)} %broadcast_in_dim.171), channel_id=1, replica_groups=mesh['section'=4,'dp'=8] {'dp'}, use_global_device_ids=true, to_apply=%region_39.40 | all-reduce | flops 1536 | bytes 12288 | tf_op jit(solution)/shard_map/psum | solution.py:270
  1037.9 431.2 %all-reduce.4.cloned.1.call-done = (f32[1,768,3072]{2,1,0:T(8,128)}, f32[1,768,1536]{2,1,0:T(8,128)}) async-done(((f32[1,768,3072]{2,1,0:T(8,128)}, f32[1,768,1536]{2,1,0:T(8,128)}), (f32[1,768,3072]{2,1,0:T(8,128)}, f32[1,768,1536]{2,1,0:T(8,128)})) %all-reduce.4.cloned.1.call-update) | async-done | bytes 14155792 | tf_op jit(solution)/shard_map/psum | solution.py:270
  (601 shorter events, 675.7 us)
Async XLA Ops:
  7.2 1461.9 %all-reduce.4.cloned.1.call-start = ((), (), s32[]{:S(2)}) async-start(), calls=%async_computation | async-start | bytes 28311552 | tf_op jit(solution)/shard_map/psum | solution.py:270
  7.2 6.9 collective-permute-start.4
  53.7 8.8 collective-permute-start
  94.7 17.4 %collective-permute-start = (bf16[512,768]{1,0:T(8,128)(2,1)}, bf16[512,768]{1,0:T(8,128)(2,1)S(1)}, u32[]{:S(2)}, u32[]{:S(2)}) collective-permute-start(bf16[512,768]{1,0:T(8,128)(2,1)} %get-tuple-element.1231), channel_id=1, source_target_pairs={{0,8},{8,16},{16,24},{1,9},{9,17},{17,25},{2,10},{10,18},{18,26},{... | collective-permute-start | bytes 2359304 | tf_op jit(solution)/shard_map/while/body/eval_jaxpr/ppermute | solution.py:18
  144.3 20.0 %collective-permute-start = (bf16[512,768]{1,0:T(8,128)(2,1)}, bf16[512,768]{1,0:T(8,128)(2,1)S(1)}, u32[]{:S(2)}, u32[]{:S(2)}) collective-permute-start(bf16[512,768]{1,0:T(8,128)(2,1)} %get-tuple-element.1231), channel_id=1, source_target_pairs={{0,8},{8,16},{16,24},{1,9},{9,17},{17,25},{2,10},{10,18},{18,26},{... | collective-permute-start | bytes 2359304 | tf_op jit(solution)/shard_map/while/body/eval_jaxpr/ppermute | solution.py:18
  159.7 6.7 collective-permute-start.1
  174.8 41.7 %collective-permute-start = (bf16[512,768]{1,0:T(8,128)(2,1)}, bf16[512,768]{1,0:T(8,128)(2,1)S(1)}, u32[]{:S(2)}, u32[]{:S(2)}) collective-permute-start(bf16[512,768]{1,0:T(8,128)(2,1)} %get-tuple-element.1231), channel_id=1, source_target_pairs={{0,8},{8,16},{16,24},{1,9},{9,17},{17,25},{2,10},{10,18},{18,26},{... | collective-permute-start | bytes 2359304 | tf_op jit(solution)/shard_map/while/body/eval_jaxpr/ppermute | solution.py:18
  211.8 6.6 collective-permute-start.1
  226.9 41.6 %collective-permute-start = (bf16[512,768]{1,0:T(8,128)(2,1)}, bf16[512,768]{1,0:T(8,128)(2,1)S(1)}, u32[]{:S(2)}, u32[]{:S(2)}) collective-permute-start(bf16[512,768]{1,0:T(8,128)(2,1)} %get-tuple-element.1231), channel_id=1, source_target_pairs={{0,8},{8,16},{16,24},{1,9},{9,17},{17,25},{2,10},{10,18},{18,26},{... | collective-permute-start | bytes 2359304 | tf_op jit(solution)/shard_map/while/body/eval_jaxpr/ppermute | solution.py:18
  242.5 28.1 %collective-permute-start.1 = (bf16[512,768]{1,0:T(8,128)(2,1)}, bf16[512,768]{1,0:T(8,128)(2,1)S(1)}, u32[]{:S(2)}, u32[]{:S(2)}) collective-permute-start(bf16[512,768]{1,0:T(8,128)(2,1)} %get-tuple-element.1232), channel_id=1, source_target_pairs={{0,8},{8,16},{16,24},{1,9},{9,17},{17,25},{2,10},{10,18},{18,26},{... | collective-permute-start | bytes 2359304 | tf_op jit(solution)/shard_map/while/body/eval_jaxpr/ppermute | solution.py:18
  279.0 19.9 %collective-permute-start = (bf16[512,768]{1,0:T(8,128)(2,1)}, bf16[512,768]{1,0:T(8,128)(2,1)S(1)}, u32[]{:S(2)}, u32[]{:S(2)}) collective-permute-start(bf16[512,768]{1,0:T(8,128)(2,1)} %get-tuple-element.1231), channel_id=1, source_target_pairs={{0,8},{8,16},{16,24},{1,9},{9,17},{17,25},{2,10},{10,18},{18,26},{... | collective-permute-start | bytes 2359304 | tf_op jit(solution)/shard_map/while/body/eval_jaxpr/ppermute | solution.py:18
  335.2 26.3 %collective-permute-start.2 = (bf16[512,768]{1,0:T(8,128)(2,1)}, bf16[512,768]{1,0:T(8,128)(2,1)S(1)}, u32[]{:S(2)}, u32[]{:S(2)}) collective-permute-start(bf16[512,768]{1,0:T(8,128)(2,1)} %get-tuple-element.1257), channel_id=1, source_target_pairs={{8,0},{16,8},{24,16},{9,1},{17,9},{25,17},{10,2},{18,10},{26,18},{... | collective-permute-start | bytes 2359304 | tf_op jit(solution)/shard_map/while/body/eval_jaxpr/ppermute | solution.py:18
  338.1 22.6 %collective-permute-start.3 = (bf16[512,768]{1,0:T(8,128)(2,1)S(1)}, bf16[512,768]{1,0:T(8,128)(2,1)S(1)}, u32[]{:S(2)}, u32[]{:S(2)}) collective-permute-start(bf16[512,768]{1,0:T(8,128)(2,1)S(1)} %select_convert_fusion.2), channel_id=1, source_target_pairs={{8,0},{16,8},{24,16},{9,1},{17,9},{25,17},{10,2},{18,10},{26,18},{... | collective-permute-start | bytes 2359304 | tf_op jit(solution)/shard_map/while/body/eval_jaxpr/ppermute | solution.py:18
  380.6 31.7 %collective-permute-start.2 = (bf16[512,768]{1,0:T(8,128)(2,1)}, bf16[512,768]{1,0:T(8,128)(2,1)S(1)}, u32[]{:S(2)}, u32[]{:S(2)}) collective-permute-start(bf16[512,768]{1,0:T(8,128)(2,1)} %get-tuple-element.1257), channel_id=1, source_target_pairs={{8,0},{16,8},{24,16},{9,1},{17,9},{25,17},{10,2},{18,10},{26,18},{... | collective-permute-start | bytes 2359304 | tf_op jit(solution)/shard_map/while/body/eval_jaxpr/ppermute | solution.py:18
  383.5 27.9 %collective-permute-start.3 = (bf16[512,768]{1,0:T(8,128)(2,1)S(1)}, bf16[512,768]{1,0:T(8,128)(2,1)S(1)}, u32[]{:S(2)}, u32[]{:S(2)}) collective-permute-start(bf16[512,768]{1,0:T(8,128)(2,1)S(1)} %select_convert_fusion.2), channel_id=1, source_target_pairs={{8,0},{16,8},{24,16},{9,1},{17,9},{25,17},{10,2},{18,10},{26,18},{... | collective-permute-start | bytes 2359304 | tf_op jit(solution)/shard_map/while/body/eval_jaxpr/ppermute | solution.py:18
  431.4 153.8 %collective-permute-start.2 = (bf16[512,768]{1,0:T(8,128)(2,1)}, bf16[512,768]{1,0:T(8,128)(2,1)S(1)}, u32[]{:S(2)}, u32[]{:S(2)}) collective-permute-start(bf16[512,768]{1,0:T(8,128)(2,1)} %get-tuple-element.1257), channel_id=1, source_target_pairs={{8,0},{16,8},{24,16},{9,1},{17,9},{25,17},{10,2},{18,10},{26,18},{... | collective-permute-start | bytes 2359304 | tf_op jit(solution)/shard_map/while/body/eval_jaxpr/ppermute | solution.py:18
  434.3 150.1 %collective-permute-start.3 = (bf16[512,768]{1,0:T(8,128)(2,1)S(1)}, bf16[512,768]{1,0:T(8,128)(2,1)S(1)}, u32[]{:S(2)}, u32[]{:S(2)}) collective-permute-start(bf16[512,768]{1,0:T(8,128)(2,1)S(1)} %select_convert_fusion.2), channel_id=1, source_target_pairs={{8,0},{16,8},{24,16},{9,1},{17,9},{25,17},{10,2},{18,10},{26,18},{... | collective-permute-start | bytes 2359304 | tf_op jit(solution)/shard_map/while/body/eval_jaxpr/ppermute | solution.py:18
  684.6 36.7 %collective-permute-start.2 = (bf16[512,768]{1,0:T(8,128)(2,1)}, bf16[512,768]{1,0:T(8,128)(2,1)S(1)}, u32[]{:S(2)}, u32[]{:S(2)}) collective-permute-start(bf16[512,768]{1,0:T(8,128)(2,1)} %get-tuple-element.1257), channel_id=1, source_target_pairs={{8,0},{16,8},{24,16},{9,1},{17,9},{25,17},{10,2},{18,10},{26,18},{... | collective-permute-start | bytes 2359304 | tf_op jit(solution)/shard_map/while/body/eval_jaxpr/ppermute | solution.py:18
  687.5 33.0 %collective-permute-start.3 = (bf16[512,768]{1,0:T(8,128)(2,1)S(1)}, bf16[512,768]{1,0:T(8,128)(2,1)S(1)}, u32[]{:S(2)}, u32[]{:S(2)}) collective-permute-start(bf16[512,768]{1,0:T(8,128)(2,1)S(1)} %select_convert_fusion.2), channel_id=1, source_target_pairs={{8,0},{16,8},{24,16},{9,1},{17,9},{25,17},{10,2},{18,10},{26,18},{... | collective-permute-start | bytes 2359304 | tf_op jit(solution)/shard_map/while/body/eval_jaxpr/ppermute | solution.py:18
  820.7 33.0 %collective-permute-start.2 = (bf16[512,768]{1,0:T(8,128)(2,1)}, bf16[512,768]{1,0:T(8,128)(2,1)S(1)}, u32[]{:S(2)}, u32[]{:S(2)}) collective-permute-start(bf16[512,768]{1,0:T(8,128)(2,1)} %get-tuple-element.1257), channel_id=1, source_target_pairs={{8,0},{16,8},{24,16},{9,1},{17,9},{25,17},{10,2},{18,10},{26,18},{... | collective-permute-start | bytes 2359304 | tf_op jit(solution)/shard_map/while/body/eval_jaxpr/ppermute | solution.py:18
  823.6 29.2 %collective-permute-start.3 = (bf16[512,768]{1,0:T(8,128)(2,1)S(1)}, bf16[512,768]{1,0:T(8,128)(2,1)S(1)}, u32[]{:S(2)}, u32[]{:S(2)}) collective-permute-start(bf16[512,768]{1,0:T(8,128)(2,1)S(1)} %select_convert_fusion.2), channel_id=1, source_target_pairs={{8,0},{16,8},{24,16},{9,1},{17,9},{25,17},{10,2},{18,10},{26,18},{... | collective-permute-start | bytes 2359304 | tf_op jit(solution)/shard_map/while/body/eval_jaxpr/ppermute | solution.py:18
  953.5 31.7 %collective-permute-start.2 = (bf16[512,768]{1,0:T(8,128)(2,1)}, bf16[512,768]{1,0:T(8,128)(2,1)S(1)}, u32[]{:S(2)}, u32[]{:S(2)}) collective-permute-start(bf16[512,768]{1,0:T(8,128)(2,1)} %get-tuple-element.1257), channel_id=1, source_target_pairs={{8,0},{16,8},{24,16},{9,1},{17,9},{25,17},{10,2},{18,10},{26,18},{... | collective-permute-start | bytes 2359304 | tf_op jit(solution)/shard_map/while/body/eval_jaxpr/ppermute | solution.py:18
  956.3 27.9 %collective-permute-start.3 = (bf16[512,768]{1,0:T(8,128)(2,1)S(1)}, bf16[512,768]{1,0:T(8,128)(2,1)S(1)}, u32[]{:S(2)}, u32[]{:S(2)}) collective-permute-start(bf16[512,768]{1,0:T(8,128)(2,1)S(1)} %select_convert_fusion.2), channel_id=1, source_target_pairs={{8,0},{16,8},{24,16},{9,1},{17,9},{25,17},{10,2},{18,10},{26,18},{... | collective-permute-start | bytes 2359304 | tf_op jit(solution)/shard_map/while/body/eval_jaxpr/ppermute | solution.py:18
  992.0 10.9 collective-permute-start.5
  (128 other events, 1510.9 us)
Sparse Core Ops, SparseCore 0:
  1009.0 459.9 all-reduce.3
where the time goes:
time: 1510 us; the launch traced here: 1490 us
  waiting for transfers between devices  575 us (38%)
  other arithmetic  316 us (21%)
  matrix products  217 us (14%)
  starting transfers between devices  170 us (11%)
  local copies, waits for them, and re-layouts  131 us (9%)
  loops' own time  40.7 us (3%)
  blocking collectives  22.5 us (1%)
    psum x1, waiting for transfers between devices, per_device(): lax.psum((first_sum, second_own, gain_sum, shift_sum), 'dp')  431 us
    ppermute x26, starting transfers between devices, passed_along(): return lax.ppermute(block, axis, route)  170 us
    ppermute x26, waiting for transfers between devices, passed_along(): return lax.ppermute(block, axis, route)  144 us
    add x6, other arithmetic, backward_step(): gradients[1] + d_second  75.5 us
    add x6, other arithmetic, backward_step(): gradients[0] + d_first  65.2 us
    another operation x33, local copies, waits for them, and re-layouts  54.1 us
    sub x6, matrix products, attend(): exponent = jnp.exp(scores - row_max)  53.7 us
    dot_general x6, matrix products, attend(): jnp.einsum('hqk,khd->qhd', low_probs, values_h, preferred_element_type=jn...  35.9 us
  transfers between devices with their start and end apart: 27, of which 12 were waited for; matrix products, arithmetic and copies ran while one was open for 12% of the time, Pallas kernels for 0%

commit v1 on v0

v1 whole, which is shorter than its diff:
```python
import jax
import jax.numpy as jnp
from jax import lax
from jax.sharding import PartitionSpec as P

HEAD_DIM = 64
SEQ = 512
BLOCK = 256
LEADS = 16

epsilon = 1e-12
f32 = jnp.float32
bf16 = jnp.bfloat16
rows_rows = (((0,), (0,)), ((), ()))
cols_cols = (((1,), (1,)), ((), ()))


def normalize(summed):
    centered = summed - jnp.mean(summed, axis=-1, keepdims=True)
    rstd = lax.rsqrt(jnp.mean(centered * centered, axis=-1, keepdims=True) + epsilon)
    return centered * rstd, rstd


def normalize_back(zh, rstd, gain, upstream):
    g = upstream * gain
    mean_g = jnp.mean(g, axis=-1, keepdims=True)
    mean_gz = jnp.mean(g * zh, axis=-1, keepdims=True)
    d_gain = jnp.sum(upstream * zh, axis=0)
    d_shift = jnp.sum(upstream, axis=0)
    return rstd * (g - mean_g - zh * mean_gz), d_gain, d_shift


def attend(inputs, weights, gain, shift, allowed):
    tokens, features = inputs.shape
    heads = features // HEAD_DIM
    blocks = tokens // BLOCK
    qkv = jnp.dot(inputs, weights[:, : 3 * features], preferred_element_type=f32).astype(bf16)
    split = qkv.reshape(blocks, BLOCK, 3, heads, HEAD_DIM)
    q, k, v = split[:, :, 0], split[:, :, 1], split[:, :, 2]
    scores = jnp.einsum("bqhd,bkhd->bhqk", q, k, preferred_element_type=f32) * HEAD_DIM**-0.5
    scores = jnp.where(allowed[:, None], scores, -1e30)
    exponent = jnp.exp(scores - jnp.max(scores, axis=-1, keepdims=True))
    probs = exponent / jnp.sum(exponent, axis=-1, keepdims=True)
    low_probs = probs.astype(bf16)
    ctx = jnp.einsum("bhqk,bkhd->bqhd", low_probs, v, preferred_element_type=f32)
    ctx = ctx.reshape(tokens, features).astype(bf16)
    branch = jnp.dot(ctx, weights[:, 3 * features :], preferred_element_type=f32)
    zh, rstd = normalize(inputs.astype(f32) + branch)
    return zh * gain + shift, (q, k, v, low_probs, ctx, zh, rstd)


def attend_back(saved, weights, gain, upstream):
    q, k, v, low_probs, ctx, zh, rstd = saved
    tokens, features = ctx.shape
    blocks, _, heads, _ = q.shape
    scale = HEAD_DIM**-0.5
    dz, d_gain, d_shift = normalize_back(zh, rstd, gain, upstream)
    d_out = dz.astype(bf16)
    d_ctx = lax.dot_general(
        d_out, weights[:, 3 * features :], cols_cols, preferred_element_type=f32
    ).astype(bf16)
    d_ctx = d_ctx.reshape(blocks, BLOCK, heads, HEAD_DIM)
    probs = low_probs.astype(f32)
    d_probs = jnp.einsum("bqhd,bkhd->bhqk", d_ctx, v, preferred_element_type=f32)
    ds = probs * (d_probs - jnp.sum(d_probs * probs, axis=-1, keepdims=True))
    ds = ds.astype(bf16)
    dv = jnp.einsum("bhqk,bqhd->bkhd", low_probs, d_ctx, preferred_element_type=f32)
    dq = jnp.einsum("bhqk,bkhd->bqhd", ds, k, preferred_element_type=f32) * scale
    dk = jnp.einsum("bhqk,bqhd->bkhd", ds, q, preferred_element_type=f32) * scale
    dqkv = jnp.concatenate(
        [t.reshape(tokens, features).astype(bf16) for t in (dq, dk, dv)], axis=1
    )
    dx = dz + lax.dot_general(
        dqkv, weights[:, : 3 * features], cols_cols, preferred_element_type=f32
    )
    return dx, d_out, dqkv, d_gain, d_shift


def expand(inputs, w_up, w_down, gain, shift):
    u = jnp.dot(inputs, w_up, preferred_element_type=f32)
    cdf = 0.5 * (1.0 + lax.erf(u * (0.5**0.5)))
    pdf = jnp.exp(-0.5 * u * u) * 0.3989422804014327
    a = (u * cdf).astype(bf16)
    slope = (cdf + u * pdf).astype(bf16)
    branch = lax.dot_general(a, w_down, cols_cols, preferred_element_type=f32)
    zh, rstd = normalize(inputs.astype(f32) + branch)
    return zh * gain + shift, (a, slope, zh, rstd)


def expand_back(saved, w_up, w_down, gain, upstream):
    a, slope, zh, rstd = saved
    dz, d_gain, d_shift = normalize_back(zh, rstd, gain, upstream)
    df = dz.astype(bf16)
    da = jnp.dot(df, w_down, preferred_element_type=f32)
    du = (da * slope.astype(f32)).astype(bf16)
    dx = dz + lax.dot_general(du, w_up, cols_cols, preferred_element_type=f32)
    return dx, df, du, d_gain, d_shift


def row_tables(lengths, core):
    rows, spans = lengths.shape
    order = jnp.arange(spans)
    ends = jnp.sum(jnp.where(order[:, None] <= order[None, :], lengths[:, :, None], 0), axis=1)
    starts = ends - lengths
    first = jnp.sum(jnp.where(lengths == BLOCK, starts, 0), axis=1)
    place = jnp.arange(SEQ)
    origin = (place[None, :] + first[:, None]) % SEQ
    roll = (origin[:, :, None] == place[None, None, :]).astype(bf16)
    mine = lax.dynamic_slice_in_dim(origin, core * BLOCK, BLOCK, 1)
    segment = jnp.sum((mine[:, :, None] >= ends[:, None, :]).astype(jnp.int32), axis=2)
    allowed = segment[:, :, None] == segment[:, None, :]
    lead = (starts[:, : spans - 1] - first[:, None]) % SEQ
    spot = jnp.where(lead // BLOCK == core, jnp.arange(rows)[:, None] * BLOCK + lead % BLOCK, -1)
    spot = jnp.concatenate([spot.reshape(-1), jnp.full((LEADS,), -1)])[:LEADS]
    pick = spot[:, None] == jnp.arange(rows * BLOCK)[None, :]
    return roll, allowed, pick.astype(bf16)


def per_device(section_rows, span_lengths, first_weights, second_weights, norm_gain, norm_shift):
    sec = lax.axis_index("section")
    core = sec % 2
    at_head = sec // 2 == 1
    own_rows = section_rows[0]
    tokens, features = own_rows.shape
    rows = tokens // SEQ
    half_tokens = rows * BLOCK
    pairs = [[0, 1], [2, 3]]
    swap = [(0, 1), (1, 0), (2, 3), (3, 2)]
    roll, allowed, pick = row_tables(span_lengths, core)

    rolled = jnp.einsum(
        "rij,rjd->rid", roll, own_rows.reshape(rows, SEQ, features), preferred_element_type=f32
    ).astype(bf16)
    rolled = rolled.reshape(rows, 2, BLOCK, features)
    half0 = rolled[:, 0].reshape(half_tokens, features)
    half1 = rolled[:, 1].reshape(half_tokens, features)
    inner = lax.ppermute(jnp.where(at_head, half0, half1), "section", [(0, 1), (3, 2)])
    aux0 = lax.ppermute(half0, "section", [(1, 2), (2, 0)])
    aux1 = lax.ppermute(half1, "section", [(1, 3), (2, 1)])
    main = jnp.where(sec == 0, half0, jnp.where(sec == 3, half1, inner))
    aux = jnp.where(core == 0, aux0, aux1)

    def both(block):
        return lax.all_gather(block, "section", axis_index_groups=pairs)

    first2 = both(first_weights[0])
    second2 = both(second_weights[0])
    norm2 = both(jnp.concatenate([norm_gain, norm_shift], axis=0))
    w_att, w_up = first2[0], first2[1]
    w_down = jnp.concatenate([second2[0], second2[1]], axis=1)

    def forward(inputs):
        y_att, saved_att = attend(inputs, w_att, norm2[0, 0], norm2[0, 1], allowed)
        middle = y_att.astype(bf16)
        y_ffn, saved_ffn = expand(middle, w_up, w_down, norm2[1, 0], norm2[1, 1])
        return y_ffn, middle, saved_att, saved_ffn

    def backward(upstream, saved_att, saved_ffn):
        d_mid, df, du, dg1, ds1 = expand_back(saved_ffn, w_up, w_down, norm2[1, 0], upstream)
        d_mid = d_mid.astype(bf16).astype(f32)
        dx, d_out, dqkv, dg0, ds0 = attend_back(saved_att, w_att, norm2[0, 0], d_mid)
        return dx, df, du, d_out, dqkv, jnp.stack([jnp.stack([dg0, ds0]), jnp.stack([dg1, ds1])])

    def at_leads(values):
        return jnp.dot(pick, values, precision=lax.Precision.HIGHEST, preferred_element_type=f32)

    def from_leads(values):
        return lax.dot_general(
            pick.astype(values.dtype), values, rows_rows, precision=lax.Precision.HIGHEST,
            preferred_element_type=f32,
        )

    leading = jnp.sum(pick.astype(f32), axis=0)[:, None] > 0
    y_first = forward(main)[0]
    lead_rows = lax.ppermute(at_leads(y_first.astype(bf16)).astype(bf16), "section", [(0, 2), (1, 3)])
    head_in = jnp.where(leading, from_leads(lead_rows).astype(bf16), aux)
    inputs = jnp.where(at_head, head_in, main)
    y_ffn, middle, saved_att, saved_ffn = forward(inputs)
    dx_first = backward(main.astype(f32), saved_att, saved_ffn)[0]
    lead_grads = lax.ppermute(at_leads(dx_first), "section", [(2, 0), (3, 1)])
    d_twelve = (from_leads(lead_grads) + aux.astype(f32)).astype(bf16)
    upstream = jnp.where(at_head, main, d_twelve).astype(f32)
    dx, df, du, d_out, dqkv, d_norm = backward(upstream, saved_att, saved_ffn)

    a, ctx = saved_ffn[0], saved_att[4]

    def outer(left, right):
        return lax.dot_general(left, right, rows_rows, preferred_element_type=f32).astype(bf16)

    d_down = outer(df, a)
    half_ff = d_down.shape[1] // 2
    for_even = jnp.concatenate([outer(inputs, dqkv), outer(ctx, d_out), d_down[:, :half_ff]], axis=1)
    for_odd = jnp.concatenate([outer(middle, du), d_down[:, half_ff:]], axis=1)
    kept = jnp.where(core == 0, for_even, for_odd)
    given = lax.ppermute(jnp.where(core == 0, for_odd, for_even), "section", swap)
    total = (kept.astype(f32) + given.astype(f32)).astype(bf16)
    total = lax.psum(total, "dp").astype(f32)
    ff = first_weights.shape[2]
    d_norm_kept = jnp.where(core == 0, d_norm[0], d_norm[1])
    d_norm_given = lax.ppermute(jnp.where(core == 0, d_norm[1], d_norm[0]), "section", swap)
    norm_total = lax.psum(d_norm_kept + d_norm_given, "dp")

    dskip = jnp.where(leading, 0.0, dx).astype(bf16)
    across = jnp.where(at_head, dskip, y_ffn.astype(bf16))
    out0 = lax.ppermute(across, "section", [(0, 2), (2, 1)])
    out1 = lax.ppermute(across, "section", [(1, 2), (3, 1)])
    own_out = jnp.where(at_head, y_ffn, dx).astype(bf16)
    inner_out = lax.ppermute(own_out, "section", [(1, 0), (2, 3)])
    out0 = jnp.where(sec == 0, own_out, jnp.where(sec == 3, inner_out, out0))
    out1 = jnp.where(sec == 0, inner_out, jnp.where(sec == 3, own_out, out1))
    out = jnp.stack([t.reshape(rows, BLOCK, features) for t in (out0, out1)], axis=1)
    out = jnp.einsum(
        "rij,rid->rjd", roll, out.reshape(rows, SEQ, features), preferred_element_type=f32
    ).reshape(tokens, features)
    return (
        out[None], total[None, :, :ff], total[None, :, ff:], norm_total[None, 0], norm_total[None, 1]
    )


def solution(mesh):
    in_specs = (
        P("section", "dp", None),
        P("dp", None),
        P("section", None, None),
        P("section", None, None),
        P("section", None),
        P("section", None),
    )
    out_specs = (
        P("section", "dp", None),
        P("section", None, None),
        P("section", None, None),
        P("section", None),
        P("section", None),
    )
    return jax.shard_map(
        per_device, mesh=mesh, in_specs=in_specs, out_specs=out_specs, check_vma=False
    )
```

time: 1510 us -> 681 us (0.45); the launches traced: 1490 us -> 676 us
  waiting for transfers between devices: 575 us -> 219 us
  other arithmetic: 316 us -> 81.2 us
  starting transfers between devices: 170 us -> 23.1 us
  loops' own time: 40.7 us -> 0 us
  matrix products: 217 us -> 180 us
    psum x1, waiting for transfers between devices: 431 us -> 184 us  [per_device(): total = lax.psum(total, 'dp').astype(f32)]
    ppermute x26 -> x10, starting transfers between devices: 170 us -> 23 us  [the longest x1 7.93 us: per_device(): lax.ppermute(jnp.where(at_head, half0, half1), 'section', [(0, 1), (3, 2)])]
    add x21 -> x1, other arithmetic: 142 us -> 0.02 us  [per_device(): norm_total = lax.psum(d_norm_kept + d_norm_given, 'dp')]
    ppermute x26 -> x10, waiting for transfers between devices: 144 us -> 18.3 us  [the longest x1 11.3 us: per_device(): lax.ppermute(jnp.where(core == 0, for_odd, for_even), 'section', swap)]
    dynamic_update_slice x24 -> x0, other arithmetic: 75.9 us -> none  [the longest x6 23 us: backward_step(): lax.dynamic_update_slice_in_dim(results, jnp.where(active & (section_id =...]
    sub x6 -> x0, matrix products: 53.7 us -> none  [attend(): exponent = jnp.exp(scores - row_max)]
    another operation x33 -> x7, local copies, waits for them, and re-layouts: 54.1 us -> 1.46 us  [the longest x1 0.64 us: per_device(): half0 = rolled[:, 0].reshape(half_tokens, features)]
    another operation x14 -> x0, loops' own time: 40.7 us -> none  [the longest x6 26.3 us: backward_step(): lax.switch(choose, [empty_backward, attend_backward, expand_backward], in...]
  transfers between devices with their start and end apart: 27 -> 13, of which waited for: 12 -> 6; matrix products, arithmetic and copies ran while one was open for 12% -> 18% of each run, Pallas kernels for 0% -> 0%
where the time goes in v1:
time: 681 us; the launch traced here: 676 us
  waiting for transfers between devices  219 us (32%)
  matrix products  180 us (26%)
  local copies, waits for them, and re-layouts  133 us (20%)
  other arithmetic  81.2 us (12%)
  blocking collectives  25.2 us (4%)
  starting transfers between devices  23.1 us (3%)
  between operations  15.3 us (2%)
    psum x1, waiting for transfers between devices, per_device(): total = lax.psum(total, 'dp').astype(f32)  184 us
    unnamed x182, local copies, waits for them, and re-layouts  41.8 us
    sub x2, other arithmetic, attend(): exponent = jnp.exp(scores - jnp.max(scores, axis=-1, keepdims=True))  26.7 us
    dot_general x2, matrix products, expand_back(): dx = dz + lax.dot_general(du, w_up, cols_cols, preferred_element_type=f32)  26.1 us
    psum x1, blocking collectives, per_device(): norm_total = lax.psum(d_norm_kept + d_norm_given, 'dp')  23.4 us
    reshape x2, local copies, waits for them, and re-layouts, attend(): split = qkv.reshape(blocks, BLOCK, 3, heads, HEAD_DIM)  23 us
    convert_element_type x2, other arithmetic, attend_back(): ds = ds.astype(bf16)  22.1 us
    dot_general x4, matrix products, outer(): lax.dot_general(left, right, rows_rows, preferred_element_type=f32)  20.2 us
  transfers between devices with their start and end apart: 13, of which 6 were waited for; matrix products, arithmetic and copies ran while one was open for 18% of the time, Pallas kernels for 0%

profile of v1, /device:TPU:0, one launch (start us, length us, event | category | flops | bytes accessed | tf_op | source)
XLA Modules:
  0.0 676.3 jit_solution(15212010775617956775)
XLA Ops:
  15.7 7.9 %collective-permute-start = (bf16[768,768]{0,1:T(8,128)(2,1)S(1)}, bf16[768,768]{0,1:T(8,128)(2,1)}, u32[]{:S(2)}, u32[]{:S(2)}) collective-permute-start(bf16[768,768]{0,1:T(8,128)(2,1)S(1)} %broadcast_select_fusion.2), channel_id=1, source_target_pairs={{0,8},{24,16},{1,9},{25,17},{2,10},{26,18},{3,11},{27,19},{4,12},{... | collective-permute-start | bytes 3538952 | tf_op jit(solution)/shard_map/ppermute | solution.py:137
  37.1 15.9 %all-gather.5.cloned.1.call-done = bf16[2,768,3072]{2,1,0:T(8,128)(2,1)} async-done(((bf16[1,768,3072]{2,1,0:T(8,128)(2,1)}), bf16[2,768,3072]{2,1,0:T(8,128)(2,1)}) %all-gather.5.cloned.1.call-update) | async-done | bytes 9437200 | tf_op jit(solution)/shard_map/all_gather | solution.py:144
  62.3 11.5 %reshape.196 = bf16[3,256,3,12,64]{4,3,2,1,0:T(8,128)(2,1)} reshape(bf16[768,2304]{1,0:T(8,128)(2,1)} %convolution_convert_fusion.2) | data formatting | bytes 7077888 | tf_op jit(solution)/shard_map/reshape | solution.py:38
  73.8 6.9 %fusion.142 = (bf16[3,256,1,12,64]{4,3,2,1,0:T(8,128)(2,1)}, bf16[3,256,1,12,64]{4,3,2,1,0:T(8,128)(2,1)}, bf16[3,256,1,12,64]{4,3,2,1,0:T(8,128)(2,1)}) fusion(bf16[3,256,3,12,64]{4,3,2,1,0:T(8,128)(2,1)} %reshape.196), kind=kLoop, calls=%fused_computation.261 | loop fusion | bytes 7077888 | tf_op jit(solution)/shard_map/slice | solution.py:39
  96.3 16.9 %fusion.146 = (f32[3,12,256]{2,1,0:T(8,128)S(1)}, f32[3,12,256,256]{2,3,1,0:T(8,128)}) fusion(f32[3,12,256,256]{2,3,1,0:T(8,128)S(1)} %fusion.95, pred[3,256,256]{1,2,0:T(8,128)(4,1)S(1)} %copy-done.42), kind=kOutput, calls=%fused_computation.265 | output fusion | flops 14156031 | bytes 19107840 | tf_op jit(solution)/shard_map/sub | solution.py:42
  124.0 16.1 %fusion.148 = (f32[768]{0:T(1024)}, f32[768,768]{0,1:T(8,128)}) fusion(bf16[768,1536]{1,0:T(8,128)(2,1)} %get-tuple-element.34, bf16[768,1536]{1,0:T(8,128)(2,1)} %get-tuple-element.33, bf16[2,768,3072]{2,1,0:T(8,128)(2,1)} %all-gather.5.cloned.1.call-done, f32[768,768]{0,1:T(8,128)} %copy-done.25, f32[768]{0:T(1024)} %get-tuple-element.18, ...), kind=kOutput, calls=%fused_computation.267 | convolution fusion | flops 7276657664 | bytes 16550912 | tf_op jit(solution)/shard_map/dot_general | solution.py:85
  151.2 6.8 %convolution_convert_fusion.1 = bf16[768,2304]{1,0:T(8,128)(2,1)} fusion(bf16[768,768]{0,1:T(8,128)(2,1)S(1)} %fusion.81, bf16[768,3072]{1,0:T(8,128)(2,1)} %copy-done.19), kind=kOutput, calls=%fused_computation.37 | convolution fusion | flops 2719678464 | bytes 8257536 | tf_op jit(solution)/shard_map/dot_general | solution.py:37
  158.1 11.5 %reshape.197 = bf16[3,256,3,12,64]{4,3,2,1,0:T(8,128)(2,1)} reshape(bf16[768,2304]{1,0:T(8,128)(2,1)} %convolution_convert_fusion.1) | data formatting | bytes 7077888 | tf_op jit(solution)/shard_map/reshape | solution.py:38
  169.6 6.9 %fusion.141 = (bf16[3,256,1,12,64]{4,3,2,1,0:T(8,128)(2,1)}, bf16[3,256,1,12,64]{4,3,2,1,0:T(8,128)(2,1)}, bf16[3,256,1,12,64]{4,3,2,1,0:T(8,128)(2,1)}) fusion(bf16[3,256,3,12,64]{4,3,2,1,0:T(8,128)(2,1)} %reshape.197), kind=kLoop, calls=%fused_computation.260 | loop fusion | bytes 7077888 | tf_op jit(solution)/shard_map/slice | solution.py:39
  193.6 9.8 %fusion.149 = (f32[3,12,256]{2,1,0:T(8,128)S(1)}, f32[3,12,256,256]{2,3,1,0:T(8,128)S(1)}) fusion(f32[3,12,256,256]{2,3,1,0:T(8,128)} %fusion.85, pred[3,256,256]{1,2,0:T(8,128)(4,1)S(1)} %copy-done.43), kind=kOutput, calls=%fused_computation.268 | output fusion | flops 14156031 | bytes 19107840 | tf_op jit(solution)/shard_map/sub | solution.py:42
  214.2 11.1 %multiply_convert_fusion = (bf16[768,3072]{1,0:T(8,128)(2,1)S(1)}, bf16[768,3072]{1,0:T(8,128)(2,1)}) fusion(bf16[2,768,3072]{2,1,0:T(8,128)(2,1)} %all-gather.5.cloned.1.call-done, f32[768]{0:T(1024)S(1)} %copy-done.60, f32[768]{0:T(1024)S(1)} %copy-done.46, f32[768]{0:T(1024)S(1)} %add_rsqrt_fusion.1, f32[768,768]{0,1:T(8,128)S(1)} %get-tuple-element.52, ...), kind=kOutput, calls=%fused_computation.22 | convolution fusion | flops 3652780032 | bytes 16527360 | tf_op jit(solution)/shard_map/dot_general | solution.py:80
  232.7 18.0 %fusion.57 = (f32[768]{0:T(1024)}, f32[768]{0:T(1024)}, bf16[768,768]{0,1:T(8,128)(2,1)}) fusion(f32[768]{0:T(1024)S(1)} %copy-done.46, f32[768]{0:T(1024)} %copy-done.47, f32[768,768]{0,1:T(8,128)} %copy-done.15, f32[768]{0:T(1024)S(1)} %broadcast_multiply_fusion.9, bf16[2,768,3072]{2,1,0:T(8,128)(2,1)} %all-gather.5.cloned.1.call-done, ...), kind=kOutput, calls=%fused_computation.110 | convolution fusion | flops 7279605760 | bytes 24832000 | tf_op jit(solution)/shard_map/dot_general | solution.py:96
  275.6 11.0 %fusion.10 = bf16[3,12,256,256]{2,3,1,0:T(8,128)(2,1)} fusion(f32[3,12,256,256]{2,3,1,0:T(8,128)} %get-tuple-element.57, f32[3,12,256]{2,1,0:T(8,128)S(1)} %get-tuple-element.56, f32[3,12,256,256]{2,3,1,0:T(8,128)} %copy-done.3, f32[3,12,256]{2,1,0:T(8,128)S(1)} %copy-done.37), kind=kLoop, calls=%fused_computation.18 | loop fusion | flops 14155776 | bytes 23666688 | tf_op jit(solution)/shard_map/convert_element_type | solution.py:66
  311.8 8.5 %fusion.3 = bf16[768,3072]{1,0:T(8,128)(2,1)} fusion(bf16[768,3072]{1,0:T(8,128)(2,1)} %get-tuple-element.24, bf16[768,1536]{1,0:T(8,128)(2,1)S(1)} %copy-done.29, bf16[768,1536]{1,0:T(8,128)(2,1)S(1)} %copy-done.27, bf16[768,768]{0,1:T(8,128)(2,1)S(1)} %get-tuple-element.58, f32[768]{0:T(1024)S(1)} %broadcast_multiply_fusion.2, ...), kind=kOutput, calls=%fused_computation.11 | convolution fusion | flops 3645702144 | bytes 17710080 | tf_op jit(solution)/shard_map/dot_general | solution.py:94
  320.3 8.4 %convolution_convert_fusion.4 = bf16[768,3072]{1,0:T(8,128)(2,1)} fusion(bf16[768,3072]{1,0:T(8,128)(2,1)} %copy-done.74, bf16[768,768]{0,1:T(8,128)(2,1)S(1)} %get-tuple-element.58, f32[768]{0:T(1024)S(1)} %broadcast_multiply_fusion.2, f32[768]{0:T(1024)S(1)} %broadcast_multiply_fusion.3, f32[768]{0:T(1024)S(1)} %copy-done.50, ...), kind=kOutput, calls=%fused_computation.40 | convolution fusion | flops 3631546368 | bytes 12991488 | tf_op jit(solution)/shard_map/dot_general | solution.py:188
  328.7 6.0 convolution_convert_fusion.3
  334.7 8.2 %fusion.54 = (f32[768]{0:T(1024)}, f32[768]{0:T(1024)S(1)}, f32[768]{0:T(1024)S(1)}, f32[768]{0:T(1024)}, bf16[768,768]{0,1:T(8,128)(2,1)S(1)}) fusion(f32[768]{0:T(1024)S(1)} %copy-done.48, f32[768,768]{0,1:T(8,128)S(1)} %copy-done.16, f32[768]{0:T(1024)S(1)} %broadcast_multiply_fusion.9, f32[768]{0:T(1024)S(1)} %copy-done.46, ...), kind=kOutput, calls=%fused_computation.93 | convolution fusion | flops 3635672064 | bytes 16551936 | tf_op jit(solution)/shard_map/dot_general | solution.py:96
  366.1 11.1 %fusion.12 = bf16[3,12,256,256]{2,3,1,0:T(8,128)(2,1)} fusion(f32[3,12,256,256]{2,3,1,0:T(8,128)} %get-tuple-element.61, f32[3,12,256]{2,1,0:T(8,128)S(1)} %get-tuple-element.60, f32[3,12,256,256]{2,3,1,0:T(8,128)} %copy-done.3, f32[3,12,256]{2,1,0:T(8,128)S(1)} %copy-done.38), kind=kLoop, calls=%fused_computation.20 | loop fusion | flops 14155776 | bytes 23666688 | tf_op jit(solution)/shard_map/convert_element_type | solution.py:66
  395.6 11.3 %collective-permute-done.8 = bf16[768,4608]{1,0:T(8,128)(2,1)S(1)} collective-permute-done((bf16[768,4608]{1,0:T(8,128)(2,1)S(1)}, bf16[768,4608]{1,0:T(8,128)(2,1)S(1)}, u32[]{:S(2)}, u32[]{:S(2)}) %collective-permute-start.8) | collective-permute-done | bytes 7077920 | tf_op jit(solution)/shard_map/ppermute | solution.py:195
  413.0 8.9 %fusion.82 = (bf16[768,768]{0,1:T(8,128)(2,1)}, bf16[768,768]{0,1:T(8,128)(2,1)S(1)}) fusion(f32[768]{0:T(1024)S(1)} %copy-done.45, f32[768]{0:T(1024)S(1)} %get-tuple-element.17, pred[768]{0:T(1024)(128)(4,1)} %copy-done.68, pred[]{:T(512)S(6)} %eq.84, f32[768]{0:T(1024)} %copy-done.49, f32[768,768]{0,1:T(8,128)S(1)} %copy-done.13, ...), kind=kOutput, calls=%fused_computation.154 | convolution fusion | flops 2728525824 | bytes 15369217 | tf_op jit(solution)/shard_map/dot_general | solution.py:73
  429.4 23.4 %psum.15 = f32[2,768]{1,0:T(2,128)S(1)} all-reduce(f32[2,768]{1,0:T(2,128)S(1)} %select_add_fusion), channel_id=1, replica_groups=mesh['section'=4,'dp'=8] {'dp'}, use_global_device_ids=true, to_apply=%region_31.32 | all-reduce | flops 1536 | bytes 12288 | tf_op jit(solution)/shard_map/psum | solution.py:201
  462.5 183.5 %all-reduce.3.cloned.1.call-done = bf16[768,4608]{1,0:T(8,128)(2,1)} async-done(((bf16[768,4608]{1,0:T(8,128)(2,1)}), bf16[768,4608]{1,0:T(8,128)(2,1)}) %all-reduce.3.cloned.1.call-update) | async-done | bytes 7077904 | tf_op jit(solution)/shard_map/psum | solution.py:197
  646.0 10.0 %convert_element_type.300 = f32[768,4608]{1,0:T(8,128)} convert(bf16[768,4608]{1,0:T(8,128)(2,1)} %all-reduce.3.cloned.1.call-done) | non-fusion elementwise | flops 3538944 | bytes 21233664 | tf_op jit(solution)/shard_map/convert_element_type | solution.py:197
  660.8 8.8 %slice_bitcast_fusion = f32[1,768,3072]{2,1,0:T(8,128)} fusion(f32[768,4608]{1,0:T(8,128)} %convert_element_type.300), kind=kLoop, calls=%fused_computation.21 | loop fusion | bytes 18874368 | tf_op jit(solution)/shard_map/broadcast_in_dim | solution.py:216
  (311 shorter events, 222.8 us)
Async XLA Ops:
  7.2 24.6 %all-gather.7.cloned.1.call-start = ((), (), s32[]{:S(2)}) async-start(), calls=%async_computation.1 | async-start | bytes 7077888 | tf_op jit(solution)/shard_map/all_gather | solution.py:144
  7.9 45.0 %all-gather.5.cloned.1.call-start = ((), (), s32[]{:S(2)}) async-start(), calls=%async_computation | async-start | bytes 14155776 | tf_op jit(solution)/shard_map/all_gather | solution.py:144
  8.7 637.3 %all-reduce.3.cloned.1.call-start = ((), (), s32[]{:S(2)}) async-start(), calls=%async_computation.2 | async-start | bytes 14155776 | tf_op jit(solution)/shard_map/psum | solution.py:197
  9.6 19.1 %copy-start.40 = (s32[3,512]{1,0:T(4,128)}, s32[3,512]{1,0:T(4,128)S(1)}, u32[]{:S(2)}) copy-start(s32[3,512]{1,0:T(4,128)S(1)} %add_select_fusion) | copy-start | bytes 18436
  11.9 136.4 %collective-permute-start.2 = (bf16[768,768]{0,1:T(8,128)(2,1)S(1)}, bf16[768,768]{0,1:T(8,128)(2,1)}, u32[]{:S(2)}, u32[]{:S(2)}) collective-permute-start(bf16[768,768]{0,1:T(8,128)(2,1)S(1)} %copy.145), channel_id=1, source_target_pairs={{8,16},{16,0},{9,17},{17,1},{10,18},{18,2},{11,19},{19,3},{12,20},... | collective-permute-start | bytes 3538952 | tf_op jit(solution)/shard_map/ppermute | solution.py:138
  13.8 134.5 %collective-permute-start.3 = (bf16[768,768]{0,1:T(8,128)(2,1)S(1)}, bf16[768,768]{0,1:T(8,128)(2,1)}, u32[]{:S(2)}, u32[]{:S(2)}) collective-permute-start(bf16[768,768]{0,1:T(8,128)(2,1)S(1)} %copy.144), channel_id=1, source_target_pairs={{8,24},{16,8},{9,25},{17,9},{10,26},{18,10},{11,27},{19,11},{12,28... | collective-permute-start | bytes 3538952 | tf_op jit(solution)/shard_map/ppermute | solution.py:139
  15.7 14.7 %collective-permute-start = (bf16[768,768]{0,1:T(8,128)(2,1)S(1)}, bf16[768,768]{0,1:T(8,128)(2,1)}, u32[]{:S(2)}, u32[]{:S(2)}) collective-permute-start(bf16[768,768]{0,1:T(8,128)(2,1)S(1)} %broadcast_select_fusion.2), channel_id=1, source_target_pairs={{0,8},{24,16},{1,9},{25,17},{2,10},{26,18},{3,11},{27,19},{4,12},{... | collective-permute-start | bytes 3538952 | tf_op jit(solution)/shard_map/ppermute | solution.py:137
  29.4 113.5 %copy-start.44 = (f32[768]{0:T(1024)}, f32[768]{0:T(1024)S(1)}, u32[]{:S(2)}) copy-start(f32[768]{0:T(1024)S(1)} %get-tuple-element.20) | copy-start | bytes 9220
  31.8 23.9 %copy-start.20 = (bf16[768,768]{0,1:T(8,128)(2,1)}, bf16[768,768]{0,1:T(8,128)(2,1)S(1)}, u32[]{:S(2)}) copy-start(bf16[768,768]{0,1:T(8,128)(2,1)S(1)} %select_select_fusion.2) | copy-start | bytes 3538948
  96.3 16.9 %copy-start.33 = (bf16[3,256,1,12,64]{1,4,3,0,2:T(8,128)(2,1)S(1)}, bf16[3,256,1,12,64]{1,4,3,0,2:T(8,128)(2,1)}, u32[]{:S(2)}) copy-start(bf16[3,256,1,12,64]{1,4,3,0,2:T(8,128)(2,1)} %copy.216) | copy-start | bytes 3538948
  144.1 5.3 collective-permute-start.1
  180.2 24.6 %copy-start.6 = (bf16[3,256,1,12,64]{1,4,3,0,2:T(8,128)(2,1)}, bf16[3,256,1,12,64]{1,4,3,0,2:T(8,128)(2,1)S(1)}, u32[]{:S(2)}) copy-start(bf16[3,256,1,12,64]{1,4,3,0,2:T(8,128)(2,1)S(1)} %copy.219) | copy-start | bytes 3538948
  213.5 11.8 %copy-start.15 = (f32[768,768]{0,1:T(8,128)}, f32[768,768]{0,1:T(8,128)S(1)}, u32[]{:S(2)}) copy-start(f32[768,768]{0,1:T(8,128)S(1)} %get-tuple-element.52) | copy-start | bytes 7077892
  301.2 6.4 collective-permute-start.4
  395.5 11.3 %collective-permute-start.8 = (bf16[768,4608]{1,0:T(8,128)(2,1)S(1)}, bf16[768,4608]{1,0:T(8,128)(2,1)S(1)}, u32[]{:S(2)}, u32[]{:S(2)}) collective-permute-start(bf16[768,4608]{1,0:T(8,128)(2,1)S(1)} %broadcast_select_fusion), channel_id=1, source_target_pairs={{0,8},{8,0},{16,24},{24,16},{1,9},{9,1},{17,25},{25,17},{2,10},{10... | collective-permute-start | bytes 21233672 | tf_op jit(solution)/shard_map/ppermute | solution.py:195
  413.0 13.0 %copy-start.63 = (f32[768]{0:T(1024)S(1)}, f32[768]{0:T(1024)}, u32[]{:S(2)}) copy-start(f32[768]{0:T(1024)} %get-tuple-element.7) | copy-start | bytes 9220
  413.0 13.0 %copy-start.62 = (f32[768]{0:T(1024)S(1)}, f32[768]{0:T(1024)}, u32[]{:S(2)}) copy-start(f32[768]{0:T(1024)} %get-tuple-element.16) | copy-start | bytes 9220
  413.0 13.0 %copy-start.65 = (f32[768]{0:T(1024)S(1)}, f32[768]{0:T(1024)}, u32[]{:S(2)}) copy-start(f32[768]{0:T(1024)} %get-tuple-element.5) | copy-start | bytes 9220
  413.0 13.0 %copy-start.64 = (f32[768]{0:T(1024)S(1)}, f32[768]{0:T(1024)}, u32[]{:S(2)}) copy-start(f32[768]{0:T(1024)} %get-tuple-element.15) | copy-start | bytes 9220
  421.9 31.5 %copy-start.34 = (bf16[768,768]{0,1:T(8,128)(2,1)}, bf16[768,768]{0,1:T(8,128)(2,1)S(1)}, u32[]{:S(2)}) copy-start(bf16[768,768]{0,1:T(8,128)(2,1)S(1)} %get-tuple-element.36) | copy-start | bytes 3538948
  421.9 31.5 %collective-permute-start.7 = (bf16[768,768]{0,1:T(8,128)(2,1)}, bf16[768,768]{0,1:T(8,128)(2,1)S(1)}, u32[]{:S(2)}, u32[]{:S(2)}) collective-permute-start(bf16[768,768]{0,1:T(8,128)(2,1)} %get-tuple-element.35), channel_id=1, source_target_pairs={{8,16},{24,8},{9,17},{25,9},{10,18},{26,10},{11,19},{27,11},{12,20... | collective-permute-start | bytes 3538952 | tf_op jit(solution)/shard_map/ppermute | solution.py:206
  422.7 30.8 %collective-permute-start.6 = (bf16[768,768]{0,1:T(8,128)(2,1)}, bf16[768,768]{0,1:T(8,128)(2,1)S(1)}, u32[]{:S(2)}, u32[]{:S(2)}) collective-permute-start(bf16[768,768]{0,1:T(8,128)(2,1)} %get-tuple-element.35), channel_id=1, source_target_pairs={{0,16},{16,8},{1,17},{17,9},{2,18},{18,10},{3,19},{19,11},{4,20},{... | collective-permute-start | bytes 3538952 | tf_op jit(solution)/shard_map/ppermute | solution.py:205
  424.7 29.8 %collective-permute-start.5 = (bf16[768,768]{0,1:T(8,128)(2,1)S(1)}, bf16[768,768]{0,1:T(8,128)(2,1)}, u32[]{:S(2)}, u32[]{:S(2)}) collective-permute-start(bf16[768,768]{0,1:T(8,128)(2,1)S(1)} %get-tuple-element.36), channel_id=1, source_target_pairs={{8,0},{16,24},{9,1},{17,25},{10,2},{18,26},{11,3},{19,27},{12,4},{... | collective-permute-start | bytes 3538952 | tf_op jit(solution)/shard_map/ppermute | solution.py:208
  426.1 3.3 collective-permute-start.9
  (72 other events, 301.1 us)
Sparse Core Ops, SparseCore 0:
  9.6 18.6 all-gather.6
  29.8 23.1 all-gather.4
  411.5 234.4 all-reduce.2

commit v2 on v1

v2 whole, which is shorter than its diff:
```python
import jax
import jax.numpy as jnp
from jax import lax
from jax.experimental import pallas as pl
from jax.experimental.pallas import tpu as pltpu
from jax.sharding import PartitionSpec as P

HEAD_DIM = 64
PAIR = 2 * HEAD_DIM
BLOCK = 256
SEQ = 512
LEADS = 16
CHUNK = 512
f32 = jnp.float32
bf16 = jnp.bfloat16
epsilon = 1e-12
NN = (((1,), (0,)), ((), ()))
NT = (((1,), (1,)), ((), ()))
TN = (((0,), (0,)), ((), ()))
LOG2E = 1.4426950408889634


def mm(a, b, dims=NN):
    return lax.dot_general(a, b, dims, preferred_element_type=f32)


def gelu_and_slope(u):
    x = jnp.abs(u)
    bell = jnp.exp2(u * u * (-0.5 * LOG2E))
    t = 1.0 / (1.0 + (0.3275911 * 0.5**0.5) * x)
    poly = t * (0.127414796 + t * (-0.142248368 + t * (0.7107068705 + t * (-0.7265760135 + t * 0.5307027145))))
    tail = poly * bell
    cdf = jnp.where(u < 0, tail, 1.0 - tail)
    return u * cdf, cdf + u * bell * 0.3989422804014327


def normalize(z):
    centered = z - jnp.mean(z, axis=-1, keepdims=True)
    rstd = lax.rsqrt(jnp.mean(centered * centered, axis=-1, keepdims=True) + epsilon)
    return centered * rstd, rstd


def lane_masks(rows):
    lane = lax.broadcasted_iota(jnp.int32, (rows, PAIR), 1)
    return lane < HEAD_DIM


def forward_kernel(
    x, seg_rows, seg_cols, norms, pick, first_h, second_h,
    y_h, lead, qkv_h, p_h, ctx_h, zh0_h, rstd0, mid_h, a_h, slope_h, zh1_h, rstd1,
    wa, wu, wd, qkv, p, ctx, zh0, mid, a, slope, zh1, y, acc, sems, out_sems,
):
    tokens, features = x.shape
    ff = wu.shape[1]
    blocks = tokens // BLOCK
    pairs = features // PAIR
    half = ff // 2
    n3 = 3 * features
    loads = [
        pltpu.make_async_copy(first_h.at[0], wa, sems.at[0]),
        pltpu.make_async_copy(first_h.at[1], wu, sems.at[1]),
        pltpu.make_async_copy(second_h.at[0], wd.at[:, pl.ds(0, half)], sems.at[2]),
        pltpu.make_async_copy(second_h.at[1], wd.at[:, pl.ds(half, half)], sems.at[3]),
    ]
    for c in loads:
        c.start()
    stores = []

    def keep(src, dst):
        c = pltpu.make_async_copy(src, dst, out_sems.at[len(stores)])
        c.start()
        stores.append(c)

    loads[0].wait()
    for c in range(n3 // features):
        cols = pl.ds(c * features, features)
        qkv[:, cols] = mm(x[...], wa[:, cols]).astype(bf16)
    keep(qkv, qkv_h)
    first = lane_masks(BLOCK)
    zero = jnp.zeros((BLOCK, PAIR), bf16)

    def block_step(b, carry):
        rows = pl.ds(pl.multiple_of(b * BLOCK, BLOCK), BLOCK)
        bias = jnp.where(seg_rows[rows, :] == seg_cols[b], 0.0, -1e30)
        for h in range(pairs):
            q = qkv[rows, pl.ds(h * PAIR, PAIR)]
            k = qkv[rows, pl.ds(features + h * PAIR, PAIR)]
            v = qkv[rows, pl.ds(2 * features + h * PAIR, PAIR)]
            total = None
            for side in range(2):
                own = first if side == 0 else ~first
                s = mm(q, jnp.where(own, k, zero), NT) * (HEAD_DIM**-0.5) + bias
                e = jnp.exp(s - jnp.max(s, axis=-1, keepdims=True))
                pr = (e * (1.0 / jnp.sum(e, axis=-1, keepdims=True))).astype(bf16)
                p[b, h, :, pl.ds(side * BLOCK, BLOCK)] = pr
                part = mm(pr, jnp.where(own, v, zero))
                total = part if total is None else total + part
            ctx[rows, pl.ds(h * PAIR, PAIR)] = total.astype(bf16)
        return carry

    lax.fori_loop(0, blocks, block_step, 0)
    keep(p, p_h)
    keep(ctx, ctx_h)
    z = x[...].astype(f32) + mm(ctx[...], wa[:, pl.ds(n3, features)])
    zn, r = normalize(z)
    rstd0[...] = r
    zh0[...] = zn.astype(bf16)
    mid[...] = (zn * norms[0:1, :] + norms[1:2, :]).astype(bf16)
    keep(zh0, zh0_h)
    keep(mid, mid_h)
    for c in loads[1:]:
        c.wait()
    acc[...] = mid[...].astype(f32)

    for c in range(ff // CHUNK):
        cols = pl.ds(c * CHUNK, CHUNK)
        u = mm(mid[...], wu[:, cols])
        act, sl = gelu_and_slope(u)
        act = act.astype(bf16)
        a[:, cols] = act
        slope[:, cols] = sl.astype(bf16)
        acc[...] += mm(act, wd[:, cols], NT)
    keep(a, a_h)
    keep(slope, slope_h)
    zn, r = normalize(acc[...])
    rstd1[...] = r
    zh1[...] = zn.astype(bf16)
    y[...] = (zn * norms[2:3, :] + norms[3:4, :]).astype(bf16)
    keep(zh1, zh1_h)
    keep(y, y_h)
    lead[...] = mm(pick[...], y[...]).astype(bf16)
    for c in stores:
        c.wait()


def forward(x, seg_rows, seg_cols, norms, pick, firsts, seconds):
    tokens, features = x.shape
    ff = firsts.shape[2]
    blocks, pairs = tokens // BLOCK, features // PAIR
    S = jax.ShapeDtypeStruct
    any_ = pl.BlockSpec(memory_space=pl.ANY)
    vm = pl.BlockSpec(memory_space=pltpu.VMEM)
    shapes = dict(
        y=S((tokens, features), bf16), lead=S((pick.shape[0], features), bf16),
        qkv=S((tokens, 3 * features), bf16), p=S((blocks, pairs, BLOCK, 2 * BLOCK), bf16),
        ctx=S((tokens, features), bf16), zh0=S((tokens, features), bf16), rstd0=S((tokens, 1), f32),
        mid=S((tokens, features), bf16), a=S((tokens, ff), bf16), slope=S((tokens, ff), bf16),
        zh1=S((tokens, features), bf16), rstd1=S((tokens, 1), f32),
    )
    V = lambda k: pltpu.VMEM(shapes[k].shape, shapes[k].dtype)
    outs = pl.pallas_call(
        forward_kernel,
        out_shape=list(shapes.values()),
        in_specs=[vm] * 5 + [any_] * 2,
        out_specs=[vm if k in ("lead", "rstd0", "rstd1") else any_ for k in shapes],
        scratch_shapes=[
            pltpu.VMEM(firsts.shape[1:], bf16), pltpu.VMEM(firsts.shape[1:], bf16), pltpu.VMEM((features, ff), bf16),
            V("qkv"), V("p"), V("ctx"), V("zh0"), V("mid"), V("a"), V("slope"), V("zh1"), V("y"),
            pltpu.VMEM((tokens, features), f32),
            pltpu.SemaphoreType.DMA((4,)), pltpu.SemaphoreType.DMA((9,)),
        ],
        compiler_params=pltpu.CompilerParams(vmem_limit_bytes=60 << 20),
        name="layer_forward",
    )(x, seg_rows, seg_cols, norms, pick, firsts, seconds)
    return dict(zip(shapes, outs))


def normalize_back(zh, rstd, gain, dy):
    g = dy * gain
    mean_g = jnp.mean(g, axis=-1, keepdims=True)
    mean_gz = jnp.mean(g * zh, axis=-1, keepdims=True)
    dz = rstd * (g - mean_g - zh * mean_gz)
    return dz, jnp.sum(dy * zh, axis=0, keepdims=True), jnp.sum(dy, axis=0, keepdims=True)


def backward_kernel(
    dy, norms, pick, rstd0, rstd1, first_h, second_h,
    qkv_h, p_h, zh0_h, slope_h, zh1_h,
    dx_h, lead, df_h, du_h, do_h, dqkv_h, dnorm,
    wa, wu, wd, qkv, p, zh0, slope, zh1, dx, df, du, do, dqkv, dctx, acc, sems, out_sems,
):
    tokens, features = dy.shape
    ff = wu.shape[1]
    blocks = tokens // BLOCK
    pairs = features // PAIR
    half = ff // 2
    n3 = 3 * features
    C = pltpu.make_async_copy
    ld = [
        C(zh1_h, zh1, sems.at[0]),
        C(second_h.at[0], wd.at[:, pl.ds(0, half)], sems.at[1]),
        C(first_h.at[1], wu, sems.at[2]),
        C(slope_h, slope, sems.at[3]),
        C(second_h.at[1], wd.at[:, pl.ds(half, half)], sems.at[4]),
        C(zh0_h, zh0, sems.at[5]),
        C(first_h.at[0], wa, sems.at[6]),
        C(qkv_h, qkv, sems.at[7]),
        C(p_h, p, sems.at[8]),
    ]
    for c in ld:
        c.start()
    stores = []

    def keep(src, dst):
        c = C(src, dst, out_sems.at[len(stores)])
        c.start()
        stores.append(c)

    ld[0].wait()
    dz, dg, ds_ = normalize_back(zh1[...].astype(f32), rstd1[...], norms[2:3, :], dy[...].astype(f32))
    dnorm[2:3, :] = dg
    dnorm[3:4, :] = ds_
    df[...] = dz.astype(bf16)
    acc[...] = dz
    keep(df, df_h)
    for i in (1, 2, 3):
        ld[i].wait()
    for c in range(ff // CHUNK):
        if c == ff // CHUNK // 2:
            ld[4].wait()
        cols = pl.ds(c * CHUNK, CHUNK)
        da = mm(df[...], wd[:, cols])
        g = (da * slope[:, cols].astype(f32)).astype(bf16)
        du[:, cols] = g
        acc[...] += mm(g, wu[:, cols], NT)
    keep(du, du_h)
    ld[5].wait()
    d_mid = acc[...].astype(bf16).astype(f32)
    dz, dg, ds_ = normalize_back(zh0[...].astype(f32), rstd0[...], norms[0:1, :], d_mid)
    dnorm[0:1, :] = dg
    dnorm[1:2, :] = ds_
    do[...] = dz.astype(bf16)
    acc[...] = dz
    keep(do, do_h)
    ld[6].wait()
    dctx[...] = mm(do[...], wa[:, pl.ds(n3, features)], NT).astype(bf16)
    ld[7].wait()
    ld[8].wait()
    first = lane_masks(BLOCK)
    zero = jnp.zeros((BLOCK, PAIR), bf16)
    scale = HEAD_DIM**-0.5

    def block_step(b, carry):
        rows = pl.ds(pl.multiple_of(b * BLOCK, BLOCK), BLOCK)
        for h in range(pairs):
            q = qkv[rows, pl.ds(h * PAIR, PAIR)]
            k = qkv[rows, pl.ds(features + h * PAIR, PAIR)]
            v = qkv[rows, pl.ds(2 * features + h * PAIR, PAIR)]
            dc = dctx[rows, pl.ds(h * PAIR, PAIR)]
            dq = dk = dv = None
            for side in range(2):
                own = first if side == 0 else ~first
                pr = p[b, h, :, pl.ds(side * BLOCK, BLOCK)]
                prf = pr.astype(f32)
                dp = mm(dc, jnp.where(own, v, zero), NT)
                r = jnp.sum(dp * prf, axis=-1, keepdims=True)
                ds = (prf * (dp - r)).astype(bf16)
                parts = (
                    mm(ds, jnp.where(own, k, zero)),
                    mm(ds, jnp.where(own, q, zero), TN),
                    mm(pr, jnp.where(own, dc, zero), TN),
                )
                if dq is None:
                    dq, dk, dv = parts
                else:
                    dq, dk, dv = dq + parts[0], dk + parts[1], dv + parts[2]
            dqkv[rows, pl.ds(h * PAIR, PAIR)] = (dq * scale).astype(bf16)
            dqkv[rows, pl.ds(features + h * PAIR, PAIR)] = (dk * scale).astype(bf16)
            dqkv[rows, pl.ds(2 * features + h * PAIR, PAIR)] = dv.astype(bf16)
        return carry

    lax.fori_loop(0, blocks, block_step, 0)
    keep(dqkv, dqkv_h)
    for c in range(3):
        cols = pl.ds(c * features, features)
        acc[...] += mm(dqkv[:, cols], wa[:, cols], NT)
    dx[...] = acc[...].astype(bf16)
    keep(dx, dx_h)
    hi = acc[...].astype(bf16)
    lo = (acc[...] - hi.astype(f32)).astype(bf16)
    lead[...] = mm(pick[...], hi) + mm(pick[...], lo)
    for c in stores:
        c.wait()


def backward(dy, norms, pick, sv, firsts, seconds):
    tokens, features = dy.shape
    ff = firsts.shape[2]
    blocks, pairs = tokens // BLOCK, features // PAIR
    S = jax.ShapeDtypeStruct
    any_ = pl.BlockSpec(memory_space=pl.ANY)
    vm = pl.BlockSpec(memory_space=pltpu.VMEM)
    shapes = dict(
        dx=S((tokens, features), bf16), lead=S((pick.shape[0], features), f32),
        df=S((tokens, features), bf16), du=S((tokens, ff), bf16), do=S((tokens, features), bf16),
        dqkv=S((tokens, 3 * features), bf16), dnorm=S((4, features), f32),
    )
    V = lambda k: pltpu.VMEM(shapes[k].shape, shapes[k].dtype)
    L = lambda k: pltpu.VMEM(sv[k].shape, sv[k].dtype)
    outs = pl.pallas_call(
        backward_kernel,
        out_shape=list(shapes.values()),
        in_specs=[vm] * 5 + [any_] * 7,
        out_specs=[vm if k in ("lead", "dnorm") else any_ for k in shapes],
        scratch_shapes=[
            pltpu.VMEM(firsts.shape[1:], bf16), pltpu.VMEM(firsts.shape[1:], bf16), pltpu.VMEM((features, ff), bf16),
            L("qkv"), L("p"), L("zh0"), L("slope"), L("zh1"),
            V("dx"), V("df"), V("du"), V("do"), V("dqkv"), pltpu.VMEM((tokens, features), bf16),
            pltpu.VMEM((tokens, features), f32),
            pltpu.SemaphoreType.DMA((9,)), pltpu.SemaphoreType.DMA((5,)),
        ],
        compiler_params=pltpu.CompilerParams(vmem_limit_bytes=60 << 20),
        name="layer_backward",
    )(dy, norms, pick, sv["rstd0"], sv["rstd1"], firsts, seconds, sv["qkv"], sv["p"], sv["zh0"], sv["slope"], sv["zh1"])
    return dict(zip(shapes, outs))


def row_tables(lengths, core):
    rows, spans = lengths.shape
    order = jnp.arange(spans)
    ends = jnp.sum(jnp.where(order[:, None] <= order[None, :], lengths[:, :, None], 0), axis=1)
    starts = ends - lengths
    first = jnp.sum(jnp.where(lengths == BLOCK, starts, 0), axis=1)
    place = jnp.arange(SEQ)
    origin = (place[None, :] + first[:, None]) % SEQ
    roll = (origin[:, :, None] == place[None, None, :]).astype(bf16)
    mine = lax.dynamic_slice_in_dim(origin, core * BLOCK, BLOCK, 1)
    segment = jnp.sum((mine[:, :, None] >= ends[:, None, :]).astype(jnp.int32), axis=2)
    lead = (starts[:, : spans - 1] - first[:, None]) % SEQ
    spot = jnp.where(lead // BLOCK == core, jnp.arange(rows)[:, None] * BLOCK + lead % BLOCK, -1)
    spot = jnp.concatenate([spot.reshape(-1), jnp.full((LEADS,), -1)])[:LEADS]
    pick = spot[:, None] == jnp.arange(rows * BLOCK)[None, :]
    return roll, segment, pick.astype(bf16)


def per_device(section_rows, span_lengths, first_weights, second_weights, norm_gain, norm_shift):
    sec = lax.axis_index("section")
    core = sec % 2
    at_head = sec // 2 == 1
    own_rows = section_rows[0]
    tokens, features = own_rows.shape
    rows = tokens // SEQ
    half_tokens = rows * BLOCK
    pairs = [[0, 1], [2, 3]]
    swap = [(0, 1), (1, 0), (2, 3), (3, 2)]
    roll, segment, pick = row_tables(span_lengths, core)

    rolled = jnp.einsum(
        "rij,rjd->rid", roll, own_rows.reshape(rows, SEQ, features), preferred_element_type=f32
    ).astype(bf16)
    rolled = rolled.reshape(rows, 2, BLOCK, features)
    half0 = rolled[:, 0].reshape(half_tokens, features)
    half1 = rolled[:, 1].reshape(half_tokens, features)
    inner = lax.ppermute(jnp.where(at_head, half0, half1), "section", [(0, 1), (3, 2)])
    aux0 = lax.ppermute(half0, "section", [(1, 2), (2, 0)])
    aux1 = lax.ppermute(half1, "section", [(1, 3), (2, 1)])
    main = jnp.where(sec == 0, half0, jnp.where(sec == 3, half1, inner))
    aux = jnp.where(core == 0, aux0, aux1)

    def both(block):
        return lax.all_gather(block, "section", axis_index_groups=pairs)

    first2 = both(first_weights[0])
    second2 = both(second_weights[0])
    norm2 = both(jnp.concatenate([norm_gain, norm_shift], axis=0))
    norms = norm2.reshape(4, features)
    seg_rows = segment.reshape(half_tokens, 1)
    seg_cols = segment.reshape(rows, 1, BLOCK)

    def from_leads(values):
        return lax.dot_general(
            pick.astype(values.dtype), values, TN, precision=lax.Precision.HIGHEST,
            preferred_element_type=f32,
        )

    leading = jnp.sum(pick.astype(f32), axis=0)[:, None] > 0
    lead_rows = forward(main, seg_rows, seg_cols, norms, pick, first2, second2)["lead"]
    lead_rows = lax.ppermute(lead_rows, "section", [(0, 2), (1, 3)])
    head_in = jnp.where(leading, from_leads(lead_rows).astype(bf16), aux)
    inputs = jnp.where(at_head, head_in, main)
    saved = forward(inputs, seg_rows, seg_cols, norms, pick, first2, second2)
    lead_grads = backward(main, norms, pick, saved, first2, second2)["lead"]
    lead_grads = lax.ppermute(lead_grads, "section", [(2, 0), (3, 1)])
    d_twelve = (from_leads(lead_grads) + aux.astype(f32)).astype(bf16)
    upstream = jnp.where(at_head, main, d_twelve)
    grads = backward(upstream, norms, pick, saved, first2, second2)
    dx, df, du, d_out, dqkv = (grads[k] for k in ("dx", "df", "du", "do", "dqkv"))
    d_norm = grads["dnorm"].reshape(2, 2, features)
    y_ffn, middle, a, ctx = (saved[k] for k in ("y", "mid", "a", "ctx"))

    def outer(left, right):
        return lax.dot_general(left, right, TN, preferred_element_type=f32).astype(bf16)

    d_down = outer(df, a)
    half_ff = d_down.shape[1] // 2
    for_even = jnp.concatenate([outer(inputs, dqkv), outer(ctx, d_out), d_down[:, :half_ff]], axis=1)
    for_odd = jnp.concatenate([outer(middle, du), d_down[:, half_ff:]], axis=1)
    kept = jnp.where(core == 0, for_even, for_odd)
    given = lax.ppermute(jnp.where(core == 0, for_odd, for_even), "section", swap)
    total = (kept.astype(f32) + given.astype(f32)).astype(bf16)
    total = lax.psum(total, "dp").astype(f32)
    ff = first_weights.shape[2]
    d_norm_kept = jnp.where(core == 0, d_norm[0], d_norm[1])
    d_norm_given = lax.ppermute(jnp.where(core == 0, d_norm[1], d_norm[0]), "section", swap)
    norm_total = lax.psum(d_norm_kept + d_norm_given, "dp")

    dskip = jnp.where(leading, jnp.zeros_like(dx), dx)
    across = jnp.where(at_head, dskip, y_ffn)
    out0 = lax.ppermute(across, "section", [(0, 2), (2, 1)])
    out1 = lax.ppermute(across, "section", [(1, 2), (3, 1)])
    own_out = jnp.where(at_head, y_ffn, dx)
    inner_out = lax.ppermute(own_out, "section", [(1, 0), (2, 3)])
    out0 = jnp.where(sec == 0, own_out, jnp.where(sec == 3, inner_out, out0))
    out1 = jnp.where(sec == 0, inner_out, jnp.where(sec == 3, own_out, out1))
    out = jnp.stack([t.reshape(rows, BLOCK, features) for t in (out0, out1)], axis=1)
    out = jnp.einsum(
        "rij,rid->rjd", roll, out.reshape(rows, SEQ, features), preferred_element_type=f32
    ).reshape(tokens, features)
    return (
        out[None], total[None, :, :ff], total[None, :, ff:], norm_total[None, 0], norm_total[None, 1]
    )


def solution(mesh):
    in_specs = (
        P("section", "dp", None),
        P("dp", None),
        P("section", None, None),
        P("section", None, None),
        P("section", None),
        P("section", None),
    )
    out_specs = (
        P("section", "dp", None),
        P("section", None, None),
        P("section", None, None),
        P("section", None),
        P("section", None),
    )
    return jax.shard_map(
        per_device, mesh=mesh, in_specs=in_specs, out_specs=out_specs, check_vma=False
    )
```

time: 681 us -> 514 us (0.75)
  matrix products: 180 us -> 27.3 us
  Pallas kernels: 0 us -> 136 us
  local copies, waits for them, and re-layouts: 133 us -> 24.8 us
  other arithmetic: 81.2 us -> 27.2 us
  waiting for transfers between devices: 219 us -> 230 us
    dot_general x34 -> x6, matrix products: 175 us -> 22.2 us  [the longest x4 15.4 us: outer(): lax.dot_general(left, right, TN, preferred_element_type=f32).astype(bf16)]
    pallas_call x0 -> x4, Pallas kernels: none -> 136 us  [the longest x2 70 us: forward(): pl.pallas_call(forward_kernel, out_shape=list(shapes.values()), in_specs=...]
    reshape x6 -> x1, local copies, waits for them, and re-layouts: 39.1 us -> 0.58 us  [per_device(): seg_cols = segment.reshape(rows, 1, BLOCK)]
    unnamed x182 -> x41, local copies, waits for them, and re-layouts: 41.8 us -> 6.86 us
    sub x2 -> x0, other arithmetic: 26.7 us -> none  [attend(): exponent = jnp.exp(scores - jnp.max(scores, axis=-1, keepdims=True))]
    convert_element_type x3 -> x1, other arithmetic: 23.4 us -> 0.67 us  [row_tables(): return (roll, segment, pick.astype(bf16))]
    slice x4 -> x1, local copies, waits for them, and re-layouts: 14.6 us -> 0.15 us  [per_device(): half0 = rolled[:, 0].reshape(half_tokens, features)]
    psum x1, waiting for transfers between devices: 184 us -> 194 us  [per_device(): total = lax.psum(total, 'dp').astype(f32)]
  transfers between devices with their start and end apart: 13 -> 13, of which waited for: 6 -> 6; matrix products, arithmetic and copies ran while one was open for 18% -> 4% of each run, Pallas kernels for 0% -> 7%
where the time goes in v2:
time: 514 us; the launch traced here: 507 us
  waiting for transfers between devices  230 us (45%)
  Pallas kernels  136 us (26%)
  blocking collectives  29 us (6%)
  matrix products  27.3 us (5%)
  other arithmetic  27.2 us (5%)
  local copies, waits for them, and re-layouts  24.8 us (5%)
  starting transfers between devices  17.8 us (3%)
  between operations  14.6 us (3%)
    psum x1, waiting for transfers between devices, per_device(): total = lax.psum(total, 'dp').astype(f32)  194 us
    pallas_call x2, Pallas kernels, forward(): pl.pallas_call(forward_kernel, out_shape=list(shapes.values()), in_specs=...  70 us
    pallas_call x2, Pallas kernels, backward(): pl.pallas_call(backward_kernel, out_shape=list(shapes.values()), in_specs...  66.4 us
    psum x1, blocking collectives, per_device(): norm_total = lax.psum(d_norm_kept + d_norm_given, 'dp')  23.2 us
    all_gather x2, waiting for transfers between devices, both(): return lax.all_gather(block, 'section', axis_index_groups=pairs)  16.4 us
    dot_general x4, matrix products, outer(): lax.dot_general(left, right, TN, preferred_element_type=f32).astype(bf16)  15.4 us
    ppermute x1, waiting for transfers between devices, per_device(): lax.ppermute(jnp.where(core == 0, for_odd, for_even), 'section', swap)  11.3 us
  transfers between devices with their start and end apart: 13, of which 6 were waited for; matrix products, arithmetic and copies ran while one was open for 4% of the time, Pallas kernels for 7%

profile of v2, /device:TPU:0, one launch (start us, length us, event | category | flops | bytes accessed | tf_op | source)
XLA Modules:
  0.0 507.2 jit_solution(1600945508753898203)
XLA Ops:
  13.0 2.4 collective-permute-start
  22.4 5.8 %all-gather.1 = f32[2,2,768]{2,1,0:T(2,128)} all-gather(f32[1,2,768]{2,1,0:T(2,128)S(1)} %maximum_bitcast_fusion), channel_id=2, replica_groups={{0,8},{16,24},{1,9},{17,25},{2,10},{18,26},{3,11},{19,27},{4,12},{20,28..., dimensions={0}, use_global_device_ids=true | all-gather | bytes 18432 | tf_op jit(solution)/shard_map/all_gather | solution.py:361
  35.0 16.4 %all-gather.5.cloned.1.call-done.first_h = bf16[2,768,3072]{2,1,0:T(8,128)(2,1)} async-done(((bf16[1,768,3072]{2,1,0:T(8,128)(2,1)}), bf16[2,768,3072]{2,1,0:T(8,128)(2,1)}) %all-gather.5.cloned.1.call-update) | async-done | bytes 9437200 | tf_op jit(solution)/shard_map/all_gather | solution.py:361
  51.3 35.2 %layer_forward.2 = (bf16[768,768]{1,0:T(8,128)(2,1)}, bf16[16,768]{1,0:T(8,128)(2,1)}, bf16[768,2304]{1,0:T(8,128)(2,1)}, bf16[3,6,256,512]{3,2,1,0:T(8,128)(2,1...) custom-call(bf16[768,768]{1,0:T(8,128)(2,1)} %select_select_fusion.3, ...), custom_call_target="tpu_custom_call" | custom-call | tf_op jit(solution)/shard_map/layer_forward/pallas_call | solution.py:151
  86.6 4.2 collective-permute-start.1
  91.9 3.1 fusion.7.x
  95.0 34.8 %layer_forward.3 = (bf16[768,768]{1,0:T(8,128)(2,1)}, bf16[16,768]{1,0:T(8,128)(2,1)}, bf16[768,2304]{1,0:T(8,128)(2,1)}, bf16[3,6,256,512]{3,2,1,0:T(8,128)(2,1...) custom-call(bf16[768,768]{1,0:T(8,128)(2,1)} %fusion.7.x, ...), custom_call_target="tpu_custom_call" | custom-call | tf_op jit(solution)/shard_map/layer_forward/pallas_call | solution.py:151
  129.8 33.4 %layer_backward.2 = (bf16[768,768]{1,0:T(8,128)(2,1)}, f32[16,768]{1,0:T(8,128)}, bf16[768,768]{1,0:T(8,128)(2,1)}, bf16[768,3072]{1,0:T(8,128)(2,1)}, bf16[768,...) custom-call(bf16[768,768]{1,0:T(8,128)(2,1)} %select_select_fusion.3.x.dy, f32[4,768]{1,0:T(4,128)} %reshape.87.norms, ...), custom_call_target="tpu_custom_call" | custom-call | tf_op jit(solution)/shard_map/layer_backward/pallas_call | solution.py:300
  164.6 4.7 collective-permute-done.4
  169.3 3.8 fusion.6.dy
  173.2 33.0 %layer_backward.3 = (bf16[768,768]{1,0:T(8,128)(2,1)}, f32[16,768]{1,0:T(8,128)}, bf16[768,768]{1,0:T(8,128)(2,1)}, bf16[768,3072]{1,0:T(8,128)(2,1)}, bf16[768,...) custom-call(bf16[768,768]{1,0:T(8,128)(2,1)} %fusion.6.dy, f32[4,768]{1,0:T(4,128)} %reshape.87.norms, ...), custom_call_target="tpu_custom_call" | custom-call | tf_op jit(solution)/shard_map/layer_backward/pallas_call | solution.py:300
  206.2 6.6 %convolution_convert_fusion.2 = bf16[768,3072]{1,0:T(8,128)(2,1)S(1)} fusion(bf16[768,768]{1,0:T(8,128)(2,1)} %get-tuple-element.38, bf16[768,3072]{1,0:T(8,128)(2,1)} %get-tuple-element.39), kind=kOutput, calls=%fused_computation.7 | convolution fusion | flops 3626237952 | bytes 10616832 | tf_op jit(solution)/shard_map/dot_general | solution.py:392
  215.2 3.3 convolution_convert_fusion
  219.7 4.4 convolution_convert_fusion.1
  226.1 11.3 %collective-permute-done.8 = bf16[768,4608]{1,0:T(8,128)(2,1)S(1)} collective-permute-done((bf16[768,4608]{1,0:T(8,128)(2,1)S(1)}, bf16[768,4608]{1,0:T(8,128)(2,1)S(1)}, u32[]{:S(2)}, u32[]{:S(2)}) %collective-permute-start.8) | collective-permute-done | bytes 7077920 | tf_op jit(solution)/shard_map/ppermute | solution.py:399
  237.3 4.5 add_convert_fusion
  245.4 2.3 collective-permute-start.6
  249.1 2.2 collective-permute-start.9
  253.1 23.2 %psum.15 = f32[2,768]{1,0:T(2,128)S(1)} all-reduce(f32[2,768]{1,0:T(2,128)} %select_add_fusion), channel_id=1, replica_groups=mesh['section'=4,'dp'=8] {'dp'}, use_global_device_ids=true, to_apply=%region_5.6 | all-reduce | flops 1536 | bytes 12288 | tf_op jit(solution)/shard_map/psum | solution.py:405
  278.9 3.6 fusion
  282.5 194.1 %all-reduce.3.cloned.1.call-done = bf16[768,4608]{1,0:T(8,128)(2,1)} async-done(((bf16[768,4608]{1,0:T(8,128)(2,1)}), bf16[768,4608]{1,0:T(8,128)(2,1)}) %all-reduce.3.cloned.1.call-update) | async-done | bytes 7077904 | tf_op jit(solution)/shard_map/psum | solution.py:401
  476.6 10.0 %convert_element_type.61 = f32[768,4608]{1,0:T(8,128)} convert(bf16[768,4608]{1,0:T(8,128)(2,1)} %all-reduce.3.cloned.1.call-done) | non-fusion elementwise | flops 3538944 | bytes 21233664 | tf_op jit(solution)/shard_map/convert_element_type | solution.py:401
  486.6 4.8 slice_bitcast_fusion.1
  491.4 8.8 %slice_bitcast_fusion = f32[1,768,3072]{2,1,0:T(8,128)} fusion(f32[768,4608]{1,0:T(8,128)} %convert_element_type.61), kind=kLoop, calls=%fused_computation.1 | loop fusion | bytes 18874368 | tf_op jit(solution)/shard_map/broadcast_in_dim | solution.py:420
  (92 shorter events, 36.9 us)
Async XLA Ops:
  7.2 2.9 copy-start
  7.2 27.8 %all-gather.7.cloned.1.call-start = ((), (), s32[]{:S(2)}) async-start(), calls=%async_computation.1 | async-start | bytes 7077888 | tf_op jit(solution)/shard_map/all_gather | solution.py:361
  7.9 43.4 %all-gather.5.cloned.1.call-start = ((), (), s32[]{:S(2)}) async-start(), calls=%async_computation | async-start | bytes 14155776 | tf_op jit(solution)/shard_map/all_gather | solution.py:361
  8.7 467.9 %all-reduce.3.cloned.1.call-start = ((), (), s32[]{:S(2)}) async-start(), calls=%async_computation.2 | async-start | bytes 14155776 | tf_op jit(solution)/shard_map/psum | solution.py:401
  13.0 20.6 %collective-permute-start = (bf16[768,768]{1,0:T(8,128)(2,1)}, bf16[768,768]{1,0:T(8,128)(2,1)S(1)}, u32[]{:S(2)}, u32[]{:S(2)}) collective-permute-start(bf16[768,768]{1,0:T(8,128)(2,1)} %broadcast_select_fusion.3), channel_id=1, source_target_pairs={{0,8},{24,16},{1,9},{25,17},{2,10},{26,18},{3,11},{27,19},{4,12},{... | collective-permute-start | bytes 3538952 | tf_op jit(solution)/shard_map/ppermute | solution.py:354
  15.4 75.4 %collective-permute-start.3 = (bf16[768,768]{1,0:T(8,128)(2,1)S(1)}, bf16[768,768]{1,0:T(8,128)(2,1)}, u32[]{:S(2)}, u32[]{:S(2)}) collective-permute-start(bf16[768,768]{1,0:T(8,128)(2,1)S(1)} %bitcast.41), channel_id=1, source_target_pairs={{8,24},{16,8},{9,25},{17,9},{10,26},{18,10},{11,27},{19,11},{12,28... | collective-permute-start | bytes 3538952 | tf_op jit(solution)/shard_map/ppermute | solution.py:356
  17.1 73.7 %collective-permute-start.2 = (bf16[768,768]{1,0:T(8,128)(2,1)S(1)}, bf16[768,768]{1,0:T(8,128)(2,1)}, u32[]{:S(2)}, u32[]{:S(2)}) collective-permute-start(bf16[768,768]{1,0:T(8,128)(2,1)S(1)} %bitcast.40), channel_id=1, source_target_pairs={{8,16},{16,0},{9,17},{17,1},{10,18},{18,2},{11,19},{19,3},{12,20},... | collective-permute-start | bytes 3538952 | tf_op jit(solution)/shard_map/ppermute | solution.py:355
  51.3 40.6 %copy-start.2 = (bf16[768,768]{1,0:T(8,128)(2,1)S(1)}, bf16[768,768]{1,0:T(8,128)(2,1)}, u32[]{:S(2)}) copy-start(bf16[768,768]{1,0:T(8,128)(2,1)} %select_select_fusion.3.x.dy) | copy-start | bytes 3538948
  86.6 5.4 %collective-permute-start.1 = (bf16[16,768]{1,0:T(8,128)(2,1)}, bf16[16,768]{1,0:T(8,128)(2,1)}, u32[]{:S(2)}, u32[]{:S(2)}) collective-permute-start(bf16[16,768]{1,0:T(8,128)(2,1)} %get-tuple-element.24), channel_id=1, source_target_pairs={{0,16},{8,24},{1,17},{9,25},{2,18},{10,26},{3,19},{11,27},{4,20},{... | collective-permute-start | bytes 73736 | tf_op jit(solution)/shard_map/ppermute | solution.py:378
  129.8 39.6 %copy-start.3 = (bf16[768,768]{1,0:T(8,128)(2,1)S(1)}, bf16[768,768]{1,0:T(8,128)(2,1)}, u32[]{:S(2)}) copy-start(bf16[768,768]{1,0:T(8,128)(2,1)} %select_select_fusion.3.x.dy) | copy-start | bytes 3538948
  129.8 39.6 %copy-start.12 = (s32[16]{0:T(128)S(1)}, s32[16]{0:T(128)}, u32[]{:S(2)}) copy-start(s32[16]{0:T(128)} %copy-done.11) | copy-start | bytes 196
  163.1 6.2 %collective-permute-start.4 = (f32[16,768]{1,0:T(8,128)}, f32[16,768]{1,0:T(8,128)S(1)}, u32[]{:S(2)}, u32[]{:S(2)}) collective-permute-start(f32[16,768]{1,0:T(8,128)} %get-tuple-element.33), channel_id=1, source_target_pairs={{16,0},{24,8},{17,1},{25,9},{18,2},{26,10},{19,3},{27,11},{20,4},{... | collective-permute-start | bytes 147464 | tf_op jit(solution)/shard_map/ppermute | solution.py:383
  212.8 2.4 copy-start.13
  212.8 6.8 %slice-start = ((s8[4718592]{0:T(1024)(128)(4,1)}), s8[4194304]{0:T(1024)(128)(4,1)S(1)}, s32[]{:S(2)}) async-start(s8[4718592]{0:T(1024)(128)(4,1)} %bitcast.50), calls=%async_computation.3 | async-start | bytes 8388608
  215.2 3.3 copy-start.15
  215.2 3.3 copy-start.16
  215.2 4.5 slice-start.1
  226.0 11.3 %collective-permute-start.8 = (bf16[768,4608]{1,0:T(8,128)(2,1)S(1)}, bf16[768,4608]{1,0:T(8,128)(2,1)S(1)}, u32[]{:S(2)}, u32[]{:S(2)}) collective-permute-start(bf16[768,4608]{1,0:T(8,128)(2,1)S(1)} %broadcast_select_fusion), channel_id=1, source_target_pairs={{0,8},{8,0},{16,24},{24,16},{1,9},{9,1},{17,25},{25,17},{2,10},{10... | collective-permute-start | bytes 21233672 | tf_op jit(solution)/shard_map/ppermute | solution.py:399
  243.5 5.6 %copy-start.7 = (f32[4,768]{1,0:T(4,128)S(1)}, f32[4,768]{1,0:T(4,128)}, u32[]{:S(2)}) copy-start(f32[4,768]{1,0:T(4,128)} %get-tuple-element.42) | copy-start | bytes 36868
  244.7 32.2 %collective-permute-start.7 = (bf16[768,768]{1,0:T(8,128)(2,1)}, bf16[768,768]{1,0:T(8,128)(2,1)S(1)}, u32[]{:S(2)}, u32[]{:S(2)}) collective-permute-start(bf16[768,768]{1,0:T(8,128)(2,1)} %get-tuple-element.49), channel_id=1, source_target_pairs={{8,16},{24,8},{9,17},{25,9},{10,18},{26,10},{11,19},{27,11},{12,20... | collective-permute-start | bytes 3538952 | tf_op jit(solution)/shard_map/ppermute | solution.py:410
  245.4 31.5 %collective-permute-start.6 = (bf16[768,768]{1,0:T(8,128)(2,1)}, bf16[768,768]{1,0:T(8,128)(2,1)S(1)}, u32[]{:S(2)}, u32[]{:S(2)}) collective-permute-start(bf16[768,768]{1,0:T(8,128)(2,1)} %get-tuple-element.49), channel_id=1, source_target_pairs={{0,16},{16,8},{1,17},{17,9},{2,18},{18,10},{3,19},{19,11},{4,20},{... | collective-permute-start | bytes 3538952 | tf_op jit(solution)/shard_map/ppermute | solution.py:409
  247.8 29.1 %collective-permute-start.5 = (bf16[768,768]{1,0:T(8,128)(2,1)S(1)}, bf16[768,768]{1,0:T(8,128)(2,1)}, u32[]{:S(2)}, u32[]{:S(2)}) collective-permute-start(bf16[768,768]{1,0:T(8,128)(2,1)S(1)} %get-tuple-element.50), channel_id=1, source_target_pairs={{8,0},{16,24},{9,1},{17,25},{10,2},{18,26},{11,3},{19,27},{12,4},{... | collective-permute-start | bytes 3538952 | tf_op jit(solution)/shard_map/ppermute | solution.py:412
  249.1 3.4 collective-permute-start.9
  491.4 8.8 %copy-start.1 = (bf16[1,1536,768]{2,1,0:T(8,128)(2,1)S(1)}, bf16[1,1536,768]{2,1,0:T(8,128)(2,1)}, u32[]{:S(2)}) copy-start(bf16[1,1536,768]{2,1,0:T(8,128)(2,1)} %param.6) | copy-start | bytes 7077892
  (8 other events, 8.1 us)
Sparse Core Ops, SparseCore 0:
  9.6 17.1 all-gather.6
  28.3 23.0 all-gather.4
  242.0 234.5 all-reduce.2

commit v3 on v2

--- a/solution.py
+++ b/solution.py
@@ -1,3 +1,5 @@
+import functools
+
 import jax
 import jax.numpy as jnp
 from jax import lax
@@ -175,8 +177,8 @@
 
 def backward_kernel(
     dy, norms, pick, rstd0, rstd1, first_h, second_h,
-    qkv_h, p_h, zh0_h, slope_h, zh1_h,
-    dx_h, lead, df_h, du_h, do_h, dqkv_h, dnorm,
+    qkv_h, p_h, zh0_h, slope_h, zh1_h, a_h,
+    dx_h, lead, df_h, rights, dnorm,
     wa, wu, wd, qkv, p, zh0, slope, zh1, dx, df, du, do, dqkv, dctx, acc, sems, out_sems,
 ):
     tokens, features = dy.shape
@@ -206,6 +208,8 @@
         c.start()
         stores.append(c)
 
+    keep(a_h.at[:, pl.ds(0, half)], rights.at[0, :, pl.ds(ff, half)])
+    keep(a_h.at[:, pl.ds(half, half)], rights.at[1, :, pl.ds(ff, half)])
     ld[0].wait()
     dz, dg, ds_ = normalize_back(zh1[...].astype(f32), rstd1[...], norms[2:3, :], dy[...].astype(f32))
     dnorm[2:3, :] = dg
@@ -223,7 +227,7 @@
         g = (da * slope[:, cols].astype(f32)).astype(bf16)
         du[:, cols] = g
         acc[...] += mm(g, wu[:, cols], NT)
-    keep(du, du_h)
+    keep(du, rights.at[1, :, pl.ds(0, ff)])
     ld[5].wait()
     d_mid = acc[...].astype(bf16).astype(f32)
     dz, dg, ds_ = normalize_back(zh0[...].astype(f32), rstd0[...], norms[0:1, :], d_mid)
@@ -231,7 +235,7 @@
     dnorm[1:2, :] = ds_
     do[...] = dz.astype(bf16)
     acc[...] = dz
-    keep(do, do_h)
+    keep(do, rights.at[0, :, pl.ds(n3, features)])
     ld[6].wait()
     dctx[...] = mm(do[...], wa[:, pl.ds(n3, features)], NT).astype(bf16)
     ld[7].wait()
@@ -270,7 +274,7 @@
         return carry
 
     lax.fori_loop(0, blocks, block_step, 0)
-    keep(dqkv, dqkv_h)
+    keep(dqkv, rights.at[0, :, pl.ds(0, n3)])
     for c in range(3):
         cols = pl.ds(c * features, features)
         acc[...] += mm(dqkv[:, cols], wa[:, cols], NT)
@@ -292,27 +296,363 @@
     vm = pl.BlockSpec(memory_space=pltpu.VMEM)
     shapes = dict(
         dx=S((tokens, features), bf16), lead=S((pick.shape[0], features), f32),
-        df=S((tokens, features), bf16), du=S((tokens, ff), bf16), do=S((tokens, features), bf16),
-        dqkv=S((tokens, 3 * features), bf16), dnorm=S((4, features), f32),
+        df=S((tokens, features), bf16), rights=S((2, tokens, ff + ff // 2), bf16), dnorm=S((4, features), f32),
     )
     V = lambda k: pltpu.VMEM(shapes[k].shape, shapes[k].dtype)
     L = lambda k: pltpu.VMEM(sv[k].shape, sv[k].dtype)
     outs = pl.pallas_call(
         backward_kernel,
         out_shape=list(shapes.values()),
-        in_specs=[vm] * 5 + [any_] * 7,
+        in_specs=[vm] * 5 + [any_] * 8,
         out_specs=[vm if k in ("lead", "dnorm") else any_ for k in shapes],
         scratch_shapes=[
             pltpu.VMEM(firsts.shape[1:], bf16), pltpu.VMEM(firsts.shape[1:], bf16), pltpu.VMEM((features, ff), bf16),
             L("qkv"), L("p"), L("zh0"), L("slope"), L("zh1"),
-            V("dx"), V("df"), V("du"), V("do"), V("dqkv"), pltpu.VMEM((tokens, features), bf16),
+            V("dx"), V("df"), pltpu.VMEM((tokens, ff), bf16), pltpu.VMEM((tokens, features), bf16),
+            pltpu.VMEM((tokens, 3 * features), bf16), pltpu.VMEM((tokens, features), bf16),
             pltpu.VMEM((tokens, features), f32),
-            pltpu.SemaphoreType.DMA((9,)), pltpu.SemaphoreType.DMA((5,)),
+            pltpu.SemaphoreType.DMA((9,)), pltpu.SemaphoreType.DMA((7,)),
         ],
         compiler_params=pltpu.CompilerParams(vmem_limit_bytes=60 << 20),
         name="layer_backward",
-    )(dy, norms, pick, sv["rstd0"], sv["rstd1"], firsts, seconds, sv["qkv"], sv["p"], sv["zh0"], sv["slope"], sv["zh1"])
+    )(dy, norms, pick, sv["rstd0"], sv["rstd1"], firsts, seconds, sv["qkv"], sv["p"], sv["zh0"], sv["slope"], sv["zh1"], sv["a"])
     return dict(zip(shapes, outs))
+
+
+PANEL = 128
+RING = 4
+MESH = pl.DeviceIdType.MESH
+
+
+def reduce_kernel(
+    chain, x_h, ctx_h, df_h, mid_h, rights, dnorm, out_h, norm_out,
+    left, left_t, own_ring, sib_ring, sib_send, sib_recv, part, y1, c1, zin1, mid1, zin2, mid2, d2, y2, final,
+    left_sem, own_sem, ring_sem, out_sem, sib_ss, sib_rs, y1_ss, y1_rs, z1_ss, z1_rs, m1_ss, m1_rs,
+    z2_ss, z2_rs, m2_ss, m2_rs, y2_ss, y2_rs, f_ss, f_rs,
+):
+    sec = lax.axis_index("section")
+    dp = lax.axis_index("dp")
+    core = sec % 2
+    panels, rows, _ = final.shape
+    half = rows // 2
+    features = rows
+    spot = dp // 2
+    side = spot // (chain // 2)
+    depth = chain // 2 - 1
+    dist = side * (spot - chain // 2) + (1 - side) * (chain // 2 - 1 - spot)
+    inner = dist == 0
+    y = dp % 2
+    sibling = {"section": sec + 1 - 2 * core}
+    across_y = {"dp": dp + 1 - 2 * y}
+    inward = {"dp": dp + 2 - 4 * side}
+    outward = {"dp": dp - 2 + 4 * side}
+    has_out = dist < depth
+
+    barrier = pltpu.get_barrier_semaphore()
+    for target in (sibling, across_y, inward):
+        pl.semaphore_signal(barrier, inc=1, device_id=target, device_id_type=MESH)
+
+    @pl.when(has_out)
+    def _():
+        pl.semaphore_signal(barrier, inc=1, device_id=outward, device_id_type=MESH)
+
+    def rows_at(which):
+        return pl.ds(pl.multiple_of(which * half, half), half)
+
+    mine, theirs = rows_at(y), rows_at(1 - y)
+    kept, rest = rows_at(side), rows_at(1 - side)
+
+    def remote(src, dst, ss, rs, target):
+        return pltpu.make_async_remote_copy(
+            src_ref=src, dst_ref=dst, send_sem=ss, recv_sem=rs, device_id=target, device_id_type=MESH
+        )
+
+    def to_sibling(j):
+        return remote(sib_send.at[j % RING], sib_recv.at[j], sib_ss.at[j % RING], sib_rs.at[j], sibling)
+
+    def one_y(j):
+        i = j // 2
+        return remote(part.at[j, theirs], y1.at[i], y1_ss.at[i], y1_rs.at[i], across_y)
+
+    def one_in(j):
+        i = j // 2
+        return remote(c1.at[i], zin1.at[i], z1_ss.at[i], z1_rs.at[i], inward)
+
+    def one_mid(j):
+        i = j // 2
+        return remote(c1.at[i], mid1.at[i], m1_ss.at[i], m1_rs.at[i], inward)
+
+    def one_out(j):
+        return remote(final.at[j, mine], final.at[j, mine], f_ss.at[0, j], f_rs.at[0, j], outward)
+
+    def one_back(j):
+        return remote(final.at[j, mine], final.at[j, mine], f_ss.at[1, j], f_rs.at[1, j], across_y)
+
+    def one_back_in(j):
+        return remote(final.at[j, theirs], final.at[j, theirs], f_ss.at[1, j], f_rs.at[1, j], across_y)
+
+    def two_in(j):
+        i = j // 2
+        return remote(part.at[j], zin2.at[i], z2_ss.at[i], z2_rs.at[i], inward)
+
+    def two_mid(j):
+        i = j // 2
+        return remote(part.at[j, rest], mid2.at[i], m2_ss.at[i], m2_rs.at[i], inward)
+
+    def two_y(j):
+        i = j // 2
+        return remote(d2.at[i], y2.at[i], y2_ss.at[i], y2_rs.at[i], across_y)
+
+    def two_swap(j):
+        return remote(final.at[j, kept], final.at[j, kept], f_ss.at[2, j], f_rs.at[1, j], inward)
+
+    def two_swap_in(j):
+        return remote(final.at[j, rest], final.at[j, rest], f_ss.at[2, j], f_rs.at[1, j], inward)
+
+    def two_out_kept(j):
+        return remote(final.at[j, kept], final.at[j, kept], f_ss.at[0, j], f_rs.at[0, j], outward)
+
+    def two_out_rest(j):
+        return remote(final.at[j, rest], final.at[j, rest], f_ss.at[1, j], f_rs.at[1, j], outward)
+
+    def left_of(who, j):
+        p = j - 1
+        even = p // (3 * features // PANEL) + p // (4 * features // PANEL)
+        odd = 3 - p // (4 * features // PANEL)
+        return who * odd + (1 - who) * even
+
+    def fetch(who, j, ring, sem):
+        cols = pl.ds(pl.multiple_of((j - 1) * PANEL, PANEL), PANEL)
+        return pltpu.make_async_copy(rights.at[who, :, cols], ring.at[j % RING], sem.at[j % RING])
+
+    def to_out(j):
+        cols = pl.ds(pl.multiple_of((j - 1) * PANEL, PANEL), PANEL)
+        return pltpu.make_async_copy(final.at[j], out_h.at[:, cols], out_sem.at[j])
+
+    lefts = [pltpu.make_async_copy(h, left.at[i], left_sem.at[i]) for i, h in enumerate((x_h, ctx_h, df_h, mid_h))]
+    for i in (0, 3, 1, 2):
+        lefts[i].start()
+    for j in range(1, RING):
+        fetch(core, j, own_ring, own_sem).start()
+        fetch(1 - core, j, sib_ring, ring_sem).start()
+
+    def turn(i):
+        grid = (rows, rows)
+        eye = lax.broadcasted_iota(jnp.int32, grid, 0) == lax.broadcasted_iota(jnp.int32, grid, 1)
+        left_t[i] = mm(eye.astype(bf16), left[i], NT).astype(bf16)
+
+    def norm_panel(other):
+        chosen = jnp.where(core == other, dnorm[2:4, :], dnorm[0:2, :])
+        strips = [
+            chosen[r : r + 1, c * PANEL : (c + 1) * PANEL]
+            for r in range(2)
+            for c in range(features // PANEL)
+        ]
+        return jnp.concatenate(strips + [jnp.zeros((16 - len(strips), PANEL), f32)], axis=0)
+
+    pl.semaphore_wait(barrier, 3 + has_out.astype(jnp.int32))
+
+    def when(cond, step, *args):
+        @pl.when(cond)
+        def _():
+            step(*args)
+
+    def stage_send(j):
+        when(j >= RING, lambda: to_sibling(j - RING).wait_send())
+
+        @pl.when(j == 0)
+        def _():
+            sib_send[0] = jnp.zeros((rows, PANEL), bf16)
+            sib_send[0, 0:16, :] = norm_panel(0).astype(bf16)
+
+        @pl.when(j > 0)
+        def _():
+            fetch(1 - core, j, sib_ring, ring_sem).wait()
+            sib_send[j % RING] = mm(left_t[left_of(1 - core, j)], sib_ring[j % RING]).astype(bf16)
+
+        to_sibling(j).start()
+        nxt = j + RING
+        when(
+            (j >= 0) & (nxt < panels),
+            lambda: fetch(1 - core, nxt, sib_ring, ring_sem).start(),
+        )
+
+    def stage_part(j):
+        to_sibling(j).wait_recv()
+
+        @pl.when(j == 0)
+        def _():
+            part[0] = jnp.zeros((rows, PANEL), bf16)
+            part[0, 0:16, :] = (norm_panel(1) + sib_recv[0, 0:16, :].astype(f32)).astype(bf16)
+
+        @pl.when(j > 0)
+        def _():
+            fetch(core, j, own_ring, own_sem).wait()
+            own = mm(left_t[left_of(core, j)], own_ring[j % RING])
+            part[j] = (own + sib_recv[j].astype(f32)).astype(bf16)
+
+        nxt = j + RING
+        when((nxt < panels), lambda: fetch(core, nxt, own_ring, own_sem).start())
+        when(j % 2 == 0, lambda: one_y(j).start())
+        when((j % 2 == 1) & (dist == depth) & (depth > 0), lambda: two_in(j).start())
+        when((j % 2 == 1) & (dist == depth) & (depth == 0), lambda: two_mid(j).start())
+
+    def one_halves(j):
+        one_y(j).wait_recv()
+        c1[j // 2] = (part[j, mine, :].astype(f32) + y1[j // 2].astype(f32)).astype(bf16)
+        when((dist == depth) & (dist > 0), lambda: one_in(j).start())
+        when((dist == depth) & inner, lambda: one_mid(j).start())
+
+    def one_chain(j):
+        one_in(j).wait_recv()
+        c1[j // 2] = (c1[j // 2].astype(f32) + zin1[j // 2].astype(f32)).astype(bf16)
+        when(dist > 0, lambda: one_in(j).start())
+        when(inner, lambda: one_mid(j).start())
+
+    def one_total(j):
+        one_mid(j).wait_recv()
+        final[j, mine, :] = (c1[j // 2].astype(f32) + mid1[j // 2].astype(f32)).astype(bf16)
+        when(has_out, lambda: one_out(j).start())
+        one_back(j).start()
+
+    def one_spread(j):
+        one_out(j).wait_recv()
+        when(has_out, lambda: one_out(j).start())
+        one_back(j).start()
+
+    def two_chain(j):
+        two_in(j).wait_recv()
+        part[j] = (part[j].astype(f32) + zin2[j // 2].astype(f32)).astype(bf16)
+        when(dist > 0, lambda: two_in(j).start())
+        when(inner, lambda: two_mid(j).start())
+
+    def two_halves(j):
+        two_mid(j).wait_recv()
+        d2[j // 2] = (part[j, kept, :].astype(f32) + mid2[j // 2].astype(f32)).astype(bf16)
+        two_y(j).start()
+
+    def two_total(j):
+        two_y(j).wait_recv()
+        final[j, kept, :] = (d2[j // 2].astype(f32) + y2[j // 2].astype(f32)).astype(bf16)
+        two_swap(j).start()
+        when(has_out, lambda: two_out_kept(j).start())
+
+    def two_swapped(j):
+        two_swap_in(j).wait_recv()
+        when(has_out, lambda: two_out_rest(j).start())
+
+    def two_spread_kept(j):
+        two_out_kept(j).wait_recv()
+        when(has_out, lambda: two_out_kept(j).start())
+
+    def two_spread_rest(j):
+        two_out_rest(j).wait_recv()
+        when(has_out, lambda: two_out_rest(j).start())
+
+    def finish(j):
+        when(j % 2 == 0, lambda: one_back_in(j).wait_recv())
+
+        @pl.when(j == 0)
+        def _():
+            norm_out[...] = final[0, 0:16, :].astype(f32)
+
+        when(j > 0, lambda: to_out(j).start())
+
+    last_lag = 4 + 2 * depth
+
+    def step(t, carry):
+        def at(lag, kind, cond, run):
+            j = t - lag
+            ok = (j >= 0) & (j < panels)
+            if kind is not None:
+                ok = ok & (j % 2 == kind)
+            if cond is not None:
+                ok = ok & cond
+            when(ok, run, j)
+
+        at(4 + depth + dist, 1, dist > 0, two_spread_rest)
+        at(3 + depth + dist, 1, dist > 0, two_spread_kept)
+        at(3 + depth + dist, 0, dist > 0, one_spread)
+        at(4 + depth, 1, inner, two_swapped)
+        at(3 + depth, 1, inner, two_total)
+        at(3 + depth, 0, inner, one_total)
+        at(2 + depth, 1, inner, two_halves)
+        at(2 + depth - dist, 0, dist < depth, one_chain)
+        at(1 + depth - dist, 1, dist < depth, two_chain)
+        at(2, 0, None, one_halves)
+        at(1, None, None, stage_part)
+        at(0, None, None, stage_send)
+        at(last_lag, None, None, finish)
+        when(t == 0, lambda: [lefts[0].wait(), turn(0), lefts[3].wait(), turn(3)])
+        when(t == 4, lambda: [lefts[1].wait(), turn(1), lefts[2].wait(), turn(2)])
+        return carry
+
+    lax.fori_loop(0, panels + last_lag, step, 0)
+
+    def drain(j, carry):
+        when(j >= panels - RING, lambda: to_sibling(j).wait_send())
+        when(j > 0, lambda: to_out(j).wait())
+
+        @pl.when(j % 2 == 0)
+        def _():
+            one_y(j).wait_send()
+            when(dist > 0, lambda: one_in(j).wait_send())
+            when(inner, lambda: one_mid(j).wait_send())
+            when(has_out, lambda: one_out(j).wait_send())
+            one_back(j).wait_send()
+
+        @pl.when(j % 2 == 1)
+        def _():
+            when(dist > 0, lambda: two_in(j).wait_send())
+
+            @pl.when(inner)
+            def _():
+                two_mid(j).wait_send()
+                two_y(j).wait_send()
+                two_swap(j).wait_send()
+
+            @pl.when(has_out)
+            def _():
+                two_out_kept(j).wait_send()
+                two_out_rest(j).wait_send()
+
+        return carry
+
+    lax.fori_loop(0, panels, drain, 0)
+
+
+def reduce_gradients(lefts, rights, dnorm, chain):
+    rows = lefts[0].shape[0]
+    features = lefts[0].shape[1]
+    panels = rights.shape[2] // PANEL + 1
+    evens, odds = (panels + 1) // 2, panels // 2
+    any_ = pl.BlockSpec(memory_space=pl.ANY)
+    vm = pl.BlockSpec(memory_space=pltpu.VMEM)
+    V = lambda *s: pltpu.VMEM(s, bf16)
+    D = lambda *s: pltpu.SemaphoreType.DMA(s)
+    h = features // 2
+    return pl.pallas_call(
+        functools.partial(reduce_kernel, chain),
+        out_shape=[
+            jax.ShapeDtypeStruct((features, rights.shape[2]), bf16),
+            jax.ShapeDtypeStruct((16, PANEL), f32),
+        ],
+        in_specs=[any_] * 5 + [vm],
+        out_specs=[any_, vm],
+        scratch_shapes=[
+            V(4, rows, features), V(4, features, rows), V(RING, rows, PANEL), V(RING, rows, PANEL),
+            V(RING, features, PANEL), V(panels, features, PANEL), V(panels, features, PANEL),
+            V(evens, h, PANEL), V(evens, h, PANEL), V(evens, h, PANEL), V(evens, h, PANEL),
+            V(odds, features, PANEL), V(odds, h, PANEL), V(odds, h, PANEL), V(odds, h, PANEL),
+            V(panels, features, PANEL),
+            D(4), D(RING), D(RING), D(panels), D(RING), D(panels), D(evens), D(evens), D(evens), D(evens), D(evens), D(evens),
+            D(odds), D(odds), D(odds), D(odds), D(odds), D(odds), D(3, panels), D(2, panels),
+        ],
+        compiler_params=pltpu.CompilerParams(
+            vmem_limit_bytes=60 << 20, collective_id=1, has_side_effects=True
+        ),
+        name="reduce_gradients",
+    )(*lefts, rights, dnorm)
 
 
 def row_tables(lengths, core):
@@ -342,7 +682,6 @@
     rows = tokens // SEQ
     half_tokens = rows * BLOCK
     pairs = [[0, 1], [2, 3]]
-    swap = [(0, 1), (1, 0), (2, 3), (3, 2)]
     roll, segment, pick = row_tables(span_lengths, core)
 
     rolled = jnp.einsum(
@@ -384,25 +723,11 @@
     d_twelve = (from_leads(lead_grads) + aux.astype(f32)).astype(bf16)
     upstream = jnp.where(at_head, main, d_twelve)
     grads = backward(upstream, norms, pick, saved, first2, second2)
-    dx, df, du, d_out, dqkv = (grads[k] for k in ("dx", "df", "du", "do", "dqkv"))
-    d_norm = grads["dnorm"].reshape(2, 2, features)
-    y_ffn, middle, a, ctx = (saved[k] for k in ("y", "mid", "a", "ctx"))
-
-    def outer(left, right):
-        return lax.dot_general(left, right, TN, preferred_element_type=f32).astype(bf16)
-
-    d_down = outer(df, a)
-    half_ff = d_down.shape[1] // 2
-    for_even = jnp.concatenate([outer(inputs, dqkv), outer(ctx, d_out), d_down[:, :half_ff]], axis=1)
-    for_odd = jnp.concatenate([outer(middle, du), d_down[:, half_ff:]], axis=1)
-    kept = jnp.where(core == 0, for_even, for_odd)
-    given = lax.ppermute(jnp.where(core == 0, for_odd, for_even), "section", swap)
-    total = (kept.astype(f32) + given.astype(f32)).astype(bf16)
-    total = lax.psum(total, "dp").astype(f32)
+    dx, y_ffn = grads["dx"], saved["y"]
+    lefts = (inputs, saved["ctx"], grads["df"], saved["mid"])
+    total, norm_total = reduce_gradients(lefts, grads["rights"], grads["dnorm"], lax.axis_size("dp") // 2)
     ff = first_weights.shape[2]
-    d_norm_kept = jnp.where(core == 0, d_norm[0], d_norm[1])
-    d_norm_given = lax.ppermute(jnp.where(core == 0, d_norm[1], d_norm[0]), "section", swap)
-    norm_total = lax.psum(d_norm_kept + d_norm_given, "dp")
+    norm_total = norm_total.reshape(-1)[: 2 * features].reshape(2, features)
 
     dskip = jnp.where(leading, jnp.zeros_like(dx), dx)
     across = jnp.where(at_head, dskip, y_ffn)
@@ -417,7 +742,7 @@
         "rij,rid->rjd", roll, out.reshape(rows, SEQ, features), preferred_element_type=f32
     ).reshape(tokens, features)
     return (
-        out[None], total[None, :, :ff], total[None, :, ff:], norm_total[None, 0], norm_total[None, 1]
+        out[None], total[None, :, :ff].astype(f32), total[None, :, ff:].astype(f32), norm_total[None, 0], norm_total[None, 1]
     )
 
 

time: 514 us -> 678 us (1.32)
  Pallas kernels: 136 us -> 571 us
  waiting for transfers between devices: 230 us -> 23.4 us
  blocking collectives: 29 us -> 5.77 us
  local copies, waits for them, and re-layouts: 24.8 us -> 8.02 us
  matrix products: 27.3 us -> 11.9 us
    pallas_call x2, Pallas kernels: 66.4 us -> 293 us  [backward(): pl.pallas_call(backward_kernel, out_shape=list(shapes.values()), in_specs...]
    pallas_call x0 -> x1, Pallas kernels: none -> 208 us  [reduce_gradients(): pl.pallas_call(functools.partial(reduce_kernel, chain), out_shape=[jax.Sh...]
    psum x1 -> x0, waiting for transfers between devices: 194 us -> none  [per_device(): total = lax.psum(total, 'dp').astype(f32)]
    psum x1 -> x0, blocking collectives: 23.2 us -> none  [per_device(): norm_total = lax.psum(d_norm_kept + d_norm_given, 'dp')]
    dot_general x4 -> x0, matrix products: 15.4 us -> none  [outer(): lax.dot_general(left, right, TN, preferred_element_type=f32).astype(bf16)]
    broadcast_in_dim x2 -> x0, local copies, waits for them, and re-layouts: 13.6 us -> none  [the longest x1 8.75 us: per_device(): total[None, :, :ff]]
    ppermute x2 -> x0, waiting for transfers between devices: 12.5 us -> none  [the longest x1 11.3 us: per_device(): lax.ppermute(jnp.where(core == 0, for_odd, for_even), 'section', swap)]
  transfers between devices with their start and end apart: 13 -> 10, of which waited for: 6 -> 3; matrix products, arithmetic and copies ran while one was open for 4% -> 4% of each run, Pallas kernels for 7% -> 36%
where the time goes in v3:
time: 678 us; the launch traced here: 672 us
  Pallas kernels  571 us (84%)
  waiting for transfers between devices  23.4 us (3%)
  other arithmetic  20.7 us (3%)
  starting transfers between devices  16.5 us (2%)
  between operations  14.8 us (2%)
  matrix products  11.9 us (2%)
  local copies, waits for them, and re-layouts  8.02 us (1%)
    pallas_call x2, Pallas kernels, backward(): pl.pallas_call(backward_kernel, out_shape=list(shapes.values()), in_specs...  293 us
    pallas_call x1, Pallas kernels, reduce_gradients(): pl.pallas_call(functools.partial(reduce_kernel, chain), out_shape=[jax.Sh...  208 us
    pallas_call x2, Pallas kernels, forward(): pl.pallas_call(forward_kernel, out_shape=list(shapes.values()), in_specs=...  70.4 us
    all_gather x2, waiting for transfers between devices, both(): return lax.all_gather(block, 'section', axis_index_groups=pairs)  16.2 us
  transfers between devices with their start and end apart: 10, of which 3 were waited for; matrix products, arithmetic and copies ran while one was open for 4% of the time, Pallas kernels for 36%

profile of v3, /device:TPU:0, one launch (start us, length us, event | category | flops | bytes accessed | tf_op | source)
XLA Modules:
  0.0 672.1 jit_solution(14725099205987412892)
XLA Ops:
  10.0 1.4 fusion.2
  12.9 2.4 collective-permute-start
  15.3 1.7 collective-permute-start.3
  19.1 1.4 fusion.15
  21.0 1.3 reshape.83
  22.4 5.8 all-gather.1
  33.7 1.5 select_select_fusion.3.x.dy
  35.1 16.2 %all-gather.5.cloned.1.call-done.first_h = bf16[2,768,3072]{2,1,0:T(8,128)(2,1)} async-done(((bf16[1,768,3072]{2,1,0:T(8,128)(2,1)}), bf16[2,768,3072]{2,1,0:T(8,128)(2,1)}) %all-gather.5.cloned.1.call-update) | async-done | bytes 9437200 | tf_op jit(solution)/shard_map/all_gather | solution.py:700
  51.3 35.3 %layer_forward.2 = (bf16[768,768]{1,0:T(8,128)(2,1)}, bf16[16,768]{1,0:T(8,128)(2,1)}, bf16[768,2304]{1,0:T(8,128)(2,1)}, bf16[3,6,256,512]{3,2,1,0:T(8,128)(2,1...) custom-call(bf16[768,768]{1,0:T(8,128)(2,1)} %select_select_fusion.3, ...), custom_call_target="tpu_custom_call" | custom-call | tf_op jit(solution)/shard_map/layer_forward/pallas_call | solution.py:153
  86.7 4.2 collective-permute-start.1
  92.1 3.1 fusion.7.x.x_h
  95.1 35.1 %layer_forward.3 = (bf16[768,768]{1,0:T(8,128)(2,1)}, bf16[16,768]{1,0:T(8,128)(2,1)}, bf16[768,2304]{1,0:T(8,128)(2,1)}, bf16[3,6,256,512]{3,2,1,0:T(8,128)(2,1...) custom-call(bf16[768,768]{1,0:T(8,128)(2,1)} %fusion.7.x.x_h, ...), custom_call_target="tpu_custom_call" | custom-call | tf_op jit(solution)/shard_map/layer_forward/pallas_call | solution.py:153
  130.2 146.5 %layer_backward.2 = (bf16[768,768]{1,0:T(8,128)(2,1)}, f32[16,768]{1,0:T(8,128)}, bf16[768,768]{1,0:T(8,128)(2,1)}, bf16[2,768,4608]{2,1,0:T(8,128)(2,1)}, f32[4,768]{1,0:T(4,128)}) custom-call(bf16[768,768]{1,0:T(8,128)(2,1)} %select_select_fusion.3.x.dy, f32[4,768]{1,0:T(4,128)} %reshape.94.norms, bf16[16,768]{1,0:T(8,128)(2,1)} %fusion.8.pick, ...), custom_call_target="tpu_custom_call" | custom-call | tf_op jit(solution)/shard_map/layer_backward/pallas_call | solution.py:303
  276.7 1.5 collective-permute-start.4
  278.2 4.7 collective-permute-done.4
  282.9 3.8 fusion.6.dy
  286.7 146.5 %layer_backward.3 = (bf16[768,768]{1,0:T(8,128)(2,1)}, f32[16,768]{1,0:T(8,128)}, bf16[768,768]{1,0:T(8,128)(2,1)}, bf16[2,768,4608]{2,1,0:T(8,128)(2,1)}, f32[4,768]{1,0:T(4,128)}) custom-call(bf16[768,768]{1,0:T(8,128)(2,1)} %fusion.6.dy, f32[4,768]{1,0:T(4,128)} %reshape.94.norms, bf16[16,768]{1,0:T(8,128)(2,1)} %fusion.8.pick, ...), custom_call_target="tpu_custom_call" | custom-call | tf_op jit(solution)/shard_map/layer_backward/pallas_call | solution.py:303
  433.2 1.6 select_select_fusion.2
  435.6 3.3 collective-permute-start.6
  440.2 207.6 %reduce_gradients.1 = (bf16[768,4608]{1,0:T(8,128)(2,1)}, f32[16,128]{1,0:T(8,128)}) custom-call(bf16[768,768]{1,0:T(8,128)(2,1)} %fusion.7.x.x_h, bf16[768,768]{1,0:T(8,128)(2,1)} %get-tuple-element.36.ctx_h, bf16[768,768]{1,0:T(8,128)(2,1)} %get-tuple-element.37.df_h, bf16[768,768]{1,0:T(8,128)(2,1)} %get-tuple-element.38.mid_h, ...), custom_call_target="tpu_custom_call" | custom-call | tf_op jit(solution)/shard_map/reduce_gradients/pallas_call | solution.py:634
  648.5 4.6 bitcast_convert_fusion.1
  653.7 5.0 bitcast_convert_fusion
  658.8 1.9 select_select_fusion.1
  661.1 3.6 fusion
  (59 shorter events, 17.2 us)
Async XLA Ops:
  7.2 2.9 copy-start
  7.2 27.9 %all-gather.7.cloned.1.call-start = ((), (), s32[]{:S(2)}) async-start(), calls=%async_computation.1 | async-start | bytes 7077888 | tf_op jit(solution)/shard_map/all_gather | solution.py:700
  7.9 0.8 copy-start.7
  7.9 43.4 %all-gather.5.cloned.1.call-start = ((), (), s32[]{:S(2)}) async-start(), calls=%async_computation | async-start | bytes 14155776 | tf_op jit(solution)/shard_map/all_gather | solution.py:700
  8.8 0.7 copy-start.6
  9.5 0.5 copy-start.8
  12.9 20.7 %collective-permute-start = (bf16[768,768]{1,0:T(8,128)(2,1)}, bf16[768,768]{1,0:T(8,128)(2,1)S(1)}, u32[]{:S(2)}, u32[]{:S(2)}) collective-permute-start(bf16[768,768]{1,0:T(8,128)(2,1)} %broadcast_select_fusion.2), channel_id=1, source_target_pairs={{0,8},{24,16},{1,9},{25,17},{2,10},{26,18},{3,11},{27,19},{4,12},{... | collective-permute-start | bytes 3538952 | tf_op jit(solution)/shard_map/ppermute | solution.py:693
  15.3 75.6 %collective-permute-start.3 = (bf16[768,768]{1,0:T(8,128)(2,1)S(1)}, bf16[768,768]{1,0:T(8,128)(2,1)}, u32[]{:S(2)}, u32[]{:S(2)}) collective-permute-start(bf16[768,768]{1,0:T(8,128)(2,1)S(1)} %bitcast.45), channel_id=1, source_target_pairs={{8,24},{16,8},{9,25},{17,9},{10,26},{18,10},{11,27},{19,11},{12,28... | collective-permute-start | bytes 3538952 | tf_op jit(solution)/shard_map/ppermute | solution.py:695
  17.0 73.9 %collective-permute-start.2 = (bf16[768,768]{1,0:T(8,128)(2,1)S(1)}, bf16[768,768]{1,0:T(8,128)(2,1)}, u32[]{:S(2)}, u32[]{:S(2)}) collective-permute-start(bf16[768,768]{1,0:T(8,128)(2,1)S(1)} %bitcast.44), channel_id=1, source_target_pairs={{8,16},{16,0},{9,17},{17,1},{10,18},{18,2},{11,19},{19,3},{12,20},... | collective-permute-start | bytes 3538952 | tf_op jit(solution)/shard_map/ppermute | solution.py:694
  32.5 0.5 copy-start.9
  51.3 40.7 %copy-start.2 = (bf16[768,768]{1,0:T(8,128)(2,1)S(1)}, bf16[768,768]{1,0:T(8,128)(2,1)}, u32[]{:S(2)}) copy-start(bf16[768,768]{1,0:T(8,128)(2,1)} %select_select_fusion.3.x.dy) | copy-start | bytes 3538948
  86.7 5.4 collective-permute-start.1
  130.2 152.7 %copy-start.3 = (bf16[768,768]{1,0:T(8,128)(2,1)S(1)}, bf16[768,768]{1,0:T(8,128)(2,1)}, u32[]{:S(2)}) copy-start(bf16[768,768]{1,0:T(8,128)(2,1)} %select_select_fusion.3.x.dy) | copy-start | bytes 3538948
  130.2 152.7 %copy-start.10 = (s32[16]{0:T(128)S(1)}, s32[16]{0:T(128)}, u32[]{:S(2)}) copy-start(s32[16]{0:T(128)} %copy-done.9) | copy-start | bytes 196
  276.7 6.2 collective-permute-start.4
  286.7 146.5 %copy-start.5 = (bf16[768,768]{1,0:T(8,128)(2,1)S(1)}, bf16[768,768]{1,0:T(8,128)(2,1)}, u32[]{:S(2)}) copy-start(bf16[768,768]{1,0:T(8,128)(2,1)} %get-tuple-element.25) | copy-start | bytes 3538948
  434.8 223.9 %collective-permute-start.7 = (bf16[768,768]{1,0:T(8,128)(2,1)S(1)}, bf16[768,768]{1,0:T(8,128)(2,1)S(1)}, u32[]{:S(2)}, u32[]{:S(2)}) collective-permute-start(bf16[768,768]{1,0:T(8,128)(2,1)S(1)} %get-tuple-element.47), channel_id=1, source_target_pairs={{8,16},{24,8},{9,17},{25,9},{10,18},{26,10},{11,19},{27,11},{12,20... | collective-permute-start | bytes 3538952 | tf_op jit(solution)/shard_map/ppermute | solution.py:735
  435.6 223.2 %collective-permute-start.6 = (bf16[768,768]{1,0:T(8,128)(2,1)S(1)}, bf16[768,768]{1,0:T(8,128)(2,1)}, u32[]{:S(2)}, u32[]{:S(2)}) collective-permute-start(bf16[768,768]{1,0:T(8,128)(2,1)S(1)} %get-tuple-element.47), channel_id=1, source_target_pairs={{0,16},{16,8},{1,17},{17,9},{2,18},{18,10},{3,19},{19,11},{4,20},{... | collective-permute-start | bytes 3538952 | tf_op jit(solution)/shard_map/ppermute | solution.py:734
  438.9 219.9 %collective-permute-start.5 = (bf16[768,768]{1,0:T(8,128)(2,1)S(1)}, bf16[768,768]{1,0:T(8,128)(2,1)}, u32[]{:S(2)}, u32[]{:S(2)}) collective-permute-start(bf16[768,768]{1,0:T(8,128)(2,1)S(1)} %get-tuple-element.48), channel_id=1, source_target_pairs={{8,0},{16,24},{9,1},{17,25},{10,2},{18,26},{11,3},{19,27},{12,4},{... | collective-permute-start | bytes 3538952 | tf_op jit(solution)/shard_map/ppermute | solution.py:737
  648.5 5.2 copy-start.4
  661.1 3.6 copy-start.1
Sparse Core Ops, SparseCore 0:
  9.6 17.1 all-gather.6
  28.3 23.0 all-gather.4

commit v4 on v3

--- a/solution.py
+++ b/solution.py
@@ -177,7 +177,7 @@
 
 def backward_kernel(
     dy, norms, pick, rstd0, rstd1, first_h, second_h,
-    qkv_h, p_h, zh0_h, slope_h, zh1_h, a_h,
+    qkv_h, p_h, zh0_h, slope_h, zh1_h,
     dx_h, lead, df_h, rights, dnorm,
     wa, wu, wd, qkv, p, zh0, slope, zh1, dx, df, du, do, dqkv, dctx, acc, sems, out_sems,
 ):
@@ -208,8 +208,6 @@
         c.start()
         stores.append(c)
 
-    keep(a_h.at[:, pl.ds(0, half)], rights.at[0, :, pl.ds(ff, half)])
-    keep(a_h.at[:, pl.ds(half, half)], rights.at[1, :, pl.ds(ff, half)])
     ld[0].wait()
     dz, dg, ds_ = normalize_back(zh1[...].astype(f32), rstd1[...], norms[2:3, :], dy[...].astype(f32))
     dnorm[2:3, :] = dg
@@ -296,14 +294,14 @@
     vm = pl.BlockSpec(memory_space=pltpu.VMEM)
     shapes = dict(
         dx=S((tokens, features), bf16), lead=S((pick.shape[0], features), f32),
-        df=S((tokens, features), bf16), rights=S((2, tokens, ff + ff // 2), bf16), dnorm=S((4, features), f32),
+        df=S((tokens, features), bf16), rights=S((2, tokens, ff), bf16), dnorm=S((4, features), f32),
     )
     V = lambda k: pltpu.VMEM(shapes[k].shape, shapes[k].dtype)
     L = lambda k: pltpu.VMEM(sv[k].shape, sv[k].dtype)
     outs = pl.pallas_call(
         backward_kernel,
         out_shape=list(shapes.values()),
-        in_specs=[vm] * 5 + [any_] * 8,
+        in_specs=[vm] * 5 + [any_] * 7,
         out_specs=[vm if k in ("lead", "dnorm") else any_ for k in shapes],
         scratch_shapes=[
             pltpu.VMEM(firsts.shape[1:], bf16), pltpu.VMEM(firsts.shape[1:], bf16), pltpu.VMEM((features, ff), bf16),
@@ -311,21 +309,22 @@
             V("dx"), V("df"), pltpu.VMEM((tokens, ff), bf16), pltpu.VMEM((tokens, features), bf16),
             pltpu.VMEM((tokens, 3 * features), bf16), pltpu.VMEM((tokens, features), bf16),
             pltpu.VMEM((tokens, features), f32),
-            pltpu.SemaphoreType.DMA((9,)), pltpu.SemaphoreType.DMA((7,)),
+            pltpu.SemaphoreType.DMA((9,)), pltpu.SemaphoreType.DMA((5,)),
         ],
         compiler_params=pltpu.CompilerParams(vmem_limit_bytes=60 << 20),
         name="layer_backward",
-    )(dy, norms, pick, sv["rstd0"], sv["rstd1"], firsts, seconds, sv["qkv"], sv["p"], sv["zh0"], sv["slope"], sv["zh1"], sv["a"])
+    )(dy, norms, pick, sv["rstd0"], sv["rstd1"], firsts, seconds, sv["qkv"], sv["p"], sv["zh0"], sv["slope"], sv["zh1"])
     return dict(zip(shapes, outs))
 
 
 PANEL = 128
+SPLIT = 1
 RING = 4
 MESH = pl.DeviceIdType.MESH
 
 
 def reduce_kernel(
-    chain, x_h, ctx_h, df_h, mid_h, rights, dnorm, out_h, norm_out,
+    chain, x_h, ctx_h, df_h, mid_h, rights, a_h, dnorm, out_h, norm_out,
     left, left_t, own_ring, sib_ring, sib_send, sib_recv, part, y1, c1, zin1, mid1, zin2, mid2, d2, y2, final,
     left_sem, own_sem, ring_sem, out_sem, sib_ss, sib_rs, y1_ss, y1_rs, z1_ss, z1_rs, m1_ss, m1_rs,
     z2_ss, z2_rs, m2_ss, m2_rs, y2_ss, y2_rs, f_ss, f_rs,
@@ -335,7 +334,7 @@
     core = sec % 2
     panels, rows, _ = final.shape
     half = rows // 2
-    features = rows
+    features = rows * SPLIT
     spot = dp // 2
     side = spot // (chain // 2)
     depth = chain // 2 - 1
@@ -356,6 +355,11 @@
     def _():
         pl.semaphore_signal(barrier, inc=1, device_id=outward, device_id_type=MESH)
 
+    def when(cond, step, *args):
+        @pl.when(cond)
+        def _():
+            step(*args)
+
     def rows_at(which):
         return pl.ds(pl.multiple_of(which * half, half), half)
 
@@ -416,28 +420,52 @@
         return remote(final.at[j, rest], final.at[j, rest], f_ss.at[1, j], f_rs.at[1, j], outward)
 
     def left_of(who, j):
-        p = j - 1
+        p = (j - 1) // SPLIT
         even = p // (3 * features // PANEL) + p // (4 * features // PANEL)
         odd = 3 - p // (4 * features // PANEL)
         return who * odd + (1 - who) * even
 
-    def fetch(who, j, ring, sem):
-        cols = pl.ds(pl.multiple_of((j - 1) * PANEL, PANEL), PANEL)
-        return pltpu.make_async_copy(rights.at[who, :, cols], ring.at[j % RING], sem.at[j % RING])
+    wide = rights.shape[2] // PANEL
+
+    def strip(j):
+        return pl.ds(pl.multiple_of((j - 1) % SPLIT * rows, rows), rows)
+
+    class Fetch:
+        def __init__(self, who, j, ring, sem):
+            self.who, self.p, self.slot, self.sem = who, (j - 1) // SPLIT, ring.at[j % RING], sem.at[j % RING]
+
+        def upper(self):
+            cols = pl.ds(pl.multiple_of(self.p * PANEL, PANEL), PANEL)
+            return pltpu.make_async_copy(rights.at[self.who, :, cols], self.slot, self.sem)
+
+        def lower(self):
+            col = self.p - wide + self.who * (wide // 2)
+            cols = pl.ds(pl.multiple_of(col * PANEL, PANEL), PANEL)
+            return pltpu.make_async_copy(a_h.at[:, cols], self.slot, self.sem)
+
+        def start(self):
+            when(self.p < wide, lambda: self.upper().start())
+            when(self.p >= wide, lambda: self.lower().start())
+
+        def wait(self):
+            when(self.p < wide, lambda: self.upper().wait())
+            when(self.p >= wide, lambda: self.lower().wait())
+
+    fetch = Fetch
 
     def to_out(j):
-        cols = pl.ds(pl.multiple_of((j - 1) * PANEL, PANEL), PANEL)
-        return pltpu.make_async_copy(final.at[j], out_h.at[:, cols], out_sem.at[j])
+        cols = pl.ds(pl.multiple_of((j - 1) // SPLIT * PANEL, PANEL), PANEL)
+        return pltpu.make_async_copy(final.at[j], out_h.at[strip(j), cols], out_sem.at[j])
 
     lefts = [pltpu.make_async_copy(h, left.at[i], left_sem.at[i]) for i, h in enumerate((x_h, ctx_h, df_h, mid_h))]
     for i in (0, 3, 1, 2):
         lefts[i].start()
     for j in range(1, RING):
-        fetch(core, j, own_ring, own_sem).start()
-        fetch(1 - core, j, sib_ring, ring_sem).start()
+        fetch(core, j, own_ring, own_sem).upper().start()
+        fetch(1 - core, j, sib_ring, ring_sem).upper().start()
 
     def turn(i):
-        grid = (rows, rows)
+        grid = (features, features)
         eye = lax.broadcasted_iota(jnp.int32, grid, 0) == lax.broadcasted_iota(jnp.int32, grid, 1)
         left_t[i] = mm(eye.astype(bf16), left[i], NT).astype(bf16)
 
@@ -452,11 +480,6 @@
 
     pl.semaphore_wait(barrier, 3 + has_out.astype(jnp.int32))
 
-    def when(cond, step, *args):
-        @pl.when(cond)
-        def _():
-            step(*args)
-
     def stage_send(j):
         when(j >= RING, lambda: to_sibling(j - RING).wait_send())
 
@@ -468,7 +491,7 @@
         @pl.when(j > 0)
         def _():
             fetch(1 - core, j, sib_ring, ring_sem).wait()
-            sib_send[j % RING] = mm(left_t[left_of(1 - core, j)], sib_ring[j % RING]).astype(bf16)
+            sib_send[j % RING] = mm(left_t[left_of(1 - core, j), strip(j), :], sib_ring[j % RING]).astype(bf16)
 
         to_sibling(j).start()
         nxt = j + RING
@@ -488,7 +511,7 @@
         @pl.when(j > 0)
         def _():
             fetch(core, j, own_ring, own_sem).wait()
-            own = mm(left_t[left_of(core, j)], own_ring[j % RING])
+            own = mm(left_t[left_of(core, j), strip(j), :], own_ring[j % RING])
             part[j] = (own + sib_recv[j].astype(f32)).astype(bf16)
 
         nxt = j + RING
@@ -558,7 +581,7 @@
 
         when(j > 0, lambda: to_out(j).start())
 
-    last_lag = 4 + 2 * depth
+    last_lag = 7 + 4 * depth
 
     def step(t, carry):
         def at(lag, kind, cond, run):
@@ -570,21 +593,21 @@
                 ok = ok & cond
             when(ok, run, j)
 
-        at(4 + depth + dist, 1, dist > 0, two_spread_rest)
-        at(3 + depth + dist, 1, dist > 0, two_spread_kept)
-        at(3 + depth + dist, 0, dist > 0, one_spread)
-        at(4 + depth, 1, inner, two_swapped)
-        at(3 + depth, 1, inner, two_total)
-        at(3 + depth, 0, inner, one_total)
-        at(2 + depth, 1, inner, two_halves)
-        at(2 + depth - dist, 0, dist < depth, one_chain)
-        at(1 + depth - dist, 1, dist < depth, two_chain)
-        at(2, 0, None, one_halves)
+        at(last_lag, 1, dist > 0, two_spread_rest) if depth == 0 else at(7 + 2 * (depth + dist), 1, dist > 0, two_spread_rest)
+        at(5 + 2 * (depth + dist), 1, dist > 0, two_spread_kept)
+        at(5 + 2 * (depth + dist), 0, dist > 0, one_spread)
+        at(7 + 2 * depth, 1, inner, two_swapped)
+        at(5 + 2 * depth, 1, inner, two_total)
+        at(5 + 2 * depth, 0, inner, one_total)
+        at(3 + 2 * depth, 1, inner, two_halves)
+        at(3 + 2 * (depth - dist), 0, dist < depth, one_chain)
+        at(1 + 2 * (depth - dist), 1, dist < depth, two_chain)
+        at(3, 0, None, one_halves)
         at(1, None, None, stage_part)
         at(0, None, None, stage_send)
         at(last_lag, None, None, finish)
         when(t == 0, lambda: [lefts[0].wait(), turn(0), lefts[3].wait(), turn(3)])
-        when(t == 4, lambda: [lefts[1].wait(), turn(1), lefts[2].wait(), turn(2)])
+        when(t == 4 * SPLIT, lambda: [lefts[1].wait(), turn(1), lefts[2].wait(), turn(2)])
         return carry
 
     lax.fori_loop(0, panels + last_lag, step, 0)
@@ -621,30 +644,32 @@
     lax.fori_loop(0, panels, drain, 0)
 
 
-def reduce_gradients(lefts, rights, dnorm, chain):
+def reduce_gradients(lefts, rights, acts, dnorm, chain):
     rows = lefts[0].shape[0]
     features = lefts[0].shape[1]
-    panels = rights.shape[2] // PANEL + 1
+    width = rights.shape[2] + acts.shape[1] // 2
+    panels = SPLIT * width // PANEL + 1
+    unit = features // SPLIT
     evens, odds = (panels + 1) // 2, panels // 2
     any_ = pl.BlockSpec(memory_space=pl.ANY)
     vm = pl.BlockSpec(memory_space=pltpu.VMEM)
     V = lambda *s: pltpu.VMEM(s, bf16)
     D = lambda *s: pltpu.SemaphoreType.DMA(s)
-    h = features // 2
+    h = unit // 2
     return pl.pallas_call(
         functools.partial(reduce_kernel, chain),
         out_shape=[
-            jax.ShapeDtypeStruct((features, rights.shape[2]), bf16),
+            jax.ShapeDtypeStruct((features, width), bf16),
             jax.ShapeDtypeStruct((16, PANEL), f32),
         ],
-        in_specs=[any_] * 5 + [vm],
+        in_specs=[any_] * 6 + [vm],
         out_specs=[any_, vm],
         scratch_shapes=[
             V(4, rows, features), V(4, features, rows), V(RING, rows, PANEL), V(RING, rows, PANEL),
-            V(RING, features, PANEL), V(panels, features, PANEL), V(panels, features, PANEL),
+            V(RING, unit, PANEL), V(panels, unit, PANEL), V(panels, unit, PANEL),
             V(evens, h, PANEL), V(evens, h, PANEL), V(evens, h, PANEL), V(evens, h, PANEL),
-            V(odds, features, PANEL), V(odds, h, PANEL), V(odds, h, PANEL), V(odds, h, PANEL),
-            V(panels, features, PANEL),
+            V(odds, unit, PANEL), V(odds, h, PANEL), V(odds, h, PANEL), V(odds, h, PANEL),
+            V(panels, unit, PANEL),
             D(4), D(RING), D(RING), D(panels), D(RING), D(panels), D(evens), D(evens), D(evens), D(evens), D(evens), D(evens),
             D(odds), D(odds), D(odds), D(odds), D(odds), D(odds), D(3, panels), D(2, panels),
         ],
@@ -652,7 +677,7 @@
             vmem_limit_bytes=60 << 20, collective_id=1, has_side_effects=True
         ),
         name="reduce_gradients",
-    )(*lefts, rights, dnorm)
+    )(*lefts, rights, acts, dnorm)
 
 
 def row_tables(lengths, core):
@@ -725,7 +750,7 @@
     grads = backward(upstream, norms, pick, saved, first2, second2)
     dx, y_ffn = grads["dx"], saved["y"]
     lefts = (inputs, saved["ctx"], grads["df"], saved["mid"])
-    total, norm_total = reduce_gradients(lefts, grads["rights"], grads["dnorm"], lax.axis_size("dp") // 2)
+    total, norm_total = reduce_gradients(lefts, grads["rights"], saved["a"], grads["dnorm"], lax.axis_size("dp") // 2)
     ff = first_weights.shape[2]
     norm_total = norm_total.reshape(-1)[: 2 * features].reshape(2, features)
 

time: 678 us -> 394 us (0.58)
  Pallas kernels: 571 us -> 287 us
    pallas_call x2, Pallas kernels: 293 us -> 66.8 us  [backward(): pl.pallas_call(backward_kernel, out_shape=list(shapes.values()), in_specs...]
    pallas_call x1, Pallas kernels: 208 us -> 150 us  [reduce_gradients(): pl.pallas_call(functools.partial(reduce_kernel, chain), out_shape=[jax.Sh...]
  transfers between devices with their start and end apart: 10 -> 10, of which waited for: 3 -> 3; matrix products, arithmetic and copies ran while one was open for 4% -> 7% of each run, Pallas kernels for 36% -> 48%
where the time goes in v4:
time: 394 us; the launch traced here: 388 us
  Pallas kernels  287 us (73%)
  waiting for transfers between devices  23.3 us (6%)
  other arithmetic  20.4 us (5%)
  starting transfers between devices  16.6 us (4%)
  between operations  14.7 us (4%)
  matrix products  11.9 us (3%)
  local copies, waits for them, and re-layouts  8.05 us (2%)
  blocking collectives  5.78 us (1%)
    pallas_call x1, Pallas kernels, reduce_gradients(): pl.pallas_call(functools.partial(reduce_kernel, chain), out_shape=[jax.Sh...  150 us
    pallas_call x2, Pallas kernels, forward(): pl.pallas_call(forward_kernel, out_shape=list(shapes.values()), in_specs=...  70.4 us
    pallas_call x2, Pallas kernels, backward(): pl.pallas_call(backward_kernel, out_shape=list(shapes.values()), in_specs...  66.8 us
    all_gather x2, waiting for transfers between devices, both(): return lax.all_gather(block, 'section', axis_index_groups=pairs)  16.2 us
  transfers between devices with their start and end apart: 10, of which 3 were waited for; matrix products, arithmetic and copies ran while one was open for 7% of the time, Pallas kernels for 48%

profile of v4, /device:TPU:0, one launch (start us, length us, event | category | flops | bytes accessed | tf_op | source)
XLA Modules:
  0.0 387.6 jit_solution(3967080653162136047)
XLA Ops:
  10.0 1.4 fusion.2
  12.9 2.4 collective-permute-start
  15.3 1.7 collective-permute-start.3
  19.1 1.4 fusion.15
  21.0 1.4 reshape.83
  22.4 5.8 %all-gather.1 = f32[2,2,768]{2,1,0:T(2,128)} all-gather(f32[1,2,768]{2,1,0:T(2,128)S(1)} %maximum_bitcast_fusion), channel_id=2, replica_groups={{0,8},{16,24},{1,9},{17,25},{2,10},{18,26},{3,11},{19,27},{4,12},{20,28..., dimensions={0}, use_global_device_ids=true | all-gather | bytes 18432 | tf_op jit(solution)/shard_map/all_gather | solution.py:725
  33.7 1.5 select_select_fusion.3.x.dy
  35.2 16.2 %all-gather.5.cloned.1.call-done.first_h = bf16[2,768,3072]{2,1,0:T(8,128)(2,1)} async-done(((bf16[1,768,3072]{2,1,0:T(8,128)(2,1)}), bf16[2,768,3072]{2,1,0:T(8,128)(2,1)}) %all-gather.5.cloned.1.call-update) | async-done | bytes 9437200 | tf_op jit(solution)/shard_map/all_gather | solution.py:725
  51.3 35.3 %layer_forward.2 = (bf16[768,768]{1,0:T(8,128)(2,1)}, bf16[16,768]{1,0:T(8,128)(2,1)}, bf16[768,2304]{1,0:T(8,128)(2,1)}, bf16[3,6,256,512]{3,2,1,0:T(8,128)(2,1...) custom-call(bf16[768,768]{1,0:T(8,128)(2,1)} %select_select_fusion.3, ...), custom_call_target="tpu_custom_call" | custom-call | tf_op jit(solution)/shard_map/layer_forward/pallas_call | solution.py:153
  86.7 4.2 %collective-permute-start.1 = (bf16[16,768]{1,0:T(8,128)(2,1)}, bf16[16,768]{1,0:T(8,128)(2,1)}, u32[]{:S(2)}, u32[]{:S(2)}) collective-permute-start(bf16[16,768]{1,0:T(8,128)(2,1)} %get-tuple-element.24), channel_id=1, source_target_pairs={{0,16},{8,24},{1,17},{9,25},{2,18},{10,26},{3,19},{11,27},{4,20},{... | collective-permute-start | bytes 73736 | tf_op jit(solution)/shard_map/ppermute | solution.py:742
  92.0 3.1 fusion.7.x.x_h
  95.1 35.1 %layer_forward.3 = (bf16[768,768]{1,0:T(8,128)(2,1)}, bf16[16,768]{1,0:T(8,128)(2,1)}, bf16[768,2304]{1,0:T(8,128)(2,1)}, bf16[3,6,256,512]{3,2,1,0:T(8,128)(2,1...) custom-call(bf16[768,768]{1,0:T(8,128)(2,1)} %fusion.7.x.x_h, ...), custom_call_target="tpu_custom_call" | custom-call | tf_op jit(solution)/shard_map/layer_forward/pallas_call | solution.py:153
  130.2 33.4 %layer_backward.2 = (bf16[768,768]{1,0:T(8,128)(2,1)}, f32[16,768]{1,0:T(8,128)}, bf16[768,768]{1,0:T(8,128)(2,1)}, bf16[2,768,3072]{2,1,0:T(8,128)(2,1)}, f32[4,768]{1,0:T(4,128)}) custom-call(bf16[768,768]{1,0:T(8,128)(2,1)} %select_select_fusion.3.x.dy, f32[4,768]{1,0:T(4,128)} %reshape.94.norms, bf16[16,768]{1,0:T(8,128)(2,1)} %fusion.8.pick, ...), custom_call_target="tpu_custom_call" | custom-call | tf_op jit(solution)/shard_map/layer_backward/pallas_call | solution.py:301
  163.6 1.5 collective-permute-start.4
  165.1 4.7 %collective-permute-done.4 = f32[16,768]{1,0:T(8,128)S(1)} collective-permute-done((f32[16,768]{1,0:T(8,128)}, f32[16,768]{1,0:T(8,128)S(1)}, u32[]{:S(2)}, u32[]{:S(2)}) %collective-permute-start.4) | collective-permute-done | bytes 49184 | tf_op jit(solution)/shard_map/ppermute | solution.py:747
  169.8 3.8 fusion.6.dy
  173.6 33.4 %layer_backward.3 = (bf16[768,768]{1,0:T(8,128)(2,1)}, f32[16,768]{1,0:T(8,128)}, bf16[768,768]{1,0:T(8,128)(2,1)}, bf16[2,768,3072]{2,1,0:T(8,128)(2,1)}, f32[4,768]{1,0:T(4,128)}) custom-call(bf16[768,768]{1,0:T(8,128)(2,1)} %fusion.6.dy, f32[4,768]{1,0:T(4,128)} %reshape.94.norms, bf16[16,768]{1,0:T(8,128)(2,1)} %fusion.8.pick, ...), custom_call_target="tpu_custom_call" | custom-call | tf_op jit(solution)/shard_map/layer_backward/pallas_call | solution.py:301
  207.1 1.6 select_select_fusion.2
  209.4 3.3 collective-permute-start.6
  212.8 149.6 %reduce_gradients.1 = (bf16[768,4608]{1,0:T(8,128)(2,1)}, f32[16,128]{1,0:T(8,128)}) custom-call(bf16[768,768]{1,0:T(8,128)(2,1)} %fusion.7.x.x_h, bf16[768,768]{1,0:T(8,128)(2,1)} %get-tuple-element.35.ctx_h, bf16[768,768]{1,0:T(8,128)(2,1)} %get-tuple-element.36.df_h, bf16[768,768]{1,0:T(8,128)(2,1)} %get-tuple-element.37.mid_h, ...), custom_call_target="tpu_custom_call" | custom-call | tf_op jit(solution)/shard_map/reduce_gradients/pallas_call | solution.py:659
  364.4 4.6 %bitcast_convert_fusion.1 = f32[1,768,1536]{2,1,0:T(8,128)} fusion(bf16[768,4608]{1,0:T(8,128)(2,1)} %get-tuple-element.41), kind=kLoop, calls=%fused_computation.5 | loop fusion | flops 1179648 | bytes 7077888 | tf_op jit(solution)/shard_map/convert_element_type | solution.py:770
  369.6 5.0 %bitcast_convert_fusion = f32[1,768,3072]{2,1,0:T(8,128)} fusion(bf16[768,4608]{1,0:T(8,128)(2,1)S(1)} %copy-done.4), kind=kLoop, calls=%fused_computation | loop fusion | flops 2359296 | bytes 14155776 | tf_op jit(solution)/shard_map/convert_element_type | solution.py:770
  374.7 1.7 select_select_fusion.1
  376.7 3.6 fusion
  (59 shorter events, 17.2 us)
Async XLA Ops:
  7.2 2.9 copy-start
  7.2 28.0 %all-gather.7.cloned.1.call-start = ((), (), s32[]{:S(2)}) async-start(), calls=%async_computation.1 | async-start | bytes 7077888 | tf_op jit(solution)/shard_map/all_gather | solution.py:725
  7.9 0.8 copy-start.7
  7.9 43.4 %all-gather.5.cloned.1.call-start = ((), (), s32[]{:S(2)}) async-start(), calls=%async_computation | async-start | bytes 14155776 | tf_op jit(solution)/shard_map/all_gather | solution.py:725
  8.8 0.7 copy-start.6
  9.5 0.5 copy-start.8
  12.9 20.8 %collective-permute-start = (bf16[768,768]{1,0:T(8,128)(2,1)}, bf16[768,768]{1,0:T(8,128)(2,1)S(1)}, u32[]{:S(2)}, u32[]{:S(2)}) collective-permute-start(bf16[768,768]{1,0:T(8,128)(2,1)} %broadcast_select_fusion.2), channel_id=1, source_target_pairs={{0,8},{24,16},{1,9},{25,17},{2,10},{26,18},{3,11},{27,19},{4,12},{... | collective-permute-start | bytes 3538952 | tf_op jit(solution)/shard_map/ppermute | solution.py:718
  15.3 75.6 %collective-permute-start.3 = (bf16[768,768]{1,0:T(8,128)(2,1)S(1)}, bf16[768,768]{1,0:T(8,128)(2,1)}, u32[]{:S(2)}, u32[]{:S(2)}) collective-permute-start(bf16[768,768]{1,0:T(8,128)(2,1)S(1)} %bitcast.45), channel_id=1, source_target_pairs={{8,24},{16,8},{9,25},{17,9},{10,26},{18,10},{11,27},{19,11},{12,28... | collective-permute-start | bytes 3538952 | tf_op jit(solution)/shard_map/ppermute | solution.py:720
  17.0 73.9 %collective-permute-start.2 = (bf16[768,768]{1,0:T(8,128)(2,1)S(1)}, bf16[768,768]{1,0:T(8,128)(2,1)}, u32[]{:S(2)}, u32[]{:S(2)}) collective-permute-start(bf16[768,768]{1,0:T(8,128)(2,1)S(1)} %bitcast.44), channel_id=1, source_target_pairs={{8,16},{16,0},{9,17},{17,1},{10,18},{18,2},{11,19},{19,3},{12,20},... | collective-permute-start | bytes 3538952 | tf_op jit(solution)/shard_map/ppermute | solution.py:719
  32.5 0.5 copy-start.9
  51.3 40.7 %copy-start.2 = (bf16[768,768]{1,0:T(8,128)(2,1)S(1)}, bf16[768,768]{1,0:T(8,128)(2,1)}, u32[]{:S(2)}) copy-start(bf16[768,768]{1,0:T(8,128)(2,1)} %select_select_fusion.3.x.dy) | copy-start | bytes 3538948
  86.7 5.4 %collective-permute-start.1 = (bf16[16,768]{1,0:T(8,128)(2,1)}, bf16[16,768]{1,0:T(8,128)(2,1)}, u32[]{:S(2)}, u32[]{:S(2)}) collective-permute-start(bf16[16,768]{1,0:T(8,128)(2,1)} %get-tuple-element.24), channel_id=1, source_target_pairs={{0,16},{8,24},{1,17},{9,25},{2,18},{10,26},{3,19},{11,27},{4,20},{... | collective-permute-start | bytes 73736 | tf_op jit(solution)/shard_map/ppermute | solution.py:742
  130.2 39.6 %copy-start.3 = (bf16[768,768]{1,0:T(8,128)(2,1)S(1)}, bf16[768,768]{1,0:T(8,128)(2,1)}, u32[]{:S(2)}) copy-start(bf16[768,768]{1,0:T(8,128)(2,1)} %select_select_fusion.3.x.dy) | copy-start | bytes 3538948
  130.2 39.6 %copy-start.10 = (s32[16]{0:T(128)S(1)}, s32[16]{0:T(128)}, u32[]{:S(2)}) copy-start(s32[16]{0:T(128)} %copy-done.9) | copy-start | bytes 196
  163.6 6.2 %collective-permute-start.4 = (f32[16,768]{1,0:T(8,128)}, f32[16,768]{1,0:T(8,128)S(1)}, u32[]{:S(2)}, u32[]{:S(2)}) collective-permute-start(f32[16,768]{1,0:T(8,128)} %get-tuple-element.33), channel_id=1, source_target_pairs={{16,0},{24,8},{17,1},{25,9},{18,2},{26,10},{19,3},{27,11},{20,4},{... | collective-permute-start | bytes 147464 | tf_op jit(solution)/shard_map/ppermute | solution.py:747
  173.6 33.4 %copy-start.5 = (bf16[768,768]{1,0:T(8,128)(2,1)S(1)}, bf16[768,768]{1,0:T(8,128)(2,1)}, u32[]{:S(2)}) copy-start(bf16[768,768]{1,0:T(8,128)(2,1)} %get-tuple-element.25) | copy-start | bytes 3538948
  208.7 166.0 %collective-permute-start.7 = (bf16[768,768]{1,0:T(8,128)(2,1)S(1)}, bf16[768,768]{1,0:T(8,128)(2,1)S(1)}, u32[]{:S(2)}, u32[]{:S(2)}) collective-permute-start(bf16[768,768]{1,0:T(8,128)(2,1)S(1)} %get-tuple-element.47), channel_id=1, source_target_pairs={{8,16},{24,8},{9,17},{25,9},{10,18},{26,10},{11,19},{27,11},{12,20... | collective-permute-start | bytes 3538952 | tf_op jit(solution)/shard_map/ppermute | solution.py:760
  209.4 165.3 %collective-permute-start.6 = (bf16[768,768]{1,0:T(8,128)(2,1)S(1)}, bf16[768,768]{1,0:T(8,128)(2,1)}, u32[]{:S(2)}, u32[]{:S(2)}) collective-permute-start(bf16[768,768]{1,0:T(8,128)(2,1)S(1)} %get-tuple-element.47), channel_id=1, source_target_pairs={{0,16},{16,8},{1,17},{17,9},{2,18},{18,10},{3,19},{19,11},{4,20},{... | collective-permute-start | bytes 3538952 | tf_op jit(solution)/shard_map/ppermute | solution.py:759
  363.1 11.6 %collective-permute-start.5 = (bf16[768,768]{1,0:T(8,128)(2,1)S(1)}, bf16[768,768]{1,0:T(8,128)(2,1)S(1)}, u32[]{:S(2)}, u32[]{:S(2)}) collective-permute-start(bf16[768,768]{1,0:T(8,128)(2,1)S(1)} %get-tuple-element.48), channel_id=1, source_target_pairs={{8,0},{16,24},{9,1},{17,25},{10,2},{18,26},{11,3},{19,27},{12,4},{... | collective-permute-start | bytes 3538952 | tf_op jit(solution)/shard_map/ppermute | solution.py:762
  364.4 5.2 %copy-start.4 = (bf16[768,4608]{1,0:T(8,128)(2,1)S(1)}, bf16[768,4608]{1,0:T(8,128)(2,1)}, u32[]{:S(2)}) copy-start(bf16[768,4608]{1,0:T(8,128)(2,1)} %get-tuple-element.41) | copy-start | bytes 21233668
  376.7 3.6 copy-start.1
Sparse Core Ops, SparseCore 0:
  9.6 17.1 all-gather.6
  28.3 23.0 all-gather.4

commit v5 on v4

v5 whole, which is shorter than its diff:
```python
import functools

import jax
import jax.numpy as jnp
from jax import lax
from jax.experimental import pallas as pl
from jax.experimental.pallas import tpu as pltpu
from jax.sharding import PartitionSpec as P

HEAD_DIM = 64
PAIR = 2 * HEAD_DIM
BLOCK = 256
SEQ = 512
LEADS = 16
VMEM_LIMIT = 60 << 20
MESH = pl.DeviceIdType.MESH
f32 = jnp.float32
bf16 = jnp.bfloat16
epsilon = 1e-12
NN = (((1,), (0,)), ((), ()))
NT = (((1,), (1,)), ((), ()))
TN = (((0,), (0,)), ((), ()))
LOG2E = 1.4426950408889634


def mm(a, b, dims=NN):
    return lax.dot_general(a, b, dims, preferred_element_type=f32)


def when(cond, step, *args):
    @pl.when(cond)
    def _():
        step(*args)


def remote(src, dst, ss, rs, target):
    return pltpu.make_async_remote_copy(
        src_ref=src, dst_ref=dst, send_sem=ss, recv_sem=rs, device_id=target, device_id_type=MESH
    )


def gelu_and_slope(u):
    bell = jnp.exp2(u * u * (-0.5 * LOG2E))
    t = 1.0 / (1.0 + (0.3275911 * 0.5**0.5) * jnp.abs(u))
    poly = t * (0.127414796 + t * (-0.142248368 + t * (0.7107068705 + t * (-0.7265760135 + t * 0.5307027145))))
    tail = poly * bell
    cdf = jnp.where(u < 0, tail, 1.0 - tail)
    return u * cdf, cdf + u * bell * 0.3989422804014327


def normalize(z):
    centered = z - jnp.mean(z, axis=-1, keepdims=True)
    rstd = lax.rsqrt(jnp.mean(centered * centered, axis=-1, keepdims=True) + epsilon)
    return centered * rstd, rstd


def normalize_back(zh, rstd, gain, dy):
    g = dy * gain
    mean_g = jnp.mean(g, axis=-1, keepdims=True)
    mean_gz = jnp.mean(g * zh, axis=-1, keepdims=True)
    dz = rstd * (g - mean_g - zh * mean_gz)
    return dz, jnp.sum(dy * zh, axis=0, keepdims=True), jnp.sum(dy, axis=0, keepdims=True)


def span_scalars(lengths, row):
    ends, starts, first, total = [], [], 0, 0
    for j in range(lengths.shape[1]):
        size = lengths[row, j]
        starts.append(total)
        first = first + jnp.where(size == BLOCK, total, 0)
        total = total + size
        ends.append(total)
    return ends, starts, first


def places(first, core, shape, axis):
    at = lax.broadcasted_iota(jnp.int32, shape, axis) + (first + core * BLOCK)
    return jnp.where(at >= SEQ, at - SEQ, at)


def mask_bias(lengths, row, core):
    ends, _, first = span_scalars(lengths, row)

    def segment(at):
        return sum((at >= end).astype(jnp.int32) for end in ends)

    rows = segment(places(first, core, (BLOCK, BLOCK), 0))
    cols = segment(places(first, core, (BLOCK, BLOCK), 1))
    return jnp.where(rows == cols, 0.0, -1e30)


def lead_picks(lengths, core, by_rows):
    parts = []
    per_row = lengths.shape[1] - 1
    shape = (BLOCK, LEADS) if by_rows else (LEADS, BLOCK)
    for row in range(lengths.shape[0]):
        _, starts, first = span_scalars(lengths, row)
        at = places(first, core, shape, 0 if by_rows else 1)
        slot = lax.broadcasted_iota(jnp.int32, shape, 1 if by_rows else 0)
        hit = sum(
            ((slot == row * per_row + j) & (at == starts[j])).astype(jnp.int32) for j in range(per_row)
        )
        parts.append(hit.astype(f32))
    return jnp.concatenate(parts, axis=0 if by_rows else 1)


def lane_masks():
    return lax.broadcasted_iota(jnp.int32, (BLOCK, PAIR), 1) < HEAD_DIM


def forward_pass(x, lengths, core, norms, wa, wu, wd, qkv, ctx, mid, acc, ready, save):
    tokens, features = x.shape
    pairs = features // PAIR
    for c in range(3):
        ready["a"](c)
        cols = pl.ds(c * features, features)
        qkv[:, cols] = mm(x[...], wa[:, cols]).astype(bf16)
    first = lane_masks()
    zero = jnp.zeros((BLOCK, PAIR), bf16)

    def block_step(b, carry):
        rows = pl.ds(pl.multiple_of(b * BLOCK, BLOCK), BLOCK)
        bias = mask_bias(lengths, b, core)
        for h in range(pairs):
            q = qkv[rows, pl.ds(h * PAIR, PAIR)]
            k = qkv[rows, pl.ds(features + h * PAIR, PAIR)]
            v = qkv[rows, pl.ds(2 * features + h * PAIR, PAIR)]
            total = None
            for side in range(2):
                own = first if side == 0 else ~first
                s = mm(q, jnp.where(own, k, zero), NT) * (HEAD_DIM**-0.5) + bias
                e = jnp.exp(s - jnp.max(s, axis=-1, keepdims=True))
                pr = (e * (1.0 / jnp.sum(e, axis=-1, keepdims=True))).astype(bf16)
                if save:
                    save["p"][b, h, :, pl.ds(side * BLOCK, BLOCK)] = pr
                part = mm(pr, jnp.where(own, v, zero))
                total = part if total is None else total + part
            ctx[rows, pl.ds(h * PAIR, PAIR)] = total.astype(bf16)
        return carry

    lax.fori_loop(0, tokens // BLOCK, block_step, 0)
    ready["a"](3)
    zn, r = normalize(x[...].astype(f32) + mm(ctx[...], wa[:, pl.ds(3 * features, features)]))
    if save:
        save["keep"]("qkv", "p", "ctx")
        save["rstd0"][...] = r
        save["zh0"][...] = zn.astype(bf16)
    mid[...] = (zn * norms[0, 0:1, :] + norms[0, 1:2, :]).astype(bf16)
    acc[...] = mid[...].astype(f32)
    if save:
        save["keep"]("zh0", "mid")
    for c in range(wu.shape[1] // features):
        cols = pl.ds(c * features, features)
        ready["u"](c)
        act, slope = gelu_and_slope(mm(mid[...], wu[:, cols]))
        act = act.astype(bf16)
        if save:
            save["a"][:, cols] = act
            save["slope"][:, cols] = slope.astype(bf16)
            save["keep_cols"](c)
        ready["d"](c)
        acc[...] += mm(act, wd[:, cols], NT)
    zn, r = normalize(acc[...])
    if save:
        save["rstd1"][...] = r
        save["zh1"][...] = zn.astype(bf16)
    return (zn * norms[1, 0:1, :] + norms[1, 1:2, :]).astype(bf16)


def backward_pass(
    dy, norms, wa, wu, wd, qkv, p, zh0, slope, zh1, rstd0, rstd1, df, du, do, dqkv, dctx, acc, dnorm, ready, keep
):
    tokens, features = dy.shape
    pairs = features // PAIR
    ready["zh1"]()
    dz, dgain, dshift = normalize_back(zh1[...].astype(f32), rstd1[...], norms[1, 0:1, :], dy.astype(f32))
    dnorm[2:3, :] = dgain
    dnorm[3:4, :] = dshift
    df[...] = dz.astype(bf16)
    acc[...] = dz
    keep("df")
    for c in range(wu.shape[1] // features):
        cols = pl.ds(c * features, features)
        ready["d"](c)
        da = mm(df[...], wd[:, cols])
        ready["slope"](c)
        g = (da * slope[:, cols].astype(f32)).astype(bf16)
        du[:, cols] = g
        ready["u"](c)
        acc[...] += mm(g, wu[:, cols], NT)
    keep("du")
    ready["zh0"]()
    d_mid = acc[...].astype(bf16).astype(f32)
    dz, dgain, dshift = normalize_back(zh0[...].astype(f32), rstd0[...], norms[0, 0:1, :], d_mid)
    dnorm[0:1, :] = dgain
    dnorm[1:2, :] = dshift
    do[...] = dz.astype(bf16)
    acc[...] = dz
    keep("do")
    ready["a"](3)
    dctx[...] = mm(do[...], wa[:, pl.ds(3 * features, features)], NT).astype(bf16)
    ready["qkv"]()
    first = lane_masks()
    zero = jnp.zeros((BLOCK, PAIR), bf16)
    scale = HEAD_DIM**-0.5

    def block_step(b, carry):
        rows = pl.ds(pl.multiple_of(b * BLOCK, BLOCK), BLOCK)
        for h in range(pairs):
            q = qkv[rows, pl.ds(h * PAIR, PAIR)]
            k = qkv[rows, pl.ds(features + h * PAIR, PAIR)]
            v = qkv[rows, pl.ds(2 * features + h * PAIR, PAIR)]
            dc = dctx[rows, pl.ds(h * PAIR, PAIR)]
            dq = dk = dv = None
            for side in range(2):
                own = first if side == 0 else ~first
                pr = p[b, h, :, pl.ds(side * BLOCK, BLOCK)]
                prf = pr.astype(f32)
                dp = mm(dc, jnp.where(own, v, zero), NT)
                r = jnp.sum(dp * prf, axis=-1, keepdims=True)
                ds = (prf * (dp - r)).astype(bf16)
                parts = (
                    mm(ds, jnp.where(own, k, zero)),
                    mm(ds, jnp.where(own, q, zero), TN),
                    mm(pr, jnp.where(own, dc, zero), TN),
                )
                if dq is None:
                    dq, dk, dv = parts
                else:
                    dq, dk, dv = dq + parts[0], dk + parts[1], dv + parts[2]
            dqkv[rows, pl.ds(h * PAIR, PAIR)] = (dq * scale).astype(bf16)
            dqkv[rows, pl.ds(features + h * PAIR, PAIR)] = (dk * scale).astype(bf16)
            dqkv[rows, pl.ds(2 * features + h * PAIR, PAIR)] = dv.astype(bf16)
        return carry

    lax.fori_loop(0, tokens // BLOCK, block_step, 0)
    keep("dqkv")
    for c in range(3):
        cols = pl.ds(c * features, features)
        ready["a"](c)
        acc[...] += mm(dqkv[:, cols], wa[:, cols], NT)


def start_kernel(
    rows_in, lengths, first_h, second_h, norm_in,
    main_h, aux_h, other_first_h, other_second_h, norms, lead_out,
    wa, wu, wd, halves, main, aux, qkv, ctx, mid, acc, norm_pair, lead_own, lead_in,
    load, w_ss, w_rs, d_ss, d_rs, n_ss, n_rs, m_ss, m_rs, x_ss, x_rs, l_ss, l_rs, out_sem,
):
    sec = lax.axis_index("section")
    core = sec % 2
    at_head = sec // 2
    inside = (sec == 0) | (sec == 3)
    tokens, features = main.shape
    pieces = wu.shape[1] // features
    half = wd.shape[1] // 2
    even, odd = core == 0, core == 1
    sibling = {"section": sec + 1 - 2 * core}
    barrier = pltpu.get_barrier_semaphore()
    for step in range(1, 4):
        target = {"section": (sec + step) % 4}
        pl.semaphore_signal(barrier, inc=1, device_id=target, device_id_type=MESH)

    def cols(c):
        return pl.ds(c * features, features)

    def local_first(c, dst):
        return pltpu.make_async_copy(first_h.at[:, cols(c)], dst.at[:, cols(c)], load.at[c])

    def sent_first(c, dst):
        return remote(first_h.at[:, cols(c)], dst.at[:, cols(c)], w_ss.at[c], w_rs.at[c], sibling)

    def local_second(side):
        return pltpu.make_async_copy(second_h, wd.at[:, pl.ds(side * half, half)], load.at[pieces])

    def sent_second(side):
        return remote(second_h, wd.at[:, pl.ds(side * half, half)], d_ss, d_rs, sibling)

    for c in range(pieces):
        when(even, lambda: local_first(c, wa).start())
        when(odd, lambda: local_first(c, wu).start())
    when(even, lambda: local_second(0).start())
    when(odd, lambda: local_second(1).start())

    for row in range(lengths.shape[0]):
        _, _, first = span_scalars(lengths, row)
        packed = rows_in[pl.ds(row * SEQ, SEQ), :]
        for side in range(2):
            at = places(first, side, (BLOCK, SEQ), 0)
            hot = at == lax.broadcasted_iota(jnp.int32, (BLOCK, SEQ), 1)
            halves[side, pl.ds(row * BLOCK, BLOCK), :] = mm(hot.astype(f32).astype(bf16), packed).astype(bf16)
    norm_pair[core] = norm_in[...]

    sent_main = remote(halves.at[1 - core], main, m_ss, m_rs, sibling)
    sent_norm = remote(norm_pair.at[core], norm_pair.at[core], n_ss, n_rs, sibling)
    norm_from = remote(norm_pair.at[1 - core], norm_pair.at[1 - core], n_ss, n_rs, sibling)
    sent_aux = [
        remote(halves.at[side], aux, x_ss.at[side], x_rs, {"section": 4 + side - 2 * sec})
        for side in range(2)
    ]
    pl.semaphore_wait(barrier, 3)
    when(inside, lambda: sent_main.start())
    sent_norm.start()
    for c in range(pieces):
        when(even, lambda: sent_first(c, wa).start())
        when(odd, lambda: sent_first(c, wu).start())
    when(even, lambda: sent_second(0).start())
    when(odd, lambda: sent_second(1).start())
    when(~inside, lambda: [copy.start() for copy in sent_aux])

    @pl.when(inside)
    def _():
        main[...] = halves[core]

    when(~inside, lambda: sent_main.wait_recv())
    norm_from.wait_recv()
    norms[...] = norm_pair[...]

    def ready_a(c):
        when(even, lambda: local_first(c, wa).wait())
        when(odd, lambda: sent_first(c, wa).wait_recv())

    def ready_u(c):
        when(odd, lambda: local_first(c, wu).wait())
        when(even, lambda: sent_first(c, wu).wait_recv())

    def ready_d(c):
        if c == 0:
            when(even, lambda: local_second(0).wait())
            when(odd, lambda: sent_second(0).wait_recv())
        if c == pieces // 2:
            when(odd, lambda: local_second(1).wait())
            when(even, lambda: sent_second(1).wait_recv())

    ready = dict(a=ready_a, u=ready_u, d=ready_d)
    y = forward_pass(main, lengths, core, norms, wa, wu, wd, qkv, ctx, mid, acc, ready, None)
    lead_own[...] = mm(lead_picks(lengths, core, False).astype(bf16), y).astype(bf16)
    hop = remote(lead_own, lead_in, l_ss, l_rs, {"section": (sec + 2) % 4})
    when(at_head == 0, lambda: hop.start())

    def write(src, dst, i):
        return pltpu.make_async_copy(src, dst, out_sem.at[i])

    def store_pair(first_ref, side):
        write(first_ref, other_first_h, 0).start()
        write(wd.at[:, pl.ds(side * half, half)], other_second_h, 1).start()

    when(even, lambda: store_pair(wu, 1))
    when(odd, lambda: store_pair(wa, 0))
    write(main, main_h, 2).start()
    sent_aux[0].wait_recv()
    write(aux, aux_h, 3).start()

    @pl.when(at_head == 0)
    def _():
        lead_out[...] = jnp.zeros_like(lead_out)
        hop.wait_send()

    @pl.when(at_head == 1)
    def _():
        hop.wait_recv()
        lead_out[...] = lead_in[...]

    when(inside, lambda: sent_main.wait_send())
    sent_norm.wait_send()
    for c in range(pieces):
        sent_first(c, wa).wait_send()
    sent_second(0).wait_send()
    when(~inside, lambda: [copy.wait_send() for copy in sent_aux])
    write(wa, other_first_h, 0).wait()
    write(wd.at[:, pl.ds(0, half)], other_second_h, 1).wait()
    write(main, main_h, 2).wait()
    write(aux, aux_h, 3).wait()


ANY = pl.BlockSpec(memory_space=pl.ANY)
IN_VMEM = pl.BlockSpec(memory_space=pltpu.VMEM)
IN_SMEM = pl.BlockSpec(memory_space=pltpu.SMEM)
S = jax.ShapeDtypeStruct


def vm(*shape):
    return pltpu.VMEM(shape, bf16)


def dma(*shape):
    return pltpu.SemaphoreType.DMA(shape)


def params(number):
    if number is None:
        return pltpu.CompilerParams(vmem_limit_bytes=VMEM_LIMIT)
    return pltpu.CompilerParams(vmem_limit_bytes=VMEM_LIMIT, collective_id=number, has_side_effects=True)


def start(rows_in, lengths, first, second, norm_own):
    features, ff = first.shape
    tokens = rows_in.shape[0] // 2
    square = S((tokens, features), bf16)
    one = pltpu.SemaphoreType.DMA
    return pl.pallas_call(
        start_kernel,
        out_shape=[
            square, square, S(first.shape, bf16), S(second.shape, bf16), S((2, 2, features), f32),
            S((LEADS, features), bf16),
        ],
        in_specs=[IN_VMEM, IN_SMEM, ANY, ANY, IN_VMEM],
        out_specs=[ANY] * 4 + [IN_VMEM] * 2,
        scratch_shapes=[
            vm(features, ff), vm(features, ff), vm(features, ff), vm(2, tokens, features),
            vm(tokens, features), vm(tokens, features), vm(tokens, 3 * features), vm(tokens, features),
            vm(tokens, features), pltpu.VMEM((tokens, features), f32), pltpu.VMEM((2, 2, features), f32),
            vm(LEADS, features), vm(LEADS, features),
            dma(ff // features + 1), dma(ff // features), dma(ff // features), one, one, one, one, one, one,
            dma(2), one, one, one, dma(4),
        ],
        compiler_params=params(1),
        name="start_and_forward",
    )(rows_in, lengths, first, second, norm_own)


def weight_loads(core, first_h, second_h, other_first_h, other_second_h, wa, wu, wd, a_sem, u_sem, d_sem):
    features = wa.shape[0]
    half = wd.shape[1] // 2

    def cols(c):
        return pl.ds(c * features, features)

    def copy(kind, c, own):
        if kind == "a":
            return pltpu.make_async_copy((first_h if own else other_first_h).at[:, cols(c)], wa.at[:, cols(c)], a_sem.at[c])
        if kind == "u":
            return pltpu.make_async_copy((first_h if own else other_first_h).at[:, cols(c)], wu.at[:, cols(c)], u_sem.at[c])
        from_own = second_h if own else other_second_h
        in_half = c % (half // features)
        return pltpu.make_async_copy(from_own.at[:, cols(in_half)], wd.at[:, cols(c)], d_sem.at[c])

    def begin(kind, c):
        core_of = 0 if kind == "a" else 1 if kind == "u" else (c * features) // half
        when(core == core_of, lambda: copy(kind, c, True).start())
        when(core != core_of, lambda: copy(kind, c, False).start())

    def ready(kind, c):
        copy(kind, c, True).wait()

    return begin, ready


def middle_kernel(
    lengths, main, aux, lead, norms, first_h, second_h, other_first_h, other_second_h,
    x_h, y_h, qkv_h, p_h, ctx_h, zh0_h, mid_h, a_h, slope_h, zh1_h, rstd0, rstd1, lead_grads,
    wa, wu, wd, x, y, qkv, p, ctx, zh0, mid, a, slope, zh1, df, do, dctx, dqkv, acc, dnorm, lead_own, lead_in,
    a_sem, u_sem, d_sem, out_sem, col_sem, l_ss, l_rs,
):
    sec = lax.axis_index("section")
    core = sec % 2
    at_head = sec // 2
    tokens, features = main.shape
    pieces = wu.shape[1] // features
    peer = {"section": (sec + 2) % 4}
    barrier = pltpu.get_barrier_semaphore()
    pl.semaphore_signal(barrier, inc=1, device_id=peer, device_id_type=MESH)
    begin, ready_w = weight_loads(
        core, first_h, second_h, other_first_h, other_second_h, wa, wu, wd, a_sem, u_sem, d_sem
    )
    for c in range(pieces):
        begin("a", c)
    for c in range(pieces):
        begin("u", c)
        begin("d", c)
    refs = dict(
        x=(x, x_h), y=(y, y_h), qkv=(qkv, qkv_h), p=(p, p_h), ctx=(ctx, ctx_h), zh0=(zh0, zh0_h), mid=(mid, mid_h),
        zh1=(zh1, zh1_h),
    )
    order = list(refs)

    def store(name):
        return pltpu.make_async_copy(*refs[name], out_sem.at[order.index(name)])

    def store_cols(c, which):
        src, dst = ((a, a_h), (slope, slope_h))[which]
        cols = pl.ds(c * features, features)
        return pltpu.make_async_copy(src.at[:, cols], dst.at[:, cols], col_sem.at[which, c])

    def keep(*names):
        for name in names:
            store(name).start()

    picks = lead_picks(lengths, core, True)
    leading = jnp.max(picks, axis=1, keepdims=True) > 0

    @pl.when(at_head == 1)
    def _():
        x[...] = jnp.where(leading, mm(picks.astype(bf16), lead[...]).astype(bf16), aux[...])

    @pl.when(at_head == 0)
    def _():
        x[...] = main[...]

    keep("x")
    ready = dict(a=lambda c: ready_w("a", c), u=lambda c: ready_w("u", c), d=lambda c: ready_w("d", c))
    save = dict(
        p=p, a=a, slope=slope, zh0=zh0, zh1=zh1, rstd0=rstd0, rstd1=rstd1, keep=keep,
        keep_cols=lambda c: [store_cols(c, 0).start(), store_cols(c, 1).start()],
    )
    y[...] = forward_pass(x, lengths, core, norms, wa, wu, wd, qkv, ctx, mid, acc, ready, save)
    keep("zh1", "y")
    none = {k: (lambda *_: None) for k in ("a", "u", "d", "zh1", "zh0", "slope", "qkv")}
    backward_pass(
        main[...], norms, wa, wu, wd, qkv, p, zh0, slope, zh1, rstd0, rstd1, df, a, do, dqkv, dctx, acc, dnorm,
        none | dict(slope=lambda c: store_cols(c, 0).wait()), lambda name: None,
    )
    pick = lead_picks(lengths, core, False).astype(bf16)
    hi = acc[...].astype(bf16)
    lo = (acc[...] - hi.astype(f32)).astype(bf16)
    lead_own[...] = mm(pick, hi) + mm(pick, lo)
    pl.semaphore_wait(barrier, 1)
    hop = remote(lead_own, lead_in, l_ss, l_rs, peer)
    when(at_head == 1, lambda: hop.start())
    for name in order:
        store(name).wait()
    for c in range(pieces):
        store_cols(c, 1).wait()

    @pl.when(at_head == 1)
    def _():
        lead_grads[...] = jnp.zeros_like(lead_grads)
        hop.wait_send()

    @pl.when(at_head == 0)
    def _():
        hop.wait_recv()
        lead_grads[...] = lead_in[...]


def middle(lengths, main, aux, lead, norms, weights):
    tokens, features = main.shape
    ff = weights[0].shape[1]
    pieces = ff // features
    blocks, pairs = tokens // BLOCK, features // PAIR
    square = S((tokens, features), bf16)
    shapes = dict(
        x=square, y=square, qkv=S((tokens, 3 * features), bf16), p=S((blocks, pairs, BLOCK, 2 * BLOCK), bf16),
        ctx=square, zh0=square, mid=square, a=S((tokens, ff), bf16), slope=S((tokens, ff), bf16), zh1=square,
        rstd0=S((tokens, 1), f32), rstd1=S((tokens, 1), f32), lead_grads=S((LEADS, features), f32),
    )
    small = ("rstd0", "rstd1", "lead_grads")
    wide = vm(features, ff)
    outs = pl.pallas_call(
        middle_kernel,
        out_shape=list(shapes.values()),
        in_specs=[IN_SMEM] + [IN_VMEM] * 4 + [ANY] * 4,
        out_specs=[IN_VMEM if k in small else ANY for k in shapes],
        scratch_shapes=[wide, wide, wide]
        + [pltpu.VMEM(s.shape, s.dtype) for k, s in shapes.items() if k not in small]
        + [
            vm(tokens, features), vm(tokens, features), vm(tokens, features), vm(tokens, 3 * features),
            pltpu.VMEM((tokens, features), f32), pltpu.VMEM((4, features), f32),
            pltpu.VMEM((LEADS, features), f32), pltpu.VMEM((LEADS, features), f32),
            dma(pieces), dma(pieces), dma(pieces), dma(8), dma(2, pieces),
            pltpu.SemaphoreType.DMA, pltpu.SemaphoreType.DMA,
        ],
        compiler_params=params(2),
        name="forward_and_backward",
    )(lengths, main, aux, lead, norms, *weights)
    return dict(zip(shapes, outs))


def last_kernel(
    lengths, main, aux, lead_grads, norms, rstd0, rstd1, first_h, second_h, other_first_h, other_second_h,
    y_h, qkv_h, p_h, zh0_h, slope_h, zh1_h,
    own_h, across_h, df_h, rights, dnorm,
    wa, wu, wd, y, qkv, p, zh0, slope, zh1, df, du, do, dctx, dqkv, acc, own, across,
    a_sem, u_sem, d_sem, in_sem, col_sem, out_sem,
):
    sec = lax.axis_index("section")
    core = sec % 2
    at_head = sec // 2
    tokens, features = main.shape
    ff = wu.shape[1]
    pieces = ff // features
    begin, ready_w = weight_loads(
        core, first_h, second_h, other_first_h, other_second_h, wa, wu, wd, a_sem, u_sem, d_sem
    )
    loads = dict(zh1=(zh1_h, zh1), zh0=(zh0_h, zh0), qkv=(qkv_h, qkv), p=(p_h, p), y=(y_h, y))
    names = list(loads)

    def load(name):
        return pltpu.make_async_copy(*loads[name], in_sem.at[names.index(name)])

    def load_slope(c):
        cols = pl.ds(c * features, features)
        return pltpu.make_async_copy(slope_h.at[:, cols], slope.at[:, cols], col_sem.at[c])

    load("zh1").start()
    for c in range(pieces):
        begin("d", c)
        load_slope(c).start()
        begin("u", c)
    load("zh0").start()
    begin("a", pieces - 1)
    load("qkv").start()
    load("p").start()
    for c in range(pieces - 1):
        begin("a", c)
    load("y").start()
    stores = dict(
        df=(df, df_h), du=(du, rights.at[1, :, pl.ds(0, ff)]), do=(do, rights.at[0, :, pl.ds(3 * features, features)]),
        dqkv=(dqkv, rights.at[0, :, pl.ds(0, 3 * features)]), own=(own, own_h), across=(across, across_h),
    )
    order = list(stores)

    def store(name):
        return pltpu.make_async_copy(*stores[name], out_sem.at[order.index(name)])

    picks = lead_picks(lengths, core, True)
    leading = jnp.max(picks, axis=1, keepdims=True) > 0
    picks = picks.astype(bf16)

    @pl.when(at_head == 1)
    def _():
        own[...] = main[...]

    @pl.when(at_head == 0)
    def _():
        hi = lead_grads[...].astype(bf16)
        lo = (lead_grads[...] - hi.astype(f32)).astype(bf16)
        own[...] = (mm(picks, hi) + mm(picks, lo) + aux[...].astype(f32)).astype(bf16)

    ready = dict(
        a=lambda c: ready_w("a", c), u=lambda c: ready_w("u", c), d=lambda c: ready_w("d", c), slope=lambda c: load_slope(c).wait(),
        zh1=lambda: load("zh1").wait(), zh0=lambda: load("zh0").wait(), qkv=lambda: [load("qkv").wait(), load("p").wait()],
    )
    backward_pass(
        own[...], norms, wa, wu, wd, qkv, p, zh0, slope, zh1, rstd0, rstd1, df, du, do, dqkv, dctx, acc, dnorm,
        ready, lambda name: store(name).start(),
    )
    load("y").wait()
    dx = acc[...].astype(bf16)

    @pl.when(at_head == 1)
    def _():
        own[...] = y[...]
        across[...] = jnp.where(leading, jnp.zeros_like(dx), dx)

    @pl.when(at_head == 0)
    def _():
        own[...] = dx
        across[...] = y[...]

    store("own").start()
    store("across").start()
    for name in order:
        store(name).wait()


def last(lengths, main, aux, lead_grads, norms, weights, saved):
    tokens, features = main.shape
    ff = weights[0].shape[1]
    pieces = ff // features
    square = S((tokens, features), bf16)
    wide = vm(features, ff)
    held = [saved[k] for k in ("y", "qkv", "p", "zh0", "slope", "zh1")]
    return pl.pallas_call(
        last_kernel,
        out_shape=[square, square, square, S((2, tokens, ff), bf16), S((4, features), f32)],
        in_specs=[IN_SMEM] + [IN_VMEM] * 6 + [ANY] * 10,
        out_specs=[ANY] * 4 + [IN_VMEM],
        scratch_shapes=[wide, wide, wide]
        + [pltpu.VMEM(s.shape, s.dtype) for s in held]
        + [
            vm(tokens, features), vm(tokens, ff), vm(tokens, features), vm(tokens, features), vm(tokens, 3 * features),
            pltpu.VMEM((tokens, features), f32), vm(tokens, features), vm(tokens, features),
            dma(pieces), dma(pieces), dma(pieces), dma(5), dma(pieces), dma(6),
        ],
        compiler_params=params(None),
        name="last_backward",
    )(lengths, main, aux, lead_grads, norms, saved["rstd0"], saved["rstd1"], *weights, *held)


PANEL = 128
SPLIT = 1
RING = 4


def reduce_kernel(
    chain, x_h, ctx_h, df_h, mid_h, rights, a_h, own_h, across_h, dnorm, out_h, norm_out, halves_h,
    left, left_t, own_ring, sib_ring, sib_send, sib_recv, part, y1, c1, zin1, mid1, zin2, mid2, d2, y2, final, halves,
    left_sem, own_sem, ring_sem, out_sem, sib_ss, sib_rs, y1_ss, y1_rs, z1_ss, z1_rs, m1_ss, m1_rs,
    z2_ss, z2_rs, m2_ss, m2_rs, y2_ss, y2_rs, f_ss, f_rs, o_ss, o_rs, c_ss, c_rs, h_sem,
):
    sec = lax.axis_index("section")
    dp = lax.axis_index("dp")
    core = sec % 2
    panels, rows, _ = final.shape
    half = rows // 2
    features = rows * SPLIT
    spot = dp // 2
    side = spot // (chain // 2)
    depth = chain // 2 - 1
    dist = side * (spot - chain // 2) + (1 - side) * (chain // 2 - 1 - spot)
    inner = dist == 0
    y = dp % 2
    sibling = {"section": sec + 1 - 2 * core}
    across_y = {"dp": dp + 1 - 2 * y}
    inward = {"dp": dp + 2 - 4 * side}
    outward = {"dp": dp - 2 + 4 * side}
    has_out = dist < depth

    barrier = pltpu.get_barrier_semaphore()
    inside = (sec == 0) | (sec == 3)
    beyond = {"section": 2 - sec // 2}
    others = [{"section": (sec + step) % 4} for step in (1, 2, 3)]
    for target in (*others, across_y, inward):
        pl.semaphore_signal(barrier, inc=1, device_id=target, device_id_type=MESH)

    @pl.when(has_out)
    def _():
        pl.semaphore_signal(barrier, inc=1, device_id=outward, device_id_type=MESH)

    def rows_at(which):
        return pl.ds(pl.multiple_of(which * half, half), half)

    mine, theirs = rows_at(y), rows_at(1 - y)
    kept, rest = rows_at(side), rows_at(1 - side)

    def to_sibling(j):
        return remote(sib_send.at[j % RING], sib_recv.at[j], sib_ss.at[j % RING], sib_rs.at[j], sibling)

    def one_y(j):
        i = j // 2
        return remote(part.at[j, theirs], y1.at[i], y1_ss.at[i], y1_rs.at[i], across_y)

    def one_in(j):
        i = j // 2
        return remote(c1.at[i], zin1.at[i], z1_ss.at[i], z1_rs.at[i], inward)

    def one_mid(j):
        i = j // 2
        return remote(c1.at[i], mid1.at[i], m1_ss.at[i], m1_rs.at[i], inward)

    def one_out(j):
        return remote(final.at[j, mine], final.at[j, mine], f_ss.at[0, j], f_rs.at[0, j], outward)

    def one_back(j):
        return remote(final.at[j, mine], final.at[j, mine], f_ss.at[1, j], f_rs.at[1, j], across_y)

    def one_back_in(j):
        return remote(final.at[j, theirs], final.at[j, theirs], f_ss.at[1, j], f_rs.at[1, j], across_y)

    def two_in(j):
        i = j // 2
        return remote(part.at[j], zin2.at[i], z2_ss.at[i], z2_rs.at[i], inward)

    def two_mid(j):
        i = j // 2
        return remote(part.at[j, rest], mid2.at[i], m2_ss.at[i], m2_rs.at[i], inward)

    def two_y(j):
        i = j // 2
        return remote(d2.at[i], y2.at[i], y2_ss.at[i], y2_rs.at[i], across_y)

    def two_swap(j):
        return remote(final.at[j, kept], final.at[j, kept], f_ss.at[2, j], f_rs.at[1, j], inward)

    def two_swap_in(j):
        return remote(final.at[j, rest], final.at[j, rest], f_ss.at[2, j], f_rs.at[1, j], inward)

    def two_out_kept(j):
        return remote(final.at[j, kept], final.at[j, kept], f_ss.at[0, j], f_rs.at[0, j], outward)

    def two_out_rest(j):
        return remote(final.at[j, rest], final.at[j, rest], f_ss.at[1, j], f_rs.at[1, j], outward)

    def left_of(who, j):
        p = (j - 1) // SPLIT
        even = p // (3 * features // PANEL) + p // (4 * features // PANEL)
        odd = 3 - p // (4 * features // PANEL)
        return who * odd + (1 - who) * even

    wide = rights.shape[2] // PANEL

    def strip(j):
        return pl.ds(pl.multiple_of((j - 1) % SPLIT * rows, rows), rows)

    class Fetch:
        def __init__(self, who, j, ring, sem):
            self.who, self.p, self.slot, self.sem = who, (j - 1) // SPLIT, ring.at[j % RING], sem.at[j % RING]

        def upper(self):
            cols = pl.ds(pl.multiple_of(self.p * PANEL, PANEL), PANEL)
            return pltpu.make_async_copy(rights.at[self.who, :, cols], self.slot, self.sem)

        def lower(self):
            col = self.p - wide + self.who * (wide // 2)
            cols = pl.ds(pl.multiple_of(col * PANEL, PANEL), PANEL)
            return pltpu.make_async_copy(a_h.at[:, cols], self.slot, self.sem)

        def start(self):
            when(self.p < wide, lambda: self.upper().start())
            when(self.p >= wide, lambda: self.lower().start())

        def wait(self):
            when(self.p < wide, lambda: self.upper().wait())
            when(self.p >= wide, lambda: self.lower().wait())

    fetch = Fetch

    def to_out(j):
        cols = pl.ds(pl.multiple_of((j - 1) // SPLIT * PANEL, PANEL), PANEL)
        return pltpu.make_async_copy(final.at[j], out_h.at[strip(j), cols], out_sem.at[j])

    own_copy = pltpu.make_async_copy(own_h, halves.at[core], h_sem.at[0])
    own_send = remote(own_h, halves.at[core], o_ss, o_rs, sibling)
    own_from = remote(own_h, halves.at[1 - core], o_ss, o_rs, sibling)
    across_send = remote(across_h, halves.at[core], c_ss, c_rs.at[core], beyond)
    across_from = [remote(across_h, halves.at[side], c_ss, c_rs.at[side], beyond) for side in range(2)]
    lefts = [pltpu.make_async_copy(h, left.at[i], left_sem.at[i]) for i, h in enumerate((x_h, ctx_h, df_h, mid_h))]
    for i in (0, 3, 1, 2):
        lefts[i].start()
    for j in range(1, RING):
        fetch(core, j, own_ring, own_sem).upper().start()
        fetch(1 - core, j, sib_ring, ring_sem).upper().start()

    def turn(i):
        grid = (features, features)
        eye = lax.broadcasted_iota(jnp.int32, grid, 0) == lax.broadcasted_iota(jnp.int32, grid, 1)
        left_t[i] = mm(eye.astype(bf16), left[i], NT).astype(bf16)

    def norm_panel(other):
        chosen = jnp.where(core == other, dnorm[2:4, :], dnorm[0:2, :])
        strips = [
            chosen[r : r + 1, c * PANEL : (c + 1) * PANEL]
            for r in range(2)
            for c in range(features // PANEL)
        ]
        return jnp.concatenate(strips + [jnp.zeros((16 - len(strips), PANEL), f32)], axis=0)

    pl.semaphore_wait(barrier, 5 + has_out.astype(jnp.int32))
    when(inside, lambda: own_copy.start())
    when(~inside, lambda: own_send.start())
    across_send.start()

    def stage_send(j):
        when(j >= RING, lambda: to_sibling(j - RING).wait_send())

        @pl.when(j == 0)
        def _():
            sib_send[0] = jnp.zeros((rows, PANEL), bf16)
            sib_send[0, 0:16, :] = norm_panel(0).astype(bf16)

        @pl.when(j > 0)
        def _():
            fetch(1 - core, j, sib_ring, ring_sem).wait()
            sib_send[j % RING] = mm(left_t[left_of(1 - core, j), strip(j), :], sib_ring[j % RING]).astype(bf16)

        to_sibling(j).start()
        nxt = j + RING
        when(
            (j >= 0) & (nxt < panels),
            lambda: fetch(1 - core, nxt, sib_ring, ring_sem).start(),
        )

    def stage_part(j):
        to_sibling(j).wait_recv()

        @pl.when(j == 0)
        def _():
            part[0] = jnp.zeros((rows, PANEL), bf16)
            part[0, 0:16, :] = (norm_panel(1) + sib_recv[0, 0:16, :].astype(f32)).astype(bf16)

        @pl.when(j > 0)
        def _():
            fetch(core, j, own_ring, own_sem).wait()
            own = mm(left_t[left_of(core, j), strip(j), :], own_ring[j % RING])
            part[j] = (own + sib_recv[j].astype(f32)).astype(bf16)

        nxt = j + RING
        when((nxt < panels), lambda: fetch(core, nxt, own_ring, own_sem).start())
        when(j % 2 == 0, lambda: one_y(j).start())
        when((j % 2 == 1) & (dist == depth) & (depth > 0), lambda: two_in(j).start())
        when((j % 2 == 1) & (dist == depth) & (depth == 0), lambda: two_mid(j).start())

    def one_halves(j):
        one_y(j).wait_recv()
        c1[j // 2] = (part[j, mine, :].astype(f32) + y1[j // 2].astype(f32)).astype(bf16)
        when((dist == depth) & (dist > 0), lambda: one_in(j).start())
        when((dist == depth) & inner, lambda: one_mid(j).start())

    def one_chain(j):
        one_in(j).wait_recv()
        c1[j // 2] = (c1[j // 2].astype(f32) + zin1[j // 2].astype(f32)).astype(bf16)
        when(dist > 0, lambda: one_in(j).start())
        when(inner, lambda: one_mid(j).start())

    def one_total(j):
        one_mid(j).wait_recv()
        final[j, mine, :] = (c1[j // 2].astype(f32) + mid1[j // 2].astype(f32)).astype(bf16)
        when(has_out, lambda: one_out(j).start())
        one_back(j).start()

    def one_spread(j):
        one_out(j).wait_recv()
        when(has_out, lambda: one_out(j).start())
        one_back(j).start()

    def two_chain(j):
        two_in(j).wait_recv()
        part[j] = (part[j].astype(f32) + zin2[j // 2].astype(f32)).astype(bf16)
        when(dist > 0, lambda: two_in(j).start())
        when(inner, lambda: two_mid(j).start())

    def two_halves(j):
        two_mid(j).wait_recv()
        d2[j // 2] = (part[j, kept, :].astype(f32) + mid2[j // 2].astype(f32)).astype(bf16)
        two_y(j).start()

    def two_total(j):
        two_y(j).wait_recv()
        final[j, kept, :] = (d2[j // 2].astype(f32) + y2[j // 2].astype(f32)).astype(bf16)
        two_swap(j).start()
        when(has_out, lambda: two_out_kept(j).start())

    def two_swapped(j):
        two_swap_in(j).wait_recv()
        when(has_out, lambda: two_out_rest(j).start())

    def two_spread_kept(j):
        two_out_kept(j).wait_recv()
        when(has_out, lambda: two_out_kept(j).start())

    def two_spread_rest(j):
        two_out_rest(j).wait_recv()
        when(has_out, lambda: two_out_rest(j).start())

    def finish(j):
        when(j % 2 == 0, lambda: one_back_in(j).wait_recv())

        @pl.when(j == 0)
        def _():
            norm_out[...] = final[0, 0:16, :].astype(f32)

        when(j > 0, lambda: to_out(j).start())

    last_lag = 7 + 4 * depth

    def step(t, carry):
        def at(lag, kind, cond, run):
            j = t - lag
            ok = (j >= 0) & (j < panels)
            if kind is not None:
                ok = ok & (j % 2 == kind)
            if cond is not None:
                ok = ok & cond
            when(ok, run, j)

        at(last_lag, 1, dist > 0, two_spread_rest) if depth == 0 else at(7 + 2 * (depth + dist), 1, dist > 0, two_spread_rest)
        at(5 + 2 * (depth + dist), 1, dist > 0, two_spread_kept)
        at(5 + 2 * (depth + dist), 0, dist > 0, one_spread)
        at(7 + 2 * depth, 1, inner, two_swapped)
        at(5 + 2 * depth, 1, inner, two_total)
        at(5 + 2 * depth, 0, inner, one_total)
        at(3 + 2 * depth, 1, inner, two_halves)
        at(3 + 2 * (depth - dist), 0, dist < depth, one_chain)
        at(1 + 2 * (depth - dist), 1, dist < depth, two_chain)
        at(3, 0, None, one_halves)
        at(1, None, None, stage_part)
        at(0, None, None, stage_send)
        at(last_lag + 1, None, None, finish)
        when(t == 0, lambda: [lefts[0].wait(), turn(0), lefts[3].wait(), turn(3)])
        when(t == 4 * SPLIT, lambda: [lefts[1].wait(), turn(1), lefts[2].wait(), turn(2)])
        return carry

    lax.fori_loop(0, panels + last_lag + 1, step, 0)

    @pl.when(inside)
    def _():
        own_copy.wait()
        own_from.wait_recv()

    @pl.when(~inside)
    def _():
        own_send.wait_send()
        across_from[0].wait_recv()
        across_from[1].wait_recv()

    across_send.wait_send()
    rows_done = pltpu.make_async_copy(halves, halves_h, h_sem.at[1])
    rows_done.start()

    def drain(j, carry):
        when(j >= panels - RING, lambda: to_sibling(j).wait_send())
        when(j > 0, lambda: to_out(j).wait())

        @pl.when(j % 2 == 0)
        def _():
            one_y(j).wait_send()
            when(dist > 0, lambda: one_in(j).wait_send())
            when(inner, lambda: one_mid(j).wait_send())
            when(has_out, lambda: one_out(j).wait_send())
            one_back(j).wait_send()

        @pl.when(j % 2 == 1)
        def _():
            when(dist > 0, lambda: two_in(j).wait_send())

            @pl.when(inner)
            def _():
                two_mid(j).wait_send()
                two_y(j).wait_send()
                two_swap(j).wait_send()

            @pl.when(has_out)
            def _():
                two_out_kept(j).wait_send()
                two_out_rest(j).wait_send()

        return carry

    lax.fori_loop(0, panels, drain, 0)
    rows_done.wait()


def reduce_gradients(lefts, rights, acts, own, across, dnorm, chain):
    rows = lefts[0].shape[0]
    features = lefts[0].shape[1]
    width = rights.shape[2] + acts.shape[1] // 2
    panels = SPLIT * width // PANEL + 1
    unit = features // SPLIT
    evens, odds = (panels + 1) // 2, panels // 2
    any_ = ANY
    V = lambda *s: pltpu.VMEM(s, bf16)
    D = lambda *s: pltpu.SemaphoreType.DMA(s)
    h = unit // 2
    return pl.pallas_call(
        functools.partial(reduce_kernel, chain),
        out_shape=[
            jax.ShapeDtypeStruct((features, width), bf16),
            jax.ShapeDtypeStruct((16, PANEL), f32),
            jax.ShapeDtypeStruct((2, *own.shape), bf16),
        ],
        in_specs=[any_] * 8 + [IN_VMEM],
        out_specs=[any_, IN_VMEM, any_],
        scratch_shapes=[
            V(4, rows, features), V(4, features, rows), V(RING, rows, PANEL), V(RING, rows, PANEL),
            V(RING, unit, PANEL), V(panels, unit, PANEL), V(panels, unit, PANEL),
            V(evens, h, PANEL), V(evens, h, PANEL), V(evens, h, PANEL), V(evens, h, PANEL),
            V(odds, unit, PANEL), V(odds, h, PANEL), V(odds, h, PANEL), V(odds, h, PANEL),
            V(panels, unit, PANEL), V(2, *own.shape),
            D(4), D(RING), D(RING), D(panels), D(RING), D(panels), D(evens), D(evens), D(evens), D(evens), D(evens), D(evens),
            D(odds), D(odds), D(odds), D(odds), D(odds), D(odds), D(3, panels), D(2, panels),
            pltpu.SemaphoreType.DMA, pltpu.SemaphoreType.DMA, pltpu.SemaphoreType.DMA, D(2), D(2),
        ],
        compiler_params=params(3),
        name="reduce_gradients",
    )(*lefts, rights, acts, own, across, dnorm)


def finish_kernel(lengths, total, halves, norm_in, first_out, second_out, rows_out, gain_out, shift_out):
    step = pl.program_id(0)
    features = rows_out.shape[1]
    wide = first_out.shape[1]
    first_out[...] = total[:, pl.ds(0, wide)].astype(f32)
    second_out[...] = total[:, pl.ds(wide, second_out.shape[1])].astype(f32)
    row = step // 2
    _, _, first = span_scalars(lengths, row)
    at = lax.broadcasted_iota(jnp.int32, (BLOCK, BLOCK), 0) + (step % 2) * BLOCK
    out = None
    for side in range(2):
        hot = at == places(first, side, (BLOCK, BLOCK), 1)
        part = mm(hot.astype(f32).astype(bf16), halves[side])
        out = part if out is None else out + part
    rows_out[...] = out
    strips = features // PANEL
    for r, ref in enumerate((gain_out, shift_out)):
        ref[...] = jnp.concatenate([norm_in[r * strips + c : r * strips + c + 1, :] for c in range(strips)], axis=1)


def finish(lengths, total, halves, norm_in, ff):
    features, width = total.shape
    tokens = halves.shape[1]
    steps = 2 * tokens // BLOCK
    part = features // steps
    row_spec = pl.BlockSpec((1, features), lambda i: (0, 0))
    return pl.pallas_call(
        finish_kernel,
        grid=(steps,),
        out_shape=[
            S((features, ff), f32), S((features, width - ff), f32), S((2 * tokens, features), f32),
            S((1, features), f32), S((1, features), f32),
        ],
        in_specs=[
            IN_SMEM, pl.BlockSpec((part, width), lambda i: (i, 0)),
            pl.BlockSpec((2, BLOCK, features), lambda i: (0, i // 2, 0)), IN_VMEM,
        ],
        out_specs=[
            pl.BlockSpec((part, ff), lambda i: (i, 0)), pl.BlockSpec((part, width - ff), lambda i: (i, 0)),
            pl.BlockSpec((BLOCK, features), lambda i: (i, 0)), row_spec, row_spec,
        ],
        compiler_params=params(None),
        name="finish",
    )(lengths, total, halves, norm_in)


def per_device(section_rows, span_lengths, first_weights, second_weights, norm_gain, norm_shift):
    first, second = first_weights[0], second_weights[0]
    norm_own = jnp.concatenate([norm_gain, norm_shift], axis=0)
    main, aux, other_first, other_second, norms, lead = start(section_rows[0], span_lengths, first, second, norm_own)
    weights = (first, second, other_first, other_second)
    saved = middle(span_lengths, main, aux, lead, norms, weights)
    own, across, df, rights, dnorm = last(span_lengths, main, aux, saved["lead_grads"], norms, weights, saved)
    lefts = (saved["x"], saved["ctx"], df, saved["mid"])
    total, norm_total, halves = reduce_gradients(
        lefts, rights, saved["a"], own, across, dnorm, lax.axis_size("dp") // 2
    )
    d_first, d_second, rows, gain, shift = finish(span_lengths, total, halves, norm_total, first.shape[1])
    return rows[None], d_first[None], d_second[None], gain, shift


def solution(mesh):
    in_specs = (
        P("section", "dp", None),
        P("dp", None),
        P("section", None, None),
        P("section", None, None),
        P("section", None),
        P("section", None),
    )
    out_specs = (
        P("section", "dp", None),
        P("section", None, None),
        P("section", None, None),
        P("section", None),
        P("section", None),
    )
    return jax.shard_map(
        per_device, mesh=mesh, in_specs=in_specs, out_specs=out_specs, check_vma=False
    )
```

time: 394 us -> 315 us (0.80)
  waiting for transfers between devices: 23.3 us -> 0 us
  Pallas kernels: 287 us -> 307 us
  other arithmetic: 20.4 us -> 1.3 us
  starting transfers between devices: 16.6 us -> 0 us
  between operations: 14.7 us -> 1.16 us
  matrix products: 11.9 us -> 0 us
  local copies, waits for them, and re-layouts: 8.05 us -> 0 us
  blocking collectives: 5.78 us -> 0 us
    pallas_call x4, Pallas kernels: 137 us -> 156 us  [the longest x1 67.2 us: middle(): pl.pallas_call(middle_kernel, out_shape=list(shapes.values()), in_specs=[...]
    ppermute x8 -> x0, starting transfers between devices: 16.5 us -> none  [the longest x1 4.24 us: per_device(): lead_rows = lax.ppermute(lead_rows, 'section', [(0, 2), (1, 3)])]
    all_gather x2 -> x0, waiting for transfers between devices: 16.2 us -> none  [both(): return lax.all_gather(block, 'section', axis_index_groups=pairs)]
    dot_general x4 -> x0, matrix products: 11.9 us -> none  [the longest x2 6.89 us: from_leads(): lax.dot_general(pick.astype(values.dtype), values, TN, precision=lax.Prec...]
    convert_element_type x3 -> x0, other arithmetic: 10.3 us -> none  [the longest x1 5.03 us: per_device(): total[None, :, :ff].astype(f32)]
    select_n x6 -> x0, other arithmetic: 7.48 us -> none  [the longest x1 1.66 us: per_device(): out0 = jnp.where(sec == 0, own_out, jnp.where(sec == 3, inner_out, out0))]
    ppermute x8 -> x0, waiting for transfers between devices: 5.8 us -> none  [the longest x1 4.68 us: per_device(): lead_grads = lax.ppermute(lead_grads, 'section', [(2, 0), (3, 1)])]
    all_gather x1 -> x0, blocking collectives: 5.78 us -> none  [both(): return lax.all_gather(block, 'section', axis_index_groups=pairs)]
  transfers between devices with their start and end apart: 10 -> 0, of which waited for: 3 -> 0; matrix products, arithmetic and copies ran while one was open for 7% -> 0% of each run, Pallas kernels for 48% -> 0%
where the time goes in v5:
time: 315 us; the launch traced here: 310 us
  Pallas kernels  307 us (97%)
    pallas_call x1, Pallas kernels, reduce_gradients(): pl.pallas_call(functools.partial(reduce_kernel, chain), out_shape=[jax.Sh...  152 us
    pallas_call x1, Pallas kernels, middle(): pl.pallas_call(middle_kernel, out_shape=list(shapes.values()), in_specs=[...  67.2 us
    pallas_call x1, Pallas kernels, start(): pl.pallas_call(start_kernel, out_shape=[square, square, S(first.shape, bf...  38.5 us
    pallas_call x1, Pallas kernels, last(): pl.pallas_call(last_kernel, out_shape=[square, square, square, S((2, toke...  38.2 us
    pallas_call x1, Pallas kernels, finish(): pl.pallas_call(finish_kernel, grid=(steps,), out_shape=[S((features, ff),...  11.7 us

profile of v5, /device:TPU:0, one launch (start us, length us, event | category | flops | bytes accessed | tf_op | source)
XLA Modules:
  0.0 309.9 jit_solution(1164494198128336345)
XLA Ops:
  0.6 1.3 pad_maximum_fusion.norm_in
  1.9 38.5 %start_and_forward.1 = (bf16[768,768]{1,0:T(8,128)(2,1)}, bf16[768,768]{1,0:T(8,128)(2,1)}, bf16[768,3072]{1,0:T(8,128)(2,1)}, bf16[768,1536]{1,0:T(8,128)(2,1)}...) custom-call(bf16[1536,768]{1,0:T(8,128)(2,1)} %bitcast.12, s32[3,6]{1,0:T(4,128)} %lengths.7, bf16[768,3072]{1,0:T(8,128)(2,1)} %bitcast.6, ...), custom_call_target="tpu_custom_call" | custom-call | tf_op jit(solution)/shard_map/start_and_forward/pallas_call | solution.py:401
  40.5 67.2 %forward_and_backward.1 = (bf16[768,768]{1,0:T(8,128)(2,1)}, bf16[768,768]{1,0:T(8,128)(2,1)}, bf16[768,2304]{1,0:T(8,128)(2,1)}, bf16[3,6,256,512]{3,2,1,0:T(8,...) custom-call(s32[3,6]{1,0:T(4,128)} %lengths.7, ...), custom_call_target="tpu_custom_call" | custom-call | tf_op jit(solution)/shard_map/forward_and_backward/pallas_call | solution.py:549
  107.7 38.2 %last_backward.1 = (bf16[768,768]{1,0:T(8,128)(2,1)}, bf16[768,768]{1,0:T(8,128)(2,1)}, bf16[768,768]{1,0:T(8,128)(2,1)}, bf16[2,768,3072]{2,1,0:T(8,128)(2,1)}, f32[4,768]{1,0:T(4,128)}) custom-call(s32[3,6]{1,0:T(4,128)} %lengths.7, bf16[768,768]{1,0:T(8,128)(2,1)} %get-tuple-element.37.main, bf16[768,768]{1,0:T(8,128)(2,1)} %get-tuple-element.38.aux, ...), custom_call_target="tpu_custom_call" | custom-call | tf_op jit(solution)/shard_map/last_backward/pallas_call | solution.py:664
  145.9 151.8 %reduce_gradients.1 = (bf16[768,4608]{1,0:T(8,128)(2,1)}, f32[16,128]{1,0:T(8,128)}, bf16[2,768,768]{2,1,0:T(8,128)(2,1)}) custom-call(bf16[768,768]{1,0:T(8,128)(2,1)} %get-tuple-element.43.x_h, bf16[768,768]{1,0:T(8,128)(2,1)} %get-tuple-element.44.ctx_h, bf16[768,768]{1,0:T(8,128)(2,1)} %get-tuple-element.54.df_h, ...), custom_call_target="tpu_custom_call" | custom-call | tf_op jit(solution)/shard_map/reduce_gradients/pallas_call | solution.py:1035
  297.7 11.7 %finish.1 = (f32[768,3072]{1,0:T(8,128)}, f32[768,1536]{1,0:T(8,128)}, f32[1536,768]{1,0:T(8,128)}, f32[1,768]{1,0:T(1,128)}, f32[1,768]{1,0:T(1,128)}) custom-call(s32[3,6]{1,0:T(4,128)} %lengths.7, bf16[768,4608]{1,0:T(8,128)(2,1)} %get-tuple-element.61.total, bf16[2,768,768]{2,1,0:T(8,128)(2,1)} %get-tuple-element.62.halves, ...), custom_call_target="tpu_custom_call" | custom-call | tf_op jit(solution)/shard_map/finish/pallas_call | solution.py:1085
